TPU v7x, 32 devices: a whole 2x2x4 slice. The times are simulated.
32 devices in a mesh: row: 4 (over z), col: 8 (over y, x, core).
Axes of the slice: x: 2, y: 2, z: 4, core: 2. Of those that a mesh axis runs over, the one named last changes fastest.
Arguments:
- inputs: bfloat16 [192, 12288], P('col', 'row'), may hold values from -40 to 40
- ln_gain: float32 [12288], P('row'), may hold values from 0.25 to 1.75
- ln_bias: float32 [12288], P('row'), may hold values from -4 to 4
- w_up: bfloat16 [12288, 49152], P('row', 'col'), may hold values from -0.0546875 to 0.0546875
- up_bias: float32 [49152], P('col'), may hold values from -4 to 4
- w_down: bfloat16 [49152, 12288], P('col', 'row'), may hold values from -0.02734375 to 0.02734375
- down_bias: float32 [12288], P('row'), may hold values from -4 to 4
Outputs:
- block_out: bfloat16 [192, 12288], P('col', 'row')
All inputs are finite; a program needn't handle non-finite values.
Results may differ from a plain program's by a relative error of at most 0.0085.
Values may be sent and summed in bfloat16 or wider, within the bound.
No kernel may reach another device: no remote copies, remote signals or barrier semaphores. Data moves between devices by JAX's collectives and lax.ppermute only.
A program may use at most 128 MiB of HBM per device.

v0:
```python
import functools
import math

import jax
import jax.numpy as jnp
from jax import lax
from jax.sharding import PartitionSpec as P


SHARES = (3, 3, 3, 3, 3, 3, 3, 3)
UP_AHEAD = 3
DOWN_AHEAD = 2


class Grid:
    def __init__(self, n_row, n_col):
        self.n_row, self.n_col = n_row, n_col
        self.cores = 2
        self.side = math.isqrt(n_col // self.cores)

    def shifted(self, index, dy, dx, dc):
        y, rest = divmod(index, self.side * self.cores)
        x, core = divmod(rest, self.cores)
        y, x = (y + dy) % self.side, (x + dx) % self.side
        core = (core + dc) % self.cores
        return (y * self.side + x) * self.cores + core

    def take(self, value, dy, dx, dc):
        pairs = [(self.shifted(i, dy, dx, dc), i) for i in range(self.n_col)]
        return lax.ppermute(value, "col", pairs)

    def give(self, value, dy, dx, dc):
        pairs = [(i, self.shifted(i, dy, dx, dc)) for i in range(self.n_col)]
        return lax.ppermute(value, "col", pairs)

    def turn(self, value, step):
        pairs = []
        for i in range(self.n_col):
            far = (step, 0, 0) if i % self.cores == 0 else (0, step, 0)
            pairs.append((self.shifted(i, *far), i))
        return lax.ppermute(value, "col", pairs)


def row_sum(grid, value):
    total = value
    for step in range(1, grid.n_row):
        pairs = [(i, (i + step) % grid.n_row) for i in range(grid.n_row)]
        total = total + lax.ppermute(value, "row", pairs)
    return total


def gather(grid, own):
    side = grid.side
    core = lax.axis_index("col") % grid.cores
    along_x = [grid.take(own, 0, d, 0) for d in range(1, side)]
    along_y = [grid.take(own, d, 0, 0) for d in range(1, side)]
    turned = jnp.where(core == 0, jnp.concatenate(along_x), jnp.concatenate(along_y))
    rows = own.shape[0]
    far = {}
    for step in range(1, side):
        block = grid.turn(turned, step)
        for d in range(1, side):
            far[step, d] = block[(d - 1) * rows : d * rows]
    held = []
    for dy in range(side):
        for dx in range(side):
            if dy == 0 and dx == 0:
                held.append(own)
            elif dy == 0:
                held.append(along_x[dx - 1])
            elif dx == 0:
                held.append(along_y[dy - 1])
            else:
                first, second = far[dy, dx], far[dx, dy]
                held.append(first if side == 2 else jnp.where(core == 0, first, second))
    held = jnp.concatenate(held)
    return jnp.concatenate([held, grid.take(held, 0, 0, 1)])


def scatter_sum(grid, terms):
    half = terms.shape[0] // grid.cores
    other = grid.give(terms[half:].astype(jnp.bfloat16), 0, 0, 1)
    pair = terms[:half] + other.astype(jnp.float32)
    rows = half // (grid.side * grid.side)
    total = pair[:rows]
    sent = pair.astype(jnp.bfloat16)
    for k in range(1, grid.side * grid.side):
        dy, dx = divmod(k, grid.side)
        total = total + grid.give(sent[k * rows : (k + 1) * rows], dy, dx, 0).astype(jnp.float32)
    return total


def chained_middle(grid, early, gathered, w_up, up_bias, w_down):
    n_row, tokens = grid.n_row, gathered.shape[0]
    half = tokens // 2
    row = lax.axis_index("row")
    middle = n_row // 2
    upper = row >= middle
    depth = jnp.where(upper, n_row - 1 - row, row)
    inward = [(i, i + 1) for i in range(middle - 1)] + [(i, i - 1) for i in range(middle + 1, n_row)]
    outward = [(j, i) for i, j in inward]
    across = [(middle - 1, middle), (middle, middle - 1)]
    acc = jnp.dot(gathered, w_up, preferred_element_type=jnp.float32).astype(jnp.bfloat16)
    partial = acc.astype(jnp.float32)
    for _ in range(middle - 1):
        acc = (partial + lax.ppermute(acc, "row", inward).astype(jnp.float32)).astype(jnp.bfloat16)
    crossed = lax.ppermute(jnp.where(upper, acc[:half], acc[half:]), "row", across)
    summed = jnp.where(upper, acc[half:], acc[:half]).astype(jnp.float32) + crossed.astype(jnp.float32)
    own = jax.nn.gelu(summed + up_bias, approximate=True).astype(jnp.bfloat16)
    other = lax.ppermute(own, "row", across)
    out = jnp.where(upper, jnp.concatenate([other, own]), jnp.concatenate([own, other]))
    for hop in range(middle - 1):
        got = lax.ppermute(out, "row", outward)
        out = jnp.where(depth == middle - 2 - hop, got, out)
    return jnp.dot(out, w_down, preferred_element_type=jnp.float32)


def chunk_edges(units):
    pieces, edges = units // 128, [0]
    for share in SHARES:
        edges.append(edges[-1] + share)
    return [pieces * e // edges[-1] * 128 for e in edges]


def cut(weights, axis, low, high, after):
    weights, _ = lax.optimization_barrier((weights, after))
    return lax.optimization_barrier(lax.slice_in_dim(weights, low, high, axis=axis))


def four_rows(grid, early, gathered, w_up, up_bias, w_down):
    row = lax.axis_index("row")
    is_end = jnp.logical_or(row == 0, row == 3)
    facing = [(0, 1), (1, 0), (2, 3), (3, 2)]
    outward = [(1, 0), (2, 3)]
    across = []
    for i in range(grid.n_row * grid.n_col):
        own_row, own_col = divmod(i, grid.n_col)
        if own_row in (1, 2):
            across.append((i, (3 - own_row) * grid.n_col + own_col))
        else:
            across.append((i, own_row * grid.n_col + grid.shifted(own_col, 0, 0, 1)))
    edges = chunk_edges(w_up.shape[1])
    count = len(SHARES)
    size = [edges[k + 1] - edges[k] for k in range(count)]

    def face(sent, pairs):
        return lax.ppermute(sent, "row", pairs)

    def cross(sent):
        return lax.ppermute(sent, ("row", "col"), across)

    up_part, down_part = dict(enumerate(early)), {}

    def stage(t, after):
        k = t + UP_AHEAD
        if k < count and k not in up_part:
            up_part[k] = cut(w_up, 1, edges[k], edges[k + 1], after)
        k = t - 3 + DOWN_AHEAD
        if 0 <= k < count:
            down_part[k] = cut(w_down, 0, edges[k], edges[k + 1], after)

    def up(k):
        return jnp.dot(gathered, up_part[k], preferred_element_type=jnp.float32).astype(jnp.bfloat16)

    def down(k):
        return jnp.dot(hidden[k], down_part[k], preferred_element_type=jnp.float32)

    def widened(v, width):
        return v if v.shape[1] == width else jnp.pad(v, ((0, 0), (0, width - v.shape[1])))

    for k in range(len(early), UP_AHEAD):
        up_part[k] = cut(w_up, 1, edges[k], edges[k + 1], gathered)
    partial, sums, own, hidden = {0: up(0)}, {}, {}, {}
    terms = None
    for t in range(count + 2):
        crossed = None
        if t < 2:
            faced = face(partial[t], facing)
        elif t < count:
            width = max(size[t], size[t - 2])
            faced = face(jnp.where(is_end, widened(partial[t], width), widened(own[t - 2], width)), facing)
        else:
            faced = face(own[t - 2], outward)
        if 0 <= t - 1 < count:
            crossed = cross(sums[t - 1])
        stage(t, partial[t] if t < count else terms)
        computed = []
        if t + 1 < count:
            partial[t + 1] = up(t + 1)
            computed.append(partial[t + 1])
        if t >= 3:
            product = down(t - 3)
            terms = product if terms is None else terms + product
            computed.append(terms)
        joined = list(lax.optimization_barrier(tuple(v for v in (faced, crossed, *computed) if v is not None)))
        faced = joined.pop(0)
        if crossed is not None:
            crossed = joined.pop(0)
        if t + 1 < count:
            partial[t + 1] = joined.pop(0)
        if joined:
            terms = joined.pop(0)
        if crossed is not None:
            k = t - 1
            summed = sums[k].astype(jnp.float32) + crossed.astype(jnp.float32)
            summed = summed + up_bias[edges[k] : edges[k + 1]]
            own[k] = jax.nn.gelu(summed, approximate=True).astype(jnp.bfloat16)
        if t < count:
            sums[t] = (partial[t].astype(jnp.float32) + faced[:, : size[t]].astype(jnp.float32)).astype(jnp.bfloat16)
        if t >= 2:
            hidden[t - 2] = jnp.where(is_end, faced[:, : size[t - 2]], own[t - 2])
    return terms + down(count - 1)


def local(grid, inputs, ln_gain, ln_bias, w_up, up_bias, w_down, down_bias):
    width = inputs.shape[1] * grid.n_row
    place = (lax.axis_index("row"), lax.axis_index("col"))
    early = []
    if grid.n_row == 4:
        edges = chunk_edges(w_up.shape[1])
        early.append(cut(w_up, 1, edges[0], edges[1], place))
    in_float = inputs.astype(jnp.float32)
    sums = jnp.stack([jnp.sum(in_float, axis=1), jnp.sum(in_float * in_float, axis=1)])
    total = row_sum(grid, sums)
    average = total[0] / width
    variance = total[1] / width - average * average
    normed = (in_float - average[:, None]) * lax.rsqrt(variance + 1e-05)[:, None]
    normed = (normed * ln_gain + ln_bias).astype(jnp.bfloat16)
    if grid.n_row == 4:
        early.append(cut(w_up, 1, edges[1], edges[2], normed))
    gathered = gather(grid, normed)
    block = four_rows if grid.n_row == 4 else chained_middle
    terms = block(grid, early, gathered, w_up, up_bias, w_down)
    down_sum = scatter_sum(grid, terms)
    return (in_float + down_sum + down_bias).astype(jnp.bfloat16)


def solution(mesh):
    grid = Grid(mesh.shape["row"], mesh.shape["col"])
    placed = (
        P("col", "row"),
        P("row"),
        P("row"),
        P("row", "col"),
        P("col"),
        P("col", "row"),
        P("row"),
    )
    return jax.shard_map(
        functools.partial(local, grid), mesh=mesh, in_specs=placed, out_specs=P("col", "row"), check_vma=False
    )
```

profile of v0, /device:TPU:0, one launch (start us, length us, event | category | flops | bytes accessed | tf_op | source)
XLA Modules:
  0.0 147.1 jit_solution(17538602511628495069)
XLA Ops:
  1.1 3.1 %collective-permute-start = (f32[2,24]{1,0:T(2,128)S(1)}, f32[2,24]{1,0:T(2,128)S(1)}, u32[]{:S(2)}, u32[]{:S(2)}) collective-permute-start(f32[2,24]{1,0:T(2,128)S(1)} %pad_maximum_fusion.1), channel_id=1, source_target_pairs={{0,8},{8,16},{16,24},{24,0},{1,9},{9,17},{17,25},{25,1},{2,10},{10... | collective-permute-start | bytes 584 | tf_op jit(solution)/shard_map/ppermute | solution.py:48
  4.2 2.6 %collective-permute-start.1 = (f32[2,24]{1,0:T(2,128)S(1)}, f32[2,24]{1,0:T(2,128)S(1)}, u32[]{:S(2)}, u32[]{:S(2)}) collective-permute-start(f32[2,24]{1,0:T(2,128)S(1)} %pad_maximum_fusion.1), channel_id=1, source_target_pairs={{0,16},{8,24},{16,0},{24,8},{1,17},{9,25},{17,1},{25,9},{2,18},{10... | collective-permute-start | bytes 584 | tf_op jit(solution)/shard_map/ppermute | solution.py:48
  6.8 1.3 collective-permute-start.2
  8.6 1.7 %collective-permute-done.2 = f32[2,24]{1,0:T(2,128)S(1)} collective-permute-done((f32[2,24]{1,0:T(2,128)S(1)}, f32[2,24]{1,0:T(2,128)S(1)}, u32[]{:S(2)}, u32[]{:S(2)}) %collective-permute-start.2) | collective-permute-done | bytes 224 | tf_op jit(solution)/shard_map/ppermute | solution.py:48
  11.5 1.6 %collective-permute-start.3 = (bf16[24,3072]{1,0:T(8,128)(2,1)S(1)}, bf16[24,3072]{1,0:T(8,128)(2,1)S(1)}, u32[]{:S(2)}, u32[]{:S(2)}) collective-permute-start(bf16[24,3072]{1,0:T(8,128)(2,1)S(1)} %get-tuple-element.106), channel_id=1, source_target_pairs={{2,0},{3,1},{0,2},{1,3},{6,4},{7,5},{4,6},{5,7},{10,8},{11,9},{8,1... | collective-permute-start | bytes 442376 | tf_op jit(solution)/shard_map/ppermute | solution.py:30
  13.0 1.5 %collective-permute-start.4 = (bf16[24,3072]{1,0:T(8,128)(2,1)S(1)}, bf16[24,3072]{1,0:T(8,128)(2,1)S(1)}, u32[]{:S(2)}, u32[]{:S(2)}) collective-permute-start(bf16[24,3072]{1,0:T(8,128)(2,1)S(1)} %get-tuple-element.106), channel_id=1, source_target_pairs={{4,0},{5,1},{6,2},{7,3},{0,4},{1,5},{2,6},{3,7},{12,8},{13,9},{14,... | collective-permute-start | bytes 442376 | tf_op jit(solution)/shard_map/ppermute | solution.py:30
  14.5 2.1 %collective-permute-done.3 = bf16[24,3072]{1,0:T(8,128)(2,1)S(1)} collective-permute-done((bf16[24,3072]{1,0:T(8,128)(2,1)S(1)}, bf16[24,3072]{1,0:T(8,128)(2,1)S(1)}, u32[]{:S(2)}, u32[]{:S(2)}) %collective-permute-start.3) | collective-permute-done | bytes 147488 | tf_op jit(solution)/shard_map/ppermute | solution.py:30
  16.7 1.5 %collective-permute-done.4 = bf16[24,3072]{1,0:T(8,128)(2,1)S(1)} collective-permute-done((bf16[24,3072]{1,0:T(8,128)(2,1)S(1)}, bf16[24,3072]{1,0:T(8,128)(2,1)S(1)}, u32[]{:S(2)}, u32[]{:S(2)}) %collective-permute-start.4) | collective-permute-done | bytes 147488 | tf_op jit(solution)/shard_map/ppermute | solution.py:30
  18.2 1.6 %collective-permute-start.5 = (bf16[24,3072]{1,0:T(8,128)(2,1)S(1)}, bf16[24,3072]{1,0:T(8,128)(2,1)S(1)}, u32[]{:S(2)}, u32[]{:S(2)}) collective-permute-start(bf16[24,3072]{1,0:T(8,128)(2,1)S(1)} %get-tuple-element.110), channel_id=1, source_target_pairs={{4,0},{3,1},{6,2},{1,3},{0,4},{7,5},{2,6},{5,7},{12,8},{11,9},{14,... | collective-permute-start | bytes 442376 | tf_op jit(solution)/shard_map/ppermute | solution.py:41
  19.8 3.6 %collective-permute-done.5 = bf16[24,3072]{1,0:T(8,128)(2,1)S(1)} collective-permute-done((bf16[24,3072]{1,0:T(8,128)(2,1)S(1)}, bf16[24,3072]{1,0:T(8,128)(2,1)S(1)}, u32[]{:S(2)}, u32[]{:S(2)}) %collective-permute-start.5) | collective-permute-done | bytes 147488 | tf_op jit(solution)/shard_map/ppermute | solution.py:41
  24.3 1.2 collective-permute-done.6
  28.0 2.0 %slice-done.2 = bf16[3072,768]{1,0:T(8,128)(2,1)S(1)} async-done(((bf16[3072,6144]{1,0:T(8,128)(2,1)}), bf16[3072,768]{1,0:T(8,128)(2,1)S(1)}, s32[]{:S(2)}) %slice-start.2) | async-done | bytes 4718616 | tf_op jit(solution)/shard_map/slice | solution.py:127
  30.1 1.1 convolution_convert_fusion.4
  31.2 2.3 %slice-done.3 = bf16[3072,768]{1,0:T(8,128)(2,1)S(1)} async-done(((bf16[3072,6144]{1,0:T(8,128)(2,1)}), bf16[3072,768]{1,0:T(8,128)(2,1)S(1)}, s32[]{:S(2)}) %slice-start.3) | async-done | bytes 4718616 | tf_op jit(solution)/shard_map/slice | solution.py:127
  34.7 1.2 slice-done.1
  37.7 2.3 %slice-done.4 = bf16[3072,768]{1,0:T(8,128)(2,1)S(1)} async-done(((bf16[3072,6144]{1,0:T(8,128)(2,1)}), bf16[3072,768]{1,0:T(8,128)(2,1)S(1)}, s32[]{:S(2)}) %slice-start.4) | async-done | bytes 4718616 | tf_op jit(solution)/shard_map/slice | solution.py:127
  41.2 5.3 %collective-permute-done.8 = bf16[192,768]{1,0:T(8,128)(2,1)S(1)} collective-permute-done((bf16[192,768]{1,0:T(8,128)(2,1)S(1)}, bf16[192,768]{1,0:T(8,128)(2,1)S(1)}, u32[]{:S(2)}, u32[]{:S(2)}) %collective-permute-start.8) | collective-permute-done | bytes 294944 | tf_op jit(solution)/shard_map/ppermute | solution.py:147
  46.9 4.2 %collective-permute-start.10 = (bf16[192,768]{1,0:T(8,128)(2,1)S(1)}, bf16[192,768]{1,0:T(8,128)(2,1)S(1)}, u32[]{:S(2)}, u32[]{:S(2)}) collective-permute-start(bf16[192,768]{1,0:T(8,128)(2,1)S(1)} %broadcast_select_fusion.5), channel_id=1, source_target_pairs={{0,8},{8,0},{16,24},{24,16},{1,9},{9,1},{17,25},{25,17},{2,10},{10... | collective-permute-start | bytes 884744 | tf_op jit(solution)/shard_map/ppermute | solution.py:147
  51.1 2.3 %slice-done.5 = bf16[3072,768]{1,0:T(8,128)(2,1)S(1)} async-done(((bf16[3072,6144]{1,0:T(8,128)(2,1)}), bf16[3072,768]{1,0:T(8,128)(2,1)S(1)}, s32[]{:S(2)}) %slice-start.5) | async-done | bytes 4718616 | tf_op jit(solution)/shard_map/slice | solution.py:127
  54.6 2.6 %collective-permute-done.10 = bf16[192,768]{1,0:T(8,128)(2,1)S(1)} collective-permute-done((bf16[192,768]{1,0:T(8,128)(2,1)S(1)}, bf16[192,768]{1,0:T(8,128)(2,1)S(1)}, u32[]{:S(2)}, u32[]{:S(2)}) %collective-permute-start.10) | collective-permute-done | bytes 294944 | tf_op jit(solution)/shard_map/ppermute | solution.py:147
  57.3 1.3 fusion.86
  59.0 2.4 %collective-permute-start.12 = (bf16[192,768]{1,0:T(8,128)(2,1)S(1)}, bf16[192,768]{1,0:T(8,128)(2,1)S(1)}, u32[]{:S(2)}, u32[]{:S(2)}) collective-permute-start(bf16[192,768]{1,0:T(8,128)(2,1)S(1)} %broadcast_select_fusion.4), channel_id=1, source_target_pairs={{0,8},{8,0},{16,24},{24,16},{1,9},{9,1},{17,25},{25,17},{2,10},{10... | collective-permute-start | bytes 884744 | tf_op jit(solution)/shard_map/ppermute | solution.py:147
  61.3 2.3 %slice-done.6 = bf16[3072,768]{1,0:T(8,128)(2,1)S(1)} async-done(((bf16[3072,6144]{1,0:T(8,128)(2,1)}), bf16[3072,768]{1,0:T(8,128)(2,1)S(1)}, s32[]{:S(2)}) %slice-start.6) | async-done | bytes 4718616 | tf_op jit(solution)/shard_map/slice | solution.py:127
  64.8 3.7 %collective-permute-done.12 = bf16[192,768]{1,0:T(8,128)(2,1)S(1)} collective-permute-done((bf16[192,768]{1,0:T(8,128)(2,1)S(1)}, bf16[192,768]{1,0:T(8,128)(2,1)S(1)}, u32[]{:S(2)}, u32[]{:S(2)}) %collective-permute-start.12) | collective-permute-done | bytes 294944 | tf_op jit(solution)/shard_map/ppermute | solution.py:147
  68.5 1.3 fusion.84
  70.2 1.8 %collective-permute-start.14 = (bf16[192,768]{1,0:T(8,128)(2,1)S(1)}, bf16[192,768]{1,0:T(8,128)(2,1)S(1)}, u32[]{:S(2)}, u32[]{:S(2)}) collective-permute-start(bf16[192,768]{1,0:T(8,128)(2,1)S(1)} %broadcast_select_fusion.3), channel_id=1, source_target_pairs={{0,8},{8,0},{16,24},{24,16},{1,9},{9,1},{17,25},{25,17},{2,10},{10... | collective-permute-start | bytes 884744 | tf_op jit(solution)/shard_map/ppermute | solution.py:147
  72.3 2.0 %slice-done.7 = bf16[3072,768]{1,0:T(8,128)(2,1)S(1)} async-done(((bf16[3072,6144]{1,0:T(8,128)(2,1)}), bf16[3072,768]{1,0:T(8,128)(2,1)S(1)}, s32[]{:S(2)}) %slice-start.7) | async-done | bytes 4718616 | tf_op jit(solution)/shard_map/slice | solution.py:127
  75.4 4.2 %collective-permute-done.14 = bf16[192,768]{1,0:T(8,128)(2,1)S(1)} collective-permute-done((bf16[192,768]{1,0:T(8,128)(2,1)S(1)}, bf16[192,768]{1,0:T(8,128)(2,1)S(1)}, u32[]{:S(2)}, u32[]{:S(2)}) %collective-permute-start.14) | collective-permute-done | bytes 294944 | tf_op jit(solution)/shard_map/ppermute | solution.py:147
  80.3 1.8 %collective-permute-start.16 = (bf16[192,768]{1,0:T(8,128)(2,1)S(1)}, bf16[192,768]{1,0:T(8,128)(2,1)S(1)}, u32[]{:S(2)}, u32[]{:S(2)}) collective-permute-start(bf16[192,768]{1,0:T(8,128)(2,1)S(1)} %broadcast_select_fusion.2), channel_id=1, source_target_pairs={{0,8},{8,0},{16,24},{24,16},{1,9},{9,1},{17,25},{25,17},{2,10},{10... | collective-permute-start | bytes 884744 | tf_op jit(solution)/shard_map/ppermute | solution.py:147
  82.7 1.3 fusion.82
  84.3 5.5 %collective-permute-done.16 = bf16[192,768]{1,0:T(8,128)(2,1)S(1)} collective-permute-done((bf16[192,768]{1,0:T(8,128)(2,1)S(1)}, bf16[192,768]{1,0:T(8,128)(2,1)S(1)}, u32[]{:S(2)}, u32[]{:S(2)}) %collective-permute-start.16) | collective-permute-done | bytes 294944 | tf_op jit(solution)/shard_map/ppermute | solution.py:147
  90.3 1.8 %collective-permute-start.18 = (bf16[192,768]{1,0:T(8,128)(2,1)S(1)}, bf16[192,768]{1,0:T(8,128)(2,1)S(1)}, u32[]{:S(2)}, u32[]{:S(2)}) collective-permute-start(bf16[192,768]{1,0:T(8,128)(2,1)S(1)} %broadcast_select_fusion.1), channel_id=1, source_target_pairs={{0,8},{8,0},{16,24},{24,16},{1,9},{9,1},{17,25},{25,17},{2,10},{10... | collective-permute-start | bytes 884744 | tf_op jit(solution)/shard_map/ppermute | solution.py:147
  92.6 1.3 fusion.80
  94.2 5.5 %collective-permute-done.18 = bf16[192,768]{1,0:T(8,128)(2,1)S(1)} collective-permute-done((bf16[192,768]{1,0:T(8,128)(2,1)S(1)}, bf16[192,768]{1,0:T(8,128)(2,1)S(1)}, u32[]{:S(2)}, u32[]{:S(2)}) %collective-permute-start.18) | collective-permute-done | bytes 294944 | tf_op jit(solution)/shard_map/ppermute | solution.py:147
  100.2 1.8 %collective-permute-start.20 = (bf16[192,768]{1,0:T(8,128)(2,1)S(1)}, bf16[192,768]{1,0:T(8,128)(2,1)S(1)}, u32[]{:S(2)}, u32[]{:S(2)}) collective-permute-start(bf16[192,768]{1,0:T(8,128)(2,1)S(1)} %broadcast_select_fusion), channel_id=1, source_target_pairs={{0,8},{8,0},{16,24},{24,16},{1,9},{9,1},{17,25},{25,17},{2,10},{10... | collective-permute-start | bytes 884744 | tf_op jit(solution)/shard_map/ppermute | solution.py:147
  102.6 1.3 fusion.78
  104.2 5.5 %collective-permute-done.20 = bf16[192,768]{1,0:T(8,128)(2,1)S(1)} collective-permute-done((bf16[192,768]{1,0:T(8,128)(2,1)S(1)}, bf16[192,768]{1,0:T(8,128)(2,1)S(1)}, u32[]{:S(2)}, u32[]{:S(2)}) %collective-permute-start.20) | collective-permute-done | bytes 294944 | tf_op jit(solution)/shard_map/ppermute | solution.py:147
  110.1 1.6 %collective-permute-start.22 = (bf16[192,768]{1,0:T(8,128)(2,1)S(1)}, bf16[192,768]{1,0:T(8,128)(2,1)S(1)}, u32[]{:S(2)}, u32[]{:S(2)}) collective-permute-start(bf16[192,768]{1,0:T(8,128)(2,1)S(1)} %fusion.55), channel_id=1, source_target_pairs={{8,0},{16,24},{9,1},{17,25},{10,2},{18,26},{11,3},{19,27},{12,4},{... | collective-permute-start | bytes 884744 | tf_op jit(solution)/shard_map/ppermute | solution.py:147
  112.5 1.3 convolution_add_fusion
  113.8 7.9 %collective-permute-done.22 = bf16[192,768]{1,0:T(8,128)(2,1)S(1)} collective-permute-done((bf16[192,768]{1,0:T(8,128)(2,1)S(1)}, bf16[192,768]{1,0:T(8,128)(2,1)S(1)}, u32[]{:S(2)}, u32[]{:S(2)}) %collective-permute-start.22) | collective-permute-done | bytes 294944 | tf_op jit(solution)/shard_map/ppermute | solution.py:147
  122.0 1.3 collective-permute-start.24
  124.7 7.7 %collective-permute-done.24 = bf16[192,768]{1,0:T(8,128)(2,1)S(1)} collective-permute-done((bf16[192,768]{1,0:T(8,128)(2,1)S(1)}, bf16[192,768]{1,0:T(8,128)(2,1)S(1)}, u32[]{:S(2)}, u32[]{:S(2)}) %collective-permute-start.24) | collective-permute-done | bytes 294944 | tf_op jit(solution)/shard_map/ppermute | solution.py:147
  134.0 2.0 %collective-permute-done.25 = bf16[96,3072]{1,0:T(8,128)(2,1)S(1)} collective-permute-done((bf16[96,3072]{1,0:T(8,128)(2,1)S(1)}, bf16[96,3072]{1,0:T(8,128)(2,1)S(1)}, u32[]{:S(2)}, u32[]{:S(2)}) %collective-permute-start.25) | collective-permute-done | bytes 589856 | tf_op jit(solution)/shard_map/ppermute | solution.py:34
  136.8 1.5 %collective-permute-start.27 = (bf16[24,3072]{1,0:T(8,128)(2,1)S(1)}, bf16[24,3072]{1,0:T(8,128)(2,1)S(1)}, u32[]{:S(2)}, u32[]{:S(2)}) collective-permute-start(bf16[24,3072]{1,0:T(8,128)(2,1)S(1)} %get-tuple-element.109), channel_id=1, source_target_pairs={{0,4},{1,5},{2,6},{3,7},{4,0},{5,1},{6,2},{7,3},{8,12},{9,13},{10,... | collective-permute-start | bytes 442376 | tf_op jit(solution)/shard_map/ppermute | solution.py:34
  138.3 1.5 collective-permute-start.28
  139.8 3.2 %collective-permute-done.26 = bf16[24,3072]{1,0:T(8,128)(2,1)S(1)} collective-permute-done((bf16[24,3072]{1,0:T(8,128)(2,1)S(1)}, bf16[24,3072]{1,0:T(8,128)(2,1)S(1)}, u32[]{:S(2)}, u32[]{:S(2)}) %collective-permute-start.26) | collective-permute-done | bytes 147488 | tf_op jit(solution)/shard_map/ppermute | solution.py:34
  143.0 1.6 %collective-permute-done.27 = bf16[24,3072]{1,0:T(8,128)(2,1)S(1)} collective-permute-done((bf16[24,3072]{1,0:T(8,128)(2,1)S(1)}, bf16[24,3072]{1,0:T(8,128)(2,1)S(1)}, u32[]{:S(2)}, u32[]{:S(2)}) %collective-permute-start.27) | collective-permute-done | bytes 147488 | tf_op jit(solution)/shard_map/ppermute | solution.py:34
  144.7 1.6 %collective-permute-done.28 = bf16[24,3072]{1,0:T(8,128)(2,1)S(1)} collective-permute-done((bf16[24,3072]{1,0:T(8,128)(2,1)S(1)}, bf16[24,3072]{1,0:T(8,128)(2,1)S(1)}, u32[]{:S(2)}, u32[]{:S(2)}) %collective-permute-start.28) | collective-permute-done | bytes 147488 | tf_op jit(solution)/shard_map/ppermute | solution.py:34
  (102 shorter events, 25.4 us)
Async XLA Ops:
  1.1 7.0 %collective-permute-start = (f32[2,24]{1,0:T(2,128)S(1)}, f32[2,24]{1,0:T(2,128)S(1)}, u32[]{:S(2)}, u32[]{:S(2)}) collective-permute-start(f32[2,24]{1,0:T(2,128)S(1)} %pad_maximum_fusion.1), channel_id=1, source_target_pairs={{0,8},{8,16},{16,24},{24,0},{1,9},{9,17},{17,25},{25,1},{2,10},{10... | collective-permute-start | bytes 584 | tf_op jit(solution)/shard_map/ppermute | solution.py:48
  4.2 4.5 %collective-permute-start.1 = (f32[2,24]{1,0:T(2,128)S(1)}, f32[2,24]{1,0:T(2,128)S(1)}, u32[]{:S(2)}, u32[]{:S(2)}) collective-permute-start(f32[2,24]{1,0:T(2,128)S(1)} %pad_maximum_fusion.1), channel_id=1, source_target_pairs={{0,16},{8,24},{16,0},{24,8},{1,17},{9,25},{17,1},{25,9},{2,18},{10... | collective-permute-start | bytes 584 | tf_op jit(solution)/shard_map/ppermute | solution.py:48
  6.8 3.6 %collective-permute-start.2 = (f32[2,24]{1,0:T(2,128)S(1)}, f32[2,24]{1,0:T(2,128)S(1)}, u32[]{:S(2)}, u32[]{:S(2)}) collective-permute-start(f32[2,24]{1,0:T(2,128)S(1)} %pad_maximum_fusion.1), channel_id=1, source_target_pairs={{0,24},{8,0},{16,8},{24,16},{1,25},{9,1},{17,9},{25,17},{2,26},{10... | collective-permute-start | bytes 584 | tf_op jit(solution)/shard_map/ppermute | solution.py:48
  11.5 5.2 %collective-permute-start.3 = (bf16[24,3072]{1,0:T(8,128)(2,1)S(1)}, bf16[24,3072]{1,0:T(8,128)(2,1)S(1)}, u32[]{:S(2)}, u32[]{:S(2)}) collective-permute-start(bf16[24,3072]{1,0:T(8,128)(2,1)S(1)} %get-tuple-element.106), channel_id=1, source_target_pairs={{2,0},{3,1},{0,2},{1,3},{6,4},{7,5},{4,6},{5,7},{10,8},{11,9},{8,1... | collective-permute-start | bytes 442376 | tf_op jit(solution)/shard_map/ppermute | solution.py:30
  13.0 5.1 %collective-permute-start.4 = (bf16[24,3072]{1,0:T(8,128)(2,1)S(1)}, bf16[24,3072]{1,0:T(8,128)(2,1)S(1)}, u32[]{:S(2)}, u32[]{:S(2)}) collective-permute-start(bf16[24,3072]{1,0:T(8,128)(2,1)S(1)} %get-tuple-element.106), channel_id=1, source_target_pairs={{4,0},{5,1},{6,2},{7,3},{0,4},{1,5},{2,6},{3,7},{12,8},{13,9},{14,... | collective-permute-start | bytes 442376 | tf_op jit(solution)/shard_map/ppermute | solution.py:30
  18.2 5.2 %collective-permute-start.5 = (bf16[24,3072]{1,0:T(8,128)(2,1)S(1)}, bf16[24,3072]{1,0:T(8,128)(2,1)S(1)}, u32[]{:S(2)}, u32[]{:S(2)}) collective-permute-start(bf16[24,3072]{1,0:T(8,128)(2,1)S(1)} %get-tuple-element.110), channel_id=1, source_target_pairs={{4,0},{3,1},{6,2},{1,3},{0,4},{7,5},{2,6},{5,7},{12,8},{11,9},{14,... | collective-permute-start | bytes 442376 | tf_op jit(solution)/shard_map/ppermute | solution.py:41
  23.4 2.1 %collective-permute-start.6 = (bf16[96,3072]{1,0:T(8,128)(2,1)S(1)}, bf16[96,3072]{1,0:T(8,128)(2,1)S(1)}, u32[]{:S(2)}, u32[]{:S(2)}) collective-permute-start(bf16[96,3072]{1,0:T(8,128)(2,1)S(1)} %pad_maximum_fusion), channel_id=1, source_target_pairs={{1,0},{0,1},{3,2},{2,3},{5,4},{4,5},{7,6},{6,7},{9,8},{8,9},{11,10... | collective-permute-start | bytes 1769480 | tf_op jit(solution)/shard_map/ppermute | solution.py:30
  23.5 0.7 copy-start.1
  24.3 2.3 %slice-start = ((bf16[3072,6144]{1,0:T(8,128)(2,1)}), bf16[3072,768]{1,0:T(8,128)(2,1)S(1)}, s32[]{:S(2)}) async-start(bf16[3072,6144]{1,0:T(8,128)(2,1)} %param.10), calls=%async_computation | async-start | bytes 9437184 | tf_op jit(solution)/shard_map/slice | solution.py:127
  27.7 2.3 %slice-start.2 = ((bf16[3072,6144]{1,0:T(8,128)(2,1)}), bf16[3072,768]{1,0:T(8,128)(2,1)S(1)}, s32[]{:S(2)}) async-start(bf16[3072,6144]{1,0:T(8,128)(2,1)} %param.10), calls=%async_computation.2 | async-start | bytes 9437184 | tf_op jit(solution)/shard_map/slice | solution.py:127
  27.7 9.5 %collective-permute-start.7 = (bf16[192,768]{1,0:T(8,128)(2,1)S(1)}, bf16[192,768]{1,0:T(8,128)(2,1)S(1)}, u32[]{:S(2)}, u32[]{:S(2)}) collective-permute-start(bf16[192,768]{1,0:T(8,128)(2,1)S(1)} %convolution_convert_fusion.7), channel_id=1, source_target_pairs={{0,8},{8,0},{16,24},{24,16},{1,9},{9,1},{17,25},{25,17},{2,10},{10... | collective-permute-start | bytes 884744 | tf_op jit(solution)/shard_map/ppermute | solution.py:147
  31.2 2.3 %slice-start.3 = ((bf16[3072,6144]{1,0:T(8,128)(2,1)}), bf16[3072,768]{1,0:T(8,128)(2,1)S(1)}, s32[]{:S(2)}) async-start(bf16[3072,6144]{1,0:T(8,128)(2,1)} %param.10), calls=%async_computation.3 | async-start | bytes 9437184 | tf_op jit(solution)/shard_map/slice | solution.py:127
  33.5 2.3 %slice-start.1 = ((bf16[3072,6144]{1,0:T(8,128)(2,1)}), bf16[3072,768]{1,0:T(8,128)(2,1)S(1)}, s32[]{:S(2)}) async-start(bf16[3072,6144]{1,0:T(8,128)(2,1)} %param.10), calls=%async_computation.1 | async-start | bytes 9437184 | tf_op jit(solution)/shard_map/slice | solution.py:127
  37.2 9.3 %collective-permute-start.8 = (bf16[192,768]{1,0:T(8,128)(2,1)S(1)}, bf16[192,768]{1,0:T(8,128)(2,1)S(1)}, u32[]{:S(2)}, u32[]{:S(2)}) collective-permute-start(bf16[192,768]{1,0:T(8,128)(2,1)S(1)} %convolution_convert_fusion.6), channel_id=1, source_target_pairs={{0,8},{8,0},{16,24},{24,16},{1,9},{9,1},{17,25},{25,17},{2,10},{10... | collective-permute-start | bytes 884744 | tf_op jit(solution)/shard_map/ppermute | solution.py:147
  37.6 3.6 %collective-permute-start.9 = (bf16[192,768]{1,0:T(8,128)(2,1)S(1)}, bf16[192,768]{1,0:T(8,128)(2,1)S(1)}, u32[]{:S(2)}, u32[]{:S(2)}) collective-permute-start(bf16[192,768]{1,0:T(8,128)(2,1)S(1)} %add_convert_fusion.7), channel_id=1, source_target_pairs={{0,1},{1,0},{2,3},{3,2},{4,5},{5,4},{6,7},{7,6},{8,16},{9,17},{10,... | collective-permute-start | bytes 884744 | tf_op jit(solution)/shard_map/ppermute | solution.py:150
  37.7 2.3 %slice-start.4 = ((bf16[3072,6144]{1,0:T(8,128)(2,1)}), bf16[3072,768]{1,0:T(8,128)(2,1)S(1)}, s32[]{:S(2)}) async-start(bf16[3072,6144]{1,0:T(8,128)(2,1)} %param.10), calls=%async_computation.4 | async-start | bytes 9437184 | tf_op jit(solution)/shard_map/slice | solution.py:127
  46.5 8.1 %collective-permute-start.11 = (bf16[192,768]{1,0:T(8,128)(2,1)S(1)}, bf16[192,768]{1,0:T(8,128)(2,1)S(1)}, u32[]{:S(2)}, u32[]{:S(2)}) collective-permute-start(bf16[192,768]{1,0:T(8,128)(2,1)S(1)} %add_convert_fusion.6), channel_id=1, source_target_pairs={{0,1},{1,0},{2,3},{3,2},{4,5},{5,4},{6,7},{7,6},{8,16},{9,17},{10,... | collective-permute-start | bytes 884744 | tf_op jit(solution)/shard_map/ppermute | solution.py:150
  46.9 10.3 %collective-permute-start.10 = (bf16[192,768]{1,0:T(8,128)(2,1)S(1)}, bf16[192,768]{1,0:T(8,128)(2,1)S(1)}, u32[]{:S(2)}, u32[]{:S(2)}) collective-permute-start(bf16[192,768]{1,0:T(8,128)(2,1)S(1)} %broadcast_select_fusion.5), channel_id=1, source_target_pairs={{0,8},{8,0},{16,24},{24,16},{1,9},{9,1},{17,25},{25,17},{2,10},{10... | collective-permute-start | bytes 884744 | tf_op jit(solution)/shard_map/ppermute | solution.py:147
  51.1 2.3 %slice-start.5 = ((bf16[3072,6144]{1,0:T(8,128)(2,1)}), bf16[3072,768]{1,0:T(8,128)(2,1)S(1)}, s32[]{:S(2)}) async-start(bf16[3072,6144]{1,0:T(8,128)(2,1)} %param.10), calls=%async_computation.5 | async-start | bytes 9437184 | tf_op jit(solution)/shard_map/slice | solution.py:127
  53.5 3.8 %slice-start.8 = ((bf16[6144,3072]{1,0:T(8,128)(2,1)}), bf16[768,3072]{1,0:T(8,128)(2,1)S(1)}, s32[]{:S(2)}) async-start(bf16[6144,3072]{1,0:T(8,128)(2,1)} %param.12), calls=%async_computation.8 | async-start | bytes 9437184 | tf_op jit(solution)/shard_map/slice | solution.py:127
  58.6 6.2 %collective-permute-start.13 = (bf16[192,768]{1,0:T(8,128)(2,1)S(1)}, bf16[192,768]{1,0:T(8,128)(2,1)S(1)}, u32[]{:S(2)}, u32[]{:S(2)}) collective-permute-start(bf16[192,768]{1,0:T(8,128)(2,1)S(1)} %add_convert_fusion.5), channel_id=1, source_target_pairs={{0,1},{1,0},{2,3},{3,2},{4,5},{5,4},{6,7},{7,6},{8,16},{9,17},{10,... | collective-permute-start | bytes 884744 | tf_op jit(solution)/shard_map/ppermute | solution.py:150
  59.0 9.5 %collective-permute-start.12 = (bf16[192,768]{1,0:T(8,128)(2,1)S(1)}, bf16[192,768]{1,0:T(8,128)(2,1)S(1)}, u32[]{:S(2)}, u32[]{:S(2)}) collective-permute-start(bf16[192,768]{1,0:T(8,128)(2,1)S(1)} %broadcast_select_fusion.4), channel_id=1, source_target_pairs={{0,8},{8,0},{16,24},{24,16},{1,9},{9,1},{17,25},{25,17},{2,10},{10... | collective-permute-start | bytes 884744 | tf_op jit(solution)/shard_map/ppermute | solution.py:147
  61.3 2.3 %slice-start.6 = ((bf16[3072,6144]{1,0:T(8,128)(2,1)}), bf16[3072,768]{1,0:T(8,128)(2,1)S(1)}, s32[]{:S(2)}) async-start(bf16[3072,6144]{1,0:T(8,128)(2,1)} %param.10), calls=%async_computation.6 | async-start | bytes 9437184 | tf_op jit(solution)/shard_map/slice | solution.py:127
  63.7 4.9 %slice-start.9 = ((bf16[6144,3072]{1,0:T(8,128)(2,1)}), bf16[768,3072]{1,0:T(8,128)(2,1)S(1)}, s32[]{:S(2)}) async-start(bf16[6144,3072]{1,0:T(8,128)(2,1)} %param.12), calls=%async_computation.9 | async-start | bytes 9437184 | tf_op jit(solution)/shard_map/slice | solution.py:127
  69.8 5.6 %collective-permute-start.15 = (bf16[192,768]{1,0:T(8,128)(2,1)S(1)}, bf16[192,768]{1,0:T(8,128)(2,1)S(1)}, u32[]{:S(2)}, u32[]{:S(2)}) collective-permute-start(bf16[192,768]{1,0:T(8,128)(2,1)S(1)} %add_convert_fusion.4), channel_id=1, source_target_pairs={{0,1},{1,0},{2,3},{3,2},{4,5},{5,4},{6,7},{7,6},{8,16},{9,17},{10,... | collective-permute-start | bytes 884744 | tf_op jit(solution)/shard_map/ppermute | solution.py:150
  70.2 9.5 %collective-permute-start.14 = (bf16[192,768]{1,0:T(8,128)(2,1)S(1)}, bf16[192,768]{1,0:T(8,128)(2,1)S(1)}, u32[]{:S(2)}, u32[]{:S(2)}) collective-permute-start(bf16[192,768]{1,0:T(8,128)(2,1)S(1)} %broadcast_select_fusion.3), channel_id=1, source_target_pairs={{0,8},{8,0},{16,24},{24,16},{1,9},{9,1},{17,25},{25,17},{2,10},{10... | collective-permute-start | bytes 884744 | tf_op jit(solution)/shard_map/ppermute | solution.py:147
  72.0 2.3 %slice-start.7 = ((bf16[3072,6144]{1,0:T(8,128)(2,1)}), bf16[3072,768]{1,0:T(8,128)(2,1)S(1)}, s32[]{:S(2)}) async-start(bf16[3072,6144]{1,0:T(8,128)(2,1)} %param.10), calls=%async_computation.7 | async-start | bytes 9437184 | tf_op jit(solution)/shard_map/slice | solution.py:127
  79.7 4.5 %collective-permute-start.17 = (bf16[192,768]{1,0:T(8,128)(2,1)S(1)}, bf16[192,768]{1,0:T(8,128)(2,1)S(1)}, u32[]{:S(2)}, u32[]{:S(2)}) collective-permute-start(bf16[192,768]{1,0:T(8,128)(2,1)S(1)} %add_convert_fusion.3), channel_id=1, source_target_pairs={{0,1},{1,0},{2,3},{3,2},{4,5},{5,4},{6,7},{7,6},{8,16},{9,17},{10,... | collective-permute-start | bytes 884744 | tf_op jit(solution)/shard_map/ppermute | solution.py:150
  80.3 2.3 %slice-start.10 = ((bf16[6144,3072]{1,0:T(8,128)(2,1)}), bf16[768,3072]{1,0:T(8,128)(2,1)S(1)}, s32[]{:S(2)}) async-start(bf16[6144,3072]{1,0:T(8,128)(2,1)} %param.12), calls=%async_computation.10 | async-start | bytes 9437184 | tf_op jit(solution)/shard_map/slice | solution.py:127
  80.3 9.5 %collective-permute-start.16 = (bf16[192,768]{1,0:T(8,128)(2,1)S(1)}, bf16[192,768]{1,0:T(8,128)(2,1)S(1)}, u32[]{:S(2)}, u32[]{:S(2)}) collective-permute-start(bf16[192,768]{1,0:T(8,128)(2,1)S(1)} %broadcast_select_fusion.2), channel_id=1, source_target_pairs={{0,8},{8,0},{16,24},{24,16},{1,9},{9,1},{17,25},{25,17},{2,10},{10... | collective-permute-start | bytes 884744 | tf_op jit(solution)/shard_map/ppermute | solution.py:147
  89.9 4.3 %collective-permute-start.19 = (bf16[192,768]{1,0:T(8,128)(2,1)S(1)}, bf16[192,768]{1,0:T(8,128)(2,1)S(1)}, u32[]{:S(2)}, u32[]{:S(2)}) collective-permute-start(bf16[192,768]{1,0:T(8,128)(2,1)S(1)} %add_convert_fusion.2), channel_id=1, source_target_pairs={{0,1},{1,0},{2,3},{3,2},{4,5},{5,4},{6,7},{7,6},{8,16},{9,17},{10,... | collective-permute-start | bytes 884744 | tf_op jit(solution)/shard_map/ppermute | solution.py:150
  90.3 2.3 %slice-start.11 = ((bf16[6144,3072]{1,0:T(8,128)(2,1)}), bf16[768,3072]{1,0:T(8,128)(2,1)S(1)}, s32[]{:S(2)}) async-start(bf16[6144,3072]{1,0:T(8,128)(2,1)} %param.12), calls=%async_computation.11 | async-start | bytes 9437184 | tf_op jit(solution)/shard_map/slice | solution.py:127
  90.3 9.5 %collective-permute-start.18 = (bf16[192,768]{1,0:T(8,128)(2,1)S(1)}, bf16[192,768]{1,0:T(8,128)(2,1)S(1)}, u32[]{:S(2)}, u32[]{:S(2)}) collective-permute-start(bf16[192,768]{1,0:T(8,128)(2,1)S(1)} %broadcast_select_fusion.1), channel_id=1, source_target_pairs={{0,8},{8,0},{16,24},{24,16},{1,9},{9,1},{17,25},{25,17},{2,10},{10... | collective-permute-start | bytes 884744 | tf_op jit(solution)/shard_map/ppermute | solution.py:147
  99.8 4.3 %collective-permute-start.21 = (bf16[192,768]{1,0:T(8,128)(2,1)S(1)}, bf16[192,768]{1,0:T(8,128)(2,1)S(1)}, u32[]{:S(2)}, u32[]{:S(2)}) collective-permute-start(bf16[192,768]{1,0:T(8,128)(2,1)S(1)} %add_convert_fusion.1), channel_id=1, source_target_pairs={{0,1},{1,0},{2,3},{3,2},{4,5},{5,4},{6,7},{7,6},{8,16},{9,17},{10,... | collective-permute-start | bytes 884744 | tf_op jit(solution)/shard_map/ppermute | solution.py:150
  100.2 2.3 %slice-start.12 = ((bf16[6144,3072]{1,0:T(8,128)(2,1)}), bf16[768,3072]{1,0:T(8,128)(2,1)S(1)}, s32[]{:S(2)}) async-start(bf16[6144,3072]{1,0:T(8,128)(2,1)} %param.12), calls=%async_computation.12 | async-start | bytes 9437184 | tf_op jit(solution)/shard_map/slice | solution.py:127
  100.2 9.5 %collective-permute-start.20 = (bf16[192,768]{1,0:T(8,128)(2,1)S(1)}, bf16[192,768]{1,0:T(8,128)(2,1)S(1)}, u32[]{:S(2)}, u32[]{:S(2)}) collective-permute-start(bf16[192,768]{1,0:T(8,128)(2,1)S(1)} %broadcast_select_fusion), channel_id=1, source_target_pairs={{0,8},{8,0},{16,24},{24,16},{1,9},{9,1},{17,25},{25,17},{2,10},{10... | collective-permute-start | bytes 884744 | tf_op jit(solution)/shard_map/ppermute | solution.py:147
  109.8 4.0 %collective-permute-start.23 = (bf16[192,768]{1,0:T(8,128)(2,1)S(1)}, bf16[192,768]{1,0:T(8,128)(2,1)S(1)}, u32[]{:S(2)}, u32[]{:S(2)}) collective-permute-start(bf16[192,768]{1,0:T(8,128)(2,1)S(1)} %add_convert_fusion), channel_id=1, source_target_pairs={{0,1},{1,0},{2,3},{3,2},{4,5},{5,4},{6,7},{7,6},{8,16},{9,17},{10,... | collective-permute-start | bytes 884744 | tf_op jit(solution)/shard_map/ppermute | solution.py:150
  110.1 2.3 %slice-start.13 = ((bf16[6144,3072]{1,0:T(8,128)(2,1)}), bf16[768,3072]{1,0:T(8,128)(2,1)S(1)}, s32[]{:S(2)}) async-start(bf16[6144,3072]{1,0:T(8,128)(2,1)} %param.12), calls=%async_computation.13 | async-start | bytes 9437184 | tf_op jit(solution)/shard_map/slice | solution.py:127
  110.1 11.6 %collective-permute-start.22 = (bf16[192,768]{1,0:T(8,128)(2,1)S(1)}, bf16[192,768]{1,0:T(8,128)(2,1)S(1)}, u32[]{:S(2)}, u32[]{:S(2)}) collective-permute-start(bf16[192,768]{1,0:T(8,128)(2,1)S(1)} %fusion.55), channel_id=1, source_target_pairs={{8,0},{16,24},{9,1},{17,25},{10,2},{18,26},{11,3},{19,27},{12,4},{... | collective-permute-start | bytes 884744 | tf_op jit(solution)/shard_map/ppermute | solution.py:147
  112.5 10.8 %slice-start.14 = ((bf16[6144,3072]{1,0:T(8,128)(2,1)}), bf16[768,3072]{1,0:T(8,128)(2,1)S(1)}, s32[]{:S(2)}) async-start(bf16[6144,3072]{1,0:T(8,128)(2,1)} %param.12), calls=%async_computation.14 | async-start | bytes 9437184 | tf_op jit(solution)/shard_map/slice | solution.py:127
  122.0 10.4 %collective-permute-start.24 = (bf16[192,768]{1,0:T(8,128)(2,1)S(1)}, bf16[192,768]{1,0:T(8,128)(2,1)S(1)}, u32[]{:S(2)}, u32[]{:S(2)}) collective-permute-start(bf16[192,768]{1,0:T(8,128)(2,1)S(1)} %fusion.63), channel_id=1, source_target_pairs={{8,0},{16,24},{9,1},{17,25},{10,2},{18,26},{11,3},{19,27},{12,4},{... | collective-permute-start | bytes 884744 | tf_op jit(solution)/shard_map/ppermute | solution.py:147
  124.4 8.0 %slice-start.15 = ((bf16[6144,3072]{1,0:T(8,128)(2,1)}), bf16[768,3072]{1,0:T(8,128)(2,1)S(1)}, s32[]{:S(2)}) async-start(bf16[6144,3072]{1,0:T(8,128)(2,1)} %param.12), calls=%async_computation.15 | async-start | bytes 9437184 | tf_op jit(solution)/shard_map/slice | solution.py:127
  133.9 12.4 %copy-start = (bf16[24,3072]{1,0:T(8,128)(2,1)S(1)}, bf16[24,3072]{1,0:T(8,128)(2,1)}, u32[]{:S(2)}) copy-start(bf16[24,3072]{1,0:T(8,128)(2,1)} %param.7) | copy-start | bytes 442372
  133.9 12.4 %copy-start.2 = (f32[3072]{0:T(1024)S(1)}, f32[3072]{0:T(1024)}, u32[]{:S(2)}) copy-start(f32[3072]{0:T(1024)} %param.13) | copy-start | bytes 36868
  133.9 2.1 %collective-permute-start.25 = (bf16[96,3072]{1,0:T(8,128)(2,1)S(1)}, bf16[96,3072]{1,0:T(8,128)(2,1)S(1)}, u32[]{:S(2)}, u32[]{:S(2)}) collective-permute-start(bf16[96,3072]{1,0:T(8,128)(2,1)S(1)} %slice.148), channel_id=1, source_target_pairs={{0,1},{1,0},{2,3},{3,2},{4,5},{5,4},{6,7},{7,6},{8,9},{9,8},{10,11... | collective-permute-start | bytes 1769480 | tf_op jit(solution)/shard_map/ppermute | solution.py:34
  136.2 6.8 %collective-permute-start.26 = (bf16[24,3072]{1,0:T(8,128)(2,1)S(1)}, bf16[24,3072]{1,0:T(8,128)(2,1)S(1)}, u32[]{:S(2)}, u32[]{:S(2)}) collective-permute-start(bf16[24,3072]{1,0:T(8,128)(2,1)S(1)} %get-tuple-element.107), channel_id=1, source_target_pairs={{0,2},{1,3},{2,0},{3,1},{4,6},{5,7},{6,4},{7,5},{8,10},{9,11},{10,... | collective-permute-start | bytes 442376 | tf_op jit(solution)/shard_map/ppermute | solution.py:34
  136.8 7.8 %collective-permute-start.27 = (bf16[24,3072]{1,0:T(8,128)(2,1)S(1)}, bf16[24,3072]{1,0:T(8,128)(2,1)S(1)}, u32[]{:S(2)}, u32[]{:S(2)}) collective-permute-start(bf16[24,3072]{1,0:T(8,128)(2,1)S(1)} %get-tuple-element.109), channel_id=1, source_target_pairs={{0,4},{1,5},{2,6},{3,7},{4,0},{5,1},{6,2},{7,3},{8,12},{9,13},{10,... | collective-permute-start | bytes 442376 | tf_op jit(solution)/shard_map/ppermute | solution.py:34
  138.3 8.0 %collective-permute-start.28 = (bf16[24,3072]{1,0:T(8,128)(2,1)S(1)}, bf16[24,3072]{1,0:T(8,128)(2,1)S(1)}, u32[]{:S(2)}, u32[]{:S(2)}) collective-permute-start(bf16[24,3072]{1,0:T(8,128)(2,1)S(1)} %get-tuple-element.108), channel_id=1, source_target_pairs={{0,6},{1,7},{2,4},{3,5},{4,2},{5,3},{6,0},{7,1},{8,14},{9,15},{10,... | collective-permute-start | bytes 442376 | tf_op jit(solution)/shard_map/ppermute | solution.py:34
where the time goes:
time: 148 us; the launch traced here: 147 us
  waiting for transfers between devices  67.4 us (46%)
  starting transfers between devices  33.2 us (22%)
  local copies, waits for them, and re-layouts  19.1 us (13%)
  matrix products  18.7 us (13%)
  other arithmetic  8.06 us (5%)
    ppermute x10, waiting for transfers between devices, face(): return lax.ppermute(sent, 'row', pairs)  48.2 us
    slice x32, local copies, waits for them, and re-layouts, cut(): lax.slice_in_dim(weights, low, high, axis=axis)  18.2 us
    ppermute x10, starting transfers between devices, face(): return lax.ppermute(sent, 'row', pairs)  17 us
    dot_general x8, matrix products, down(): return jnp.dot(hidden[k], down_part[k], preferred_element_type=jnp.float32)  9.8 us
    dot_general x8, matrix products, up(): jnp.dot(gathered, up_part[k], preferred_element_type=jnp.float32)  8.9 us
    ppermute x4, waiting for transfers between devices, give(): return lax.ppermute(value, 'col', pairs)  8.51 us
    ppermute x3, starting transfers between devices, row_sum(): total = total + lax.ppermute(value, 'row', pairs)  7.04 us
    ppermute x3, waiting for transfers between devices, take(): return lax.ppermute(value, 'col', pairs)  4.83 us
  transfers between devices with their start and end apart: 29, of which 20 were waited for; matrix products, arithmetic and copies ran while one was open for 12% of the time, Pallas kernels for 0%

commit v1 on v0

--- a/solution.py
+++ b/solution.py
@@ -33,46 +33,19 @@
         pairs = [(i, self.shifted(i, dy, dx, dc)) for i in range(self.n_col)]
         return lax.ppermute(value, "col", pairs)
 
-    def turn(self, value, step):
-        pairs = []
-        for i in range(self.n_col):
-            far = (step, 0, 0) if i % self.cores == 0 else (0, step, 0)
-            pairs.append((self.shifted(i, *far), i))
-        return lax.ppermute(value, "col", pairs)
-
 
 def row_sum(grid, value):
-    total = value
-    for step in range(1, grid.n_row):
-        pairs = [(i, (i + step) % grid.n_row) for i in range(grid.n_row)]
-        total = total + lax.ppermute(value, "row", pairs)
-    return total
+    step = 1
+    while step < grid.n_row:
+        value = value + lax.ppermute(value, "row", [(i, i ^ step) for i in range(grid.n_row)])
+        step *= 2
+    return value
 
 
 def gather(grid, own):
-    side = grid.side
-    core = lax.axis_index("col") % grid.cores
-    along_x = [grid.take(own, 0, d, 0) for d in range(1, side)]
-    along_y = [grid.take(own, d, 0, 0) for d in range(1, side)]
-    turned = jnp.where(core == 0, jnp.concatenate(along_x), jnp.concatenate(along_y))
-    rows = own.shape[0]
-    far = {}
-    for step in range(1, side):
-        block = grid.turn(turned, step)
-        for d in range(1, side):
-            far[step, d] = block[(d - 1) * rows : d * rows]
-    held = []
-    for dy in range(side):
-        for dx in range(side):
-            if dy == 0 and dx == 0:
-                held.append(own)
-            elif dy == 0:
-                held.append(along_x[dx - 1])
-            elif dx == 0:
-                held.append(along_y[dy - 1])
-            else:
-                first, second = far[dy, dx], far[dx, dy]
-                held.append(first if side == 2 else jnp.where(core == 0, first, second))
+    held = [own]
+    for k in range(1, grid.side * grid.side):
+        held.append(grid.take(own, k // grid.side, k % grid.side, 0))
     held = jnp.concatenate(held)
     return jnp.concatenate([held, grid.take(held, 0, 0, 1)])
 
@@ -90,7 +63,7 @@
     return total
 
 
-def chained_middle(grid, early, gathered, w_up, up_bias, w_down):
+def chained_middle(grid, gathered, w_up, up_bias, w_down):
     n_row, tokens = grid.n_row, gathered.shape[0]
     half = tokens // 2
     row = lax.axis_index("row")
@@ -127,11 +100,8 @@
     return lax.optimization_barrier(lax.slice_in_dim(weights, low, high, axis=axis))
 
 
-def four_rows(grid, early, gathered, w_up, up_bias, w_down):
-    row = lax.axis_index("row")
-    is_end = jnp.logical_or(row == 0, row == 3)
+def four_rows(grid, is_end, early, gathered, w_up, up_bias, w_down):
     facing = [(0, 1), (1, 0), (2, 3), (3, 2)]
-    outward = [(1, 0), (2, 3)]
     across = []
     for i in range(grid.n_row * grid.n_col):
         own_row, own_col = divmod(i, grid.n_col)
@@ -180,7 +150,7 @@
             width = max(size[t], size[t - 2])
             faced = face(jnp.where(is_end, widened(partial[t], width), widened(own[t - 2], width)), facing)
         else:
-            faced = face(own[t - 2], outward)
+            faced = face(own[t - 2], facing)
         if 0 <= t - 1 < count:
             crossed = cross(sums[t - 1])
         stage(t, partial[t] if t < count else terms)
@@ -214,11 +184,12 @@
 
 def local(grid, inputs, ln_gain, ln_bias, w_up, up_bias, w_down, down_bias):
     width = inputs.shape[1] * grid.n_row
-    place = (lax.axis_index("row"), lax.axis_index("col"))
     early = []
     if grid.n_row == 4:
+        row = lax.axis_index("row")
+        is_end, w_first = lax.optimization_barrier((jnp.logical_or(row == 0, row == 3), w_up))
         edges = chunk_edges(w_up.shape[1])
-        early.append(cut(w_up, 1, edges[0], edges[1], place))
+        early.append(lax.optimization_barrier(lax.slice_in_dim(w_first, edges[0], edges[1], axis=1)))
     in_float = inputs.astype(jnp.float32)
     sums = jnp.stack([jnp.sum(in_float, axis=1), jnp.sum(in_float * in_float, axis=1)])
     total = row_sum(grid, sums)
@@ -229,8 +200,10 @@
     if grid.n_row == 4:
         early.append(cut(w_up, 1, edges[1], edges[2], normed))
     gathered = gather(grid, normed)
-    block = four_rows if grid.n_row == 4 else chained_middle
-    terms = block(grid, early, gathered, w_up, up_bias, w_down)
+    if grid.n_row == 4:
+        terms = four_rows(grid, is_end, early, gathered, w_up, up_bias, w_down)
+    else:
+        terms = chained_middle(grid, gathered, w_up, up_bias, w_down)
     down_sum = scatter_sum(grid, terms)
     return (in_float + down_sum + down_bias).astype(jnp.bfloat16)
 

time: 148 us -> 138 us (0.932)
  waiting for transfers between devices: 67.4 us -> 61.7 us
  local copies, waits for them, and re-layouts: 19.1 us -> 14.9 us
    ppermute x10, waiting for transfers between devices: 48.2 us -> 43 us  [face(): return lax.ppermute(sent, 'row', pairs)]
    ppermute x10, starting transfers between devices: 17 us -> 20.5 us  [face(): return lax.ppermute(sent, 'row', pairs)]
    slice x32 -> x30, local copies, waits for them, and re-layouts: 18.2 us -> 14.7 us  [cut(): lax.slice_in_dim(weights, low, high, axis=axis)]
    ppermute x3 -> x4, waiting for transfers between devices: 4.83 us -> 7.81 us  [take(): return lax.ppermute(value, 'col', pairs)]
    ppermute x4 -> x2, waiting for transfers between devices: 5.85 us -> 3.11 us  [row_sum(): lax.ppermute(value, 'row', [(i, i ^ step) for i in range(grid.n_row)])]
    ppermute x4 -> x2, starting transfers between devices: 8.63 us -> 6.21 us  [row_sum(): lax.ppermute(value, 'row', [(i, i ^ step) for i in range(grid.n_row)])]
    ppermute x3 -> x4, starting transfers between devices: 3.15 us -> 3.62 us  [take(): return lax.ppermute(value, 'col', pairs)]
  transfers between devices with their start and end apart: 29 -> 28, of which waited for: 20 -> 18; matrix products, arithmetic and copies ran while one was open for 12% -> 13% of each run, Pallas kernels for 0% -> 0%
where the time goes in v1:
time: 138 us
  waiting for transfers between devices  61.7 us (45%)
  starting transfers between devices  34.5 us (25%)
  matrix products  18.9 us (14%)
  local copies, waits for them, and re-layouts  14.9 us (11%)
  other arithmetic  7.11 us (5%)
    ppermute x10, waiting for transfers between devices, face(): return lax.ppermute(sent, 'row', pairs)  43 us
    ppermute x10, starting transfers between devices, face(): return lax.ppermute(sent, 'row', pairs)  20.5 us
    slice x30, local copies, waits for them, and re-layouts, cut(): lax.slice_in_dim(weights, low, high, axis=axis)  14.7 us
    dot_general x8, matrix products, down(): return jnp.dot(hidden[k], down_part[k], preferred_element_type=jnp.float32)  9.79 us
    dot_general x8, matrix products, up(): jnp.dot(gathered, up_part[k], preferred_element_type=jnp.float32)  9.08 us
    ppermute x4, waiting for transfers between devices, give(): return lax.ppermute(value, 'col', pairs)  7.82 us
    ppermute x4, waiting for transfers between devices, take(): return lax.ppermute(value, 'col', pairs)  7.81 us
    ppermute x2, starting transfers between devices, row_sum(): lax.ppermute(value, 'row', [(i, i ^ step) for i in range(grid.n_row)])  6.21 us
  transfers between devices with their start and end apart: 28, of which 18 were waited for; matrix products, arithmetic and copies ran while one was open for 13% of the time, Pallas kernels for 0%

profile of v1, /device:TPU:0, one launch (start us, length us, event | category | flops | bytes accessed | tf_op | source)
XLA Modules:
  0.0 137.8 jit_solution(775245766725338830)
XLA Ops:
  1.1 3.1 %collective-permute-start = (f32[2,24]{1,0:T(2,128)S(1)}, f32[2,24]{1,0:T(2,128)S(1)}, u32[]{:S(2)}, u32[]{:S(2)}) collective-permute-start(f32[2,24]{1,0:T(2,128)S(1)} %pad_maximum_fusion.1), channel_id=1, source_target_pairs={{0,8},{8,0},{16,24},{24,16},{1,9},{9,1},{17,25},{25,17},{2,10},{10... | collective-permute-start | bytes 584 | tf_op jit(solution)/shard_map/ppermute | solution.py:40
  4.2 1.6 %collective-permute-done = f32[2,24]{1,0:T(2,128)S(1)} collective-permute-done((f32[2,24]{1,0:T(2,128)S(1)}, f32[2,24]{1,0:T(2,128)S(1)}, u32[]{:S(2)}, u32[]{:S(2)}) %collective-permute-start) | collective-permute-done | bytes 224 | tf_op jit(solution)/shard_map/ppermute | solution.py:40
  5.8 3.1 %collective-permute-start.1 = (f32[2,24]{1,0:T(2,128)S(1)}, f32[2,24]{1,0:T(2,128)S(1)}, u32[]{:S(2)}, u32[]{:S(2)}) collective-permute-start(f32[2,24]{1,0:T(2,128)S(1)} %fusion.98), channel_id=1, source_target_pairs={{0,16},{8,24},{16,0},{24,8},{1,17},{9,25},{17,1},{25,9},{2,18},{10... | collective-permute-start | bytes 584 | tf_op jit(solution)/shard_map/ppermute | solution.py:40
  8.9 1.6 %collective-permute-done.1 = f32[2,24]{1,0:T(2,128)S(1)} collective-permute-done((f32[2,24]{1,0:T(2,128)S(1)}, f32[2,24]{1,0:T(2,128)S(1)}, u32[]{:S(2)}, u32[]{:S(2)}) %collective-permute-start.1) | collective-permute-done | bytes 224 | tf_op jit(solution)/shard_map/ppermute | solution.py:40
  10.7 1.9 %collective-permute-start.2 = (bf16[24,3072]{1,0:T(8,128)(2,1)S(1)}, bf16[24,3072]{1,0:T(8,128)(2,1)S(1)}, u32[]{:S(2)}, u32[]{:S(2)}) collective-permute-start(bf16[24,3072]{1,0:T(8,128)(2,1)S(1)} %get-tuple-element.108), channel_id=1, source_target_pairs={{2,0},{3,1},{0,2},{1,3},{6,4},{7,5},{4,6},{5,7},{10,8},{11,9},{8,1... | collective-permute-start | bytes 442376 | tf_op jit(solution)/shard_map/ppermute | solution.py:30
  12.5 1.5 %collective-permute-start.3 = (bf16[24,3072]{1,0:T(8,128)(2,1)S(1)}, bf16[24,3072]{1,0:T(8,128)(2,1)S(1)}, u32[]{:S(2)}, u32[]{:S(2)}) collective-permute-start(bf16[24,3072]{1,0:T(8,128)(2,1)S(1)} %get-tuple-element.108), channel_id=1, source_target_pairs={{4,0},{5,1},{6,2},{7,3},{0,4},{1,5},{2,6},{3,7},{12,8},{13,9},{14,... | collective-permute-start | bytes 442376 | tf_op jit(solution)/shard_map/ppermute | solution.py:30
  14.2 2.5 %collective-permute-done.2 = bf16[24,3072]{1,0:T(8,128)(2,1)S(1)} collective-permute-done((bf16[24,3072]{1,0:T(8,128)(2,1)S(1)}, bf16[24,3072]{1,0:T(8,128)(2,1)S(1)}, u32[]{:S(2)}, u32[]{:S(2)}) %collective-permute-start.2) | collective-permute-done | bytes 147488 | tf_op jit(solution)/shard_map/ppermute | solution.py:30
  16.7 1.2 collective-permute-done.3
  18.0 2.1 %collective-permute-done.4 = bf16[24,3072]{1,0:T(8,128)(2,1)S(1)} collective-permute-done((bf16[24,3072]{1,0:T(8,128)(2,1)S(1)}, bf16[24,3072]{1,0:T(8,128)(2,1)S(1)}, u32[]{:S(2)}, u32[]{:S(2)}) %collective-permute-start.4) | collective-permute-done | bytes 147488 | tf_op jit(solution)/shard_map/ppermute | solution.py:30
  20.3 1.9 %collective-permute-done.5 = bf16[96,3072]{1,0:T(8,128)(2,1)S(1)} collective-permute-done((bf16[96,3072]{1,0:T(8,128)(2,1)S(1)}, bf16[96,3072]{1,0:T(8,128)(2,1)S(1)}, u32[]{:S(2)}, u32[]{:S(2)}) %collective-permute-start.5) | collective-permute-done | bytes 589856 | tf_op jit(solution)/shard_map/ppermute | solution.py:30
  23.4 1.7 %collective-permute-start.6 = (bf16[192,768]{1,0:T(8,128)(2,1)S(1)}, bf16[192,768]{1,0:T(8,128)(2,1)S(1)}, u32[]{:S(2)}, u32[]{:S(2)}) collective-permute-start(bf16[192,768]{1,0:T(8,128)(2,1)S(1)} %convolution_convert_fusion.7), channel_id=1, source_target_pairs={{0,8},{8,0},{16,24},{24,16},{1,9},{9,1},{17,25},{25,17},{2,10},{10... | collective-permute-start | bytes 884744 | tf_op jit(solution)/shard_map/ppermute | solution.py:117
  25.7 1.1 convolution_convert_fusion.4
  26.9 2.3 %slice-done.3 = bf16[3072,768]{1,0:T(8,128)(2,1)S(1)} async-done(((bf16[3072,6144]{1,0:T(8,128)(2,1)}), bf16[3072,768]{1,0:T(8,128)(2,1)S(1)}, s32[]{:S(2)}) %slice-start.3) | async-done | bytes 4718616 | tf_op jit(solution)/shard_map/slice | solution.py:100
  30.3 1.2 slice-done.1
  31.5 1.1 convolution_convert_fusion.6
  32.7 1.6 %collective-permute-start.7 = (bf16[192,768]{1,0:T(8,128)(2,1)S(1)}, bf16[192,768]{1,0:T(8,128)(2,1)S(1)}, u32[]{:S(2)}, u32[]{:S(2)}) collective-permute-start(bf16[192,768]{1,0:T(8,128)(2,1)S(1)} %convolution_convert_fusion.6), channel_id=1, source_target_pairs={{0,8},{8,0},{16,24},{24,16},{1,9},{9,1},{17,25},{25,17},{2,10},{10... | collective-permute-start | bytes 884744 | tf_op jit(solution)/shard_map/ppermute | solution.py:117
  34.5 2.3 %slice-done.4 = bf16[3072,768]{1,0:T(8,128)(2,1)S(1)} async-done(((bf16[3072,6144]{1,0:T(8,128)(2,1)}), bf16[3072,768]{1,0:T(8,128)(2,1)S(1)}, s32[]{:S(2)}) %slice-start.4) | async-done | bytes 4718616 | tf_op jit(solution)/shard_map/slice | solution.py:100
  36.8 1.1 convolution_convert_fusion.3
  37.9 3.8 %collective-permute-done.7 = bf16[192,768]{1,0:T(8,128)(2,1)S(1)} collective-permute-done((bf16[192,768]{1,0:T(8,128)(2,1)S(1)}, bf16[192,768]{1,0:T(8,128)(2,1)S(1)}, u32[]{:S(2)}, u32[]{:S(2)}) %collective-permute-start.7) | collective-permute-done | bytes 294944 | tf_op jit(solution)/shard_map/ppermute | solution.py:117
  42.2 4.6 %collective-permute-start.9 = (bf16[192,768]{1,0:T(8,128)(2,1)S(1)}, bf16[192,768]{1,0:T(8,128)(2,1)S(1)}, u32[]{:S(2)}, u32[]{:S(2)}) collective-permute-start(bf16[192,768]{1,0:T(8,128)(2,1)S(1)} %broadcast_select_fusion.5), channel_id=1, source_target_pairs={{0,8},{8,0},{16,24},{24,16},{1,9},{9,1},{17,25},{25,17},{2,10},{10... | collective-permute-start | bytes 884744 | tf_op jit(solution)/shard_map/ppermute | solution.py:117
  46.9 2.3 %slice-done.5 = bf16[3072,768]{1,0:T(8,128)(2,1)S(1)} async-done(((bf16[3072,6144]{1,0:T(8,128)(2,1)}), bf16[3072,768]{1,0:T(8,128)(2,1)S(1)}, s32[]{:S(2)}) %slice-start.5) | async-done | bytes 4718616 | tf_op jit(solution)/shard_map/slice | solution.py:100
  50.3 2.4 %collective-permute-done.9 = bf16[192,768]{1,0:T(8,128)(2,1)S(1)} collective-permute-done((bf16[192,768]{1,0:T(8,128)(2,1)S(1)}, bf16[192,768]{1,0:T(8,128)(2,1)S(1)}, u32[]{:S(2)}, u32[]{:S(2)}) %collective-permute-start.9) | collective-permute-done | bytes 294944 | tf_op jit(solution)/shard_map/ppermute | solution.py:117
  52.9 1.3 fusion.86
  54.5 2.4 %collective-permute-start.11 = (bf16[192,768]{1,0:T(8,128)(2,1)S(1)}, bf16[192,768]{1,0:T(8,128)(2,1)S(1)}, u32[]{:S(2)}, u32[]{:S(2)}) collective-permute-start(bf16[192,768]{1,0:T(8,128)(2,1)S(1)} %broadcast_select_fusion.4), channel_id=1, source_target_pairs={{0,8},{8,0},{16,24},{24,16},{1,9},{9,1},{17,25},{25,17},{2,10},{10... | collective-permute-start | bytes 884744 | tf_op jit(solution)/shard_map/ppermute | solution.py:117
  56.9 2.3 %slice-done.6 = bf16[3072,768]{1,0:T(8,128)(2,1)S(1)} async-done(((bf16[3072,6144]{1,0:T(8,128)(2,1)}), bf16[3072,768]{1,0:T(8,128)(2,1)S(1)}, s32[]{:S(2)}) %slice-start.6) | async-done | bytes 4718616 | tf_op jit(solution)/shard_map/slice | solution.py:100
  60.3 3.6 %collective-permute-done.11 = bf16[192,768]{1,0:T(8,128)(2,1)S(1)} collective-permute-done((bf16[192,768]{1,0:T(8,128)(2,1)S(1)}, bf16[192,768]{1,0:T(8,128)(2,1)S(1)}, u32[]{:S(2)}, u32[]{:S(2)}) %collective-permute-start.11) | collective-permute-done | bytes 294944 | tf_op jit(solution)/shard_map/ppermute | solution.py:117
  64.1 1.3 fusion.84
  65.7 2.0 %collective-permute-start.13 = (bf16[192,768]{1,0:T(8,128)(2,1)S(1)}, bf16[192,768]{1,0:T(8,128)(2,1)S(1)}, u32[]{:S(2)}, u32[]{:S(2)}) collective-permute-start(bf16[192,768]{1,0:T(8,128)(2,1)S(1)} %broadcast_select_fusion.3), channel_id=1, source_target_pairs={{0,8},{8,0},{16,24},{24,16},{1,9},{9,1},{17,25},{25,17},{2,10},{10... | collective-permute-start | bytes 884744 | tf_op jit(solution)/shard_map/ppermute | solution.py:117
  68.0 2.0 %slice-done.7 = bf16[3072,768]{1,0:T(8,128)(2,1)S(1)} async-done(((bf16[3072,6144]{1,0:T(8,128)(2,1)}), bf16[3072,768]{1,0:T(8,128)(2,1)S(1)}, s32[]{:S(2)}) %slice-start.7) | async-done | bytes 4718616 | tf_op jit(solution)/shard_map/slice | solution.py:100
  70.0 1.3 convolution_convert_fusion
  71.4 3.8 %collective-permute-done.13 = bf16[192,768]{1,0:T(8,128)(2,1)S(1)} collective-permute-done((bf16[192,768]{1,0:T(8,128)(2,1)S(1)}, bf16[192,768]{1,0:T(8,128)(2,1)S(1)}, u32[]{:S(2)}, u32[]{:S(2)}) %collective-permute-start.13) | collective-permute-done | bytes 294944 | tf_op jit(solution)/shard_map/ppermute | solution.py:117
  75.7 2.0 %collective-permute-start.15 = (bf16[192,768]{1,0:T(8,128)(2,1)S(1)}, bf16[192,768]{1,0:T(8,128)(2,1)S(1)}, u32[]{:S(2)}, u32[]{:S(2)}) collective-permute-start(bf16[192,768]{1,0:T(8,128)(2,1)S(1)} %broadcast_select_fusion.2), channel_id=1, source_target_pairs={{0,8},{8,0},{16,24},{24,16},{1,9},{9,1},{17,25},{25,17},{2,10},{10... | collective-permute-start | bytes 884744 | tf_op jit(solution)/shard_map/ppermute | solution.py:117
  78.0 1.3 fusion.82
  79.6 5.5 %collective-permute-done.15 = bf16[192,768]{1,0:T(8,128)(2,1)S(1)} collective-permute-done((bf16[192,768]{1,0:T(8,128)(2,1)S(1)}, bf16[192,768]{1,0:T(8,128)(2,1)S(1)}, u32[]{:S(2)}, u32[]{:S(2)}) %collective-permute-start.15) | collective-permute-done | bytes 294944 | tf_op jit(solution)/shard_map/ppermute | solution.py:117
  85.6 2.0 %collective-permute-start.17 = (bf16[192,768]{1,0:T(8,128)(2,1)S(1)}, bf16[192,768]{1,0:T(8,128)(2,1)S(1)}, u32[]{:S(2)}, u32[]{:S(2)}) collective-permute-start(bf16[192,768]{1,0:T(8,128)(2,1)S(1)} %broadcast_select_fusion.1), channel_id=1, source_target_pairs={{0,8},{8,0},{16,24},{24,16},{1,9},{9,1},{17,25},{25,17},{2,10},{10... | collective-permute-start | bytes 884744 | tf_op jit(solution)/shard_map/ppermute | solution.py:117
  88.0 1.3 fusion.80
  89.6 5.5 %collective-permute-done.17 = bf16[192,768]{1,0:T(8,128)(2,1)S(1)} collective-permute-done((bf16[192,768]{1,0:T(8,128)(2,1)S(1)}, bf16[192,768]{1,0:T(8,128)(2,1)S(1)}, u32[]{:S(2)}, u32[]{:S(2)}) %collective-permute-start.17) | collective-permute-done | bytes 294944 | tf_op jit(solution)/shard_map/ppermute | solution.py:117
  95.6 2.0 %collective-permute-start.19 = (bf16[192,768]{1,0:T(8,128)(2,1)S(1)}, bf16[192,768]{1,0:T(8,128)(2,1)S(1)}, u32[]{:S(2)}, u32[]{:S(2)}) collective-permute-start(bf16[192,768]{1,0:T(8,128)(2,1)S(1)} %broadcast_select_fusion), channel_id=1, source_target_pairs={{0,8},{8,0},{16,24},{24,16},{1,9},{9,1},{17,25},{25,17},{2,10},{10... | collective-permute-start | bytes 884744 | tf_op jit(solution)/shard_map/ppermute | solution.py:117
  97.9 1.3 fusion.78
  99.5 5.5 %collective-permute-done.19 = bf16[192,768]{1,0:T(8,128)(2,1)S(1)} collective-permute-done((bf16[192,768]{1,0:T(8,128)(2,1)S(1)}, bf16[192,768]{1,0:T(8,128)(2,1)S(1)}, u32[]{:S(2)}, u32[]{:S(2)}) %collective-permute-start.19) | collective-permute-done | bytes 294944 | tf_op jit(solution)/shard_map/ppermute | solution.py:117
  105.5 2.0 %collective-permute-start.21 = (bf16[192,768]{1,0:T(8,128)(2,1)S(1)}, bf16[192,768]{1,0:T(8,128)(2,1)S(1)}, u32[]{:S(2)}, u32[]{:S(2)}) collective-permute-start(bf16[192,768]{1,0:T(8,128)(2,1)S(1)} %fusion.55), channel_id=1, source_target_pairs={{0,8},{8,0},{16,24},{24,16},{1,9},{9,1},{17,25},{25,17},{2,10},{10... | collective-permute-start | bytes 884744 | tf_op jit(solution)/shard_map/ppermute | solution.py:117
  107.8 1.3 convolution_add_fusion
  109.1 5.8 %collective-permute-done.21 = bf16[192,768]{1,0:T(8,128)(2,1)S(1)} collective-permute-done((bf16[192,768]{1,0:T(8,128)(2,1)S(1)}, bf16[192,768]{1,0:T(8,128)(2,1)S(1)}, u32[]{:S(2)}, u32[]{:S(2)}) %collective-permute-start.21) | collective-permute-done | bytes 294944 | tf_op jit(solution)/shard_map/ppermute | solution.py:117
  117.0 6.8 %collective-permute-done.23 = bf16[192,768]{1,0:T(8,128)(2,1)S(1)} collective-permute-done((bf16[192,768]{1,0:T(8,128)(2,1)S(1)}, bf16[192,768]{1,0:T(8,128)(2,1)S(1)}, u32[]{:S(2)}, u32[]{:S(2)}) %collective-permute-start.23) | collective-permute-done | bytes 294944 | tf_op jit(solution)/shard_map/ppermute | solution.py:117
  125.4 2.0 %collective-permute-done.24 = bf16[96,3072]{1,0:T(8,128)(2,1)S(1)} collective-permute-done((bf16[96,3072]{1,0:T(8,128)(2,1)S(1)}, bf16[96,3072]{1,0:T(8,128)(2,1)S(1)}, u32[]{:S(2)}, u32[]{:S(2)}) %collective-permute-start.24) | collective-permute-done | bytes 589856 | tf_op jit(solution)/shard_map/ppermute | solution.py:34
  129.0 2.3 %collective-permute-start.27 = (bf16[24,3072]{1,0:T(8,128)(2,1)S(1)}, bf16[24,3072]{1,0:T(8,128)(2,1)S(1)}, u32[]{:S(2)}, u32[]{:S(2)}) collective-permute-start(bf16[24,3072]{1,0:T(8,128)(2,1)S(1)} %get-tuple-element.110), channel_id=1, source_target_pairs={{0,6},{1,7},{2,4},{3,5},{4,2},{5,3},{6,0},{7,1},{8,14},{9,15},{10,... | collective-permute-start | bytes 442376 | tf_op jit(solution)/shard_map/ppermute | solution.py:34
  131.2 3.2 %collective-permute-done.25 = bf16[24,3072]{1,0:T(8,128)(2,1)S(1)} collective-permute-done((bf16[24,3072]{1,0:T(8,128)(2,1)S(1)}, bf16[24,3072]{1,0:T(8,128)(2,1)S(1)}, u32[]{:S(2)}, u32[]{:S(2)}) %collective-permute-start.25) | collective-permute-done | bytes 147488 | tf_op jit(solution)/shard_map/ppermute | solution.py:34
  134.4 2.6 %collective-permute-done.26 = bf16[24,3072]{1,0:T(8,128)(2,1)S(1)} collective-permute-done((bf16[24,3072]{1,0:T(8,128)(2,1)S(1)}, bf16[24,3072]{1,0:T(8,128)(2,1)S(1)}, u32[]{:S(2)}, u32[]{:S(2)}) %collective-permute-start.26) | collective-permute-done | bytes 147488 | tf_op jit(solution)/shard_map/ppermute | solution.py:34
  (105 shorter events, 18.6 us)
Async XLA Ops:
  1.1 4.7 %collective-permute-start = (f32[2,24]{1,0:T(2,128)S(1)}, f32[2,24]{1,0:T(2,128)S(1)}, u32[]{:S(2)}, u32[]{:S(2)}) collective-permute-start(f32[2,24]{1,0:T(2,128)S(1)} %pad_maximum_fusion.1), channel_id=1, source_target_pairs={{0,8},{8,0},{16,24},{24,16},{1,9},{9,1},{17,25},{25,17},{2,10},{10... | collective-permute-start | bytes 584 | tf_op jit(solution)/shard_map/ppermute | solution.py:40
  5.8 4.7 %copy-start = (bf16[24,3072]{1,0:T(8,128)(2,1)S(1)}, bf16[24,3072]{1,0:T(8,128)(2,1)}, u32[]{:S(2)}) copy-start(bf16[24,3072]{1,0:T(8,128)(2,1)} %param.7) | copy-start | bytes 442372
  5.8 4.7 %copy-start.3 = (f32[3072]{0:T(1024)S(1)}, f32[3072]{0:T(1024)}, u32[]{:S(2)}) copy-start(f32[3072]{0:T(1024)} %param.9) | copy-start | bytes 36868
  5.8 4.7 %copy-start.4 = (f32[3072]{0:T(1024)S(1)}, f32[3072]{0:T(1024)}, u32[]{:S(2)}) copy-start(f32[3072]{0:T(1024)} %param.8) | copy-start | bytes 36868
  5.8 8.4 %copy-start.1 = (f32[6144]{0:T(1024)S(1)}, f32[6144]{0:T(1024)}, u32[]{:S(2)}) copy-start(f32[6144]{0:T(1024)} %param.11) | copy-start | bytes 73732
  5.8 4.7 %collective-permute-start.1 = (f32[2,24]{1,0:T(2,128)S(1)}, f32[2,24]{1,0:T(2,128)S(1)}, u32[]{:S(2)}, u32[]{:S(2)}) collective-permute-start(f32[2,24]{1,0:T(2,128)S(1)} %fusion.98), channel_id=1, source_target_pairs={{0,16},{8,24},{16,0},{24,8},{1,17},{9,25},{17,1},{25,9},{2,18},{10... | collective-permute-start | bytes 584 | tf_op jit(solution)/shard_map/ppermute | solution.py:40
  10.7 6.1 %collective-permute-start.2 = (bf16[24,3072]{1,0:T(8,128)(2,1)S(1)}, bf16[24,3072]{1,0:T(8,128)(2,1)S(1)}, u32[]{:S(2)}, u32[]{:S(2)}) collective-permute-start(bf16[24,3072]{1,0:T(8,128)(2,1)S(1)} %get-tuple-element.108), channel_id=1, source_target_pairs={{2,0},{3,1},{0,2},{1,3},{6,4},{7,5},{4,6},{5,7},{10,8},{11,9},{8,1... | collective-permute-start | bytes 442376 | tf_op jit(solution)/shard_map/ppermute | solution.py:30
  12.5 5.4 %collective-permute-start.3 = (bf16[24,3072]{1,0:T(8,128)(2,1)S(1)}, bf16[24,3072]{1,0:T(8,128)(2,1)S(1)}, u32[]{:S(2)}, u32[]{:S(2)}) collective-permute-start(bf16[24,3072]{1,0:T(8,128)(2,1)S(1)} %get-tuple-element.108), channel_id=1, source_target_pairs={{4,0},{5,1},{6,2},{7,3},{0,4},{1,5},{2,6},{3,7},{12,8},{13,9},{14,... | collective-permute-start | bytes 442376 | tf_op jit(solution)/shard_map/ppermute | solution.py:30
  14.1 6.0 %collective-permute-start.4 = (bf16[24,3072]{1,0:T(8,128)(2,1)S(1)}, bf16[24,3072]{1,0:T(8,128)(2,1)S(1)}, u32[]{:S(2)}, u32[]{:S(2)}) collective-permute-start(bf16[24,3072]{1,0:T(8,128)(2,1)S(1)} %get-tuple-element.108), channel_id=1, source_target_pairs={{6,0},{7,1},{4,2},{5,3},{2,4},{3,5},{0,6},{1,7},{14,8},{15,9},{12,... | collective-permute-start | bytes 442376 | tf_op jit(solution)/shard_map/ppermute | solution.py:30
  14.2 8.0 %slice-start = ((bf16[3072,6144]{1,0:T(8,128)(2,1)}), bf16[3072,768]{1,0:T(8,128)(2,1)S(1)}, s32[]{:S(2)}) async-start(bf16[3072,6144]{1,0:T(8,128)(2,1)} %param.10), calls=%async_computation | async-start | bytes 9437184 | tf_op jit(solution)/shard_map/slice | solution.py:192
  20.1 2.1 %collective-permute-start.5 = (bf16[96,3072]{1,0:T(8,128)(2,1)S(1)}, bf16[96,3072]{1,0:T(8,128)(2,1)S(1)}, u32[]{:S(2)}, u32[]{:S(2)}) collective-permute-start(bf16[96,3072]{1,0:T(8,128)(2,1)S(1)} %pad_maximum_fusion), channel_id=1, source_target_pairs={{1,0},{0,1},{3,2},{2,3},{5,4},{4,5},{7,6},{6,7},{9,8},{8,9},{11,10... | collective-permute-start | bytes 1769480 | tf_op jit(solution)/shard_map/ppermute | solution.py:30
  23.4 2.3 %slice-start.2 = ((bf16[3072,6144]{1,0:T(8,128)(2,1)}), bf16[3072,768]{1,0:T(8,128)(2,1)S(1)}, s32[]{:S(2)}) async-start(bf16[3072,6144]{1,0:T(8,128)(2,1)} %param.10), calls=%async_computation.2 | async-start | bytes 9437184 | tf_op jit(solution)/shard_map/slice | solution.py:100
  23.4 9.3 %collective-permute-start.6 = (bf16[192,768]{1,0:T(8,128)(2,1)S(1)}, bf16[192,768]{1,0:T(8,128)(2,1)S(1)}, u32[]{:S(2)}, u32[]{:S(2)}) collective-permute-start(bf16[192,768]{1,0:T(8,128)(2,1)S(1)} %convolution_convert_fusion.7), channel_id=1, source_target_pairs={{0,8},{8,0},{16,24},{24,16},{1,9},{9,1},{17,25},{25,17},{2,10},{10... | collective-permute-start | bytes 884744 | tf_op jit(solution)/shard_map/ppermute | solution.py:117
  26.8 2.3 %slice-start.3 = ((bf16[3072,6144]{1,0:T(8,128)(2,1)}), bf16[3072,768]{1,0:T(8,128)(2,1)S(1)}, s32[]{:S(2)}) async-start(bf16[3072,6144]{1,0:T(8,128)(2,1)} %param.10), calls=%async_computation.3 | async-start | bytes 9437184 | tf_op jit(solution)/shard_map/slice | solution.py:100
  29.2 2.3 %slice-start.1 = ((bf16[3072,6144]{1,0:T(8,128)(2,1)}), bf16[3072,768]{1,0:T(8,128)(2,1)S(1)}, s32[]{:S(2)}) async-start(bf16[3072,6144]{1,0:T(8,128)(2,1)} %param.10), calls=%async_computation.1 | async-start | bytes 9437184 | tf_op jit(solution)/shard_map/slice | solution.py:100
  32.7 9.1 %collective-permute-start.7 = (bf16[192,768]{1,0:T(8,128)(2,1)S(1)}, bf16[192,768]{1,0:T(8,128)(2,1)S(1)}, u32[]{:S(2)}, u32[]{:S(2)}) collective-permute-start(bf16[192,768]{1,0:T(8,128)(2,1)S(1)} %convolution_convert_fusion.6), channel_id=1, source_target_pairs={{0,8},{8,0},{16,24},{24,16},{1,9},{9,1},{17,25},{25,17},{2,10},{10... | collective-permute-start | bytes 884744 | tf_op jit(solution)/shard_map/ppermute | solution.py:117
  34.4 3.5 %collective-permute-start.8 = (bf16[192,768]{1,0:T(8,128)(2,1)S(1)}, bf16[192,768]{1,0:T(8,128)(2,1)S(1)}, u32[]{:S(2)}, u32[]{:S(2)}) collective-permute-start(bf16[192,768]{1,0:T(8,128)(2,1)S(1)} %add_convert_fusion.7), channel_id=1, source_target_pairs={{0,1},{1,0},{2,3},{3,2},{4,5},{5,4},{6,7},{7,6},{8,16},{9,17},{10,... | collective-permute-start | bytes 884744 | tf_op jit(solution)/shard_map/ppermute | solution.py:120
  34.5 2.3 %slice-start.4 = ((bf16[3072,6144]{1,0:T(8,128)(2,1)}), bf16[3072,768]{1,0:T(8,128)(2,1)S(1)}, s32[]{:S(2)}) async-start(bf16[3072,6144]{1,0:T(8,128)(2,1)} %param.10), calls=%async_computation.4 | async-start | bytes 9437184 | tf_op jit(solution)/shard_map/slice | solution.py:100
  41.8 8.5 %collective-permute-start.10 = (bf16[192,768]{1,0:T(8,128)(2,1)S(1)}, bf16[192,768]{1,0:T(8,128)(2,1)S(1)}, u32[]{:S(2)}, u32[]{:S(2)}) collective-permute-start(bf16[192,768]{1,0:T(8,128)(2,1)S(1)} %add_convert_fusion.6), channel_id=1, source_target_pairs={{0,1},{1,0},{2,3},{3,2},{4,5},{5,4},{6,7},{7,6},{8,16},{9,17},{10,... | collective-permute-start | bytes 884744 | tf_op jit(solution)/shard_map/ppermute | solution.py:120
  42.2 10.5 %collective-permute-start.9 = (bf16[192,768]{1,0:T(8,128)(2,1)S(1)}, bf16[192,768]{1,0:T(8,128)(2,1)S(1)}, u32[]{:S(2)}, u32[]{:S(2)}) collective-permute-start(bf16[192,768]{1,0:T(8,128)(2,1)S(1)} %broadcast_select_fusion.5), channel_id=1, source_target_pairs={{0,8},{8,0},{16,24},{24,16},{1,9},{9,1},{17,25},{25,17},{2,10},{10... | collective-permute-start | bytes 884744 | tf_op jit(solution)/shard_map/ppermute | solution.py:117
  46.9 2.3 %slice-start.5 = ((bf16[3072,6144]{1,0:T(8,128)(2,1)}), bf16[3072,768]{1,0:T(8,128)(2,1)S(1)}, s32[]{:S(2)}) async-start(bf16[3072,6144]{1,0:T(8,128)(2,1)} %param.10), calls=%async_computation.5 | async-start | bytes 9437184 | tf_op jit(solution)/shard_map/slice | solution.py:100
  49.2 3.6 %slice-start.8 = ((bf16[6144,3072]{1,0:T(8,128)(2,1)}), bf16[768,3072]{1,0:T(8,128)(2,1)S(1)}, s32[]{:S(2)}) async-start(bf16[6144,3072]{1,0:T(8,128)(2,1)} %param.12), calls=%async_computation.8 | async-start | bytes 9437184 | tf_op jit(solution)/shard_map/slice | solution.py:100
  54.1 6.2 %collective-permute-start.12 = (bf16[192,768]{1,0:T(8,128)(2,1)S(1)}, bf16[192,768]{1,0:T(8,128)(2,1)S(1)}, u32[]{:S(2)}, u32[]{:S(2)}) collective-permute-start(bf16[192,768]{1,0:T(8,128)(2,1)S(1)} %add_convert_fusion.5), channel_id=1, source_target_pairs={{0,1},{1,0},{2,3},{3,2},{4,5},{5,4},{6,7},{7,6},{8,16},{9,17},{10,... | collective-permute-start | bytes 884744 | tf_op jit(solution)/shard_map/ppermute | solution.py:120
  54.5 9.5 %collective-permute-start.11 = (bf16[192,768]{1,0:T(8,128)(2,1)S(1)}, bf16[192,768]{1,0:T(8,128)(2,1)S(1)}, u32[]{:S(2)}, u32[]{:S(2)}) collective-permute-start(bf16[192,768]{1,0:T(8,128)(2,1)S(1)} %broadcast_select_fusion.4), channel_id=1, source_target_pairs={{0,8},{8,0},{16,24},{24,16},{1,9},{9,1},{17,25},{25,17},{2,10},{10... | collective-permute-start | bytes 884744 | tf_op jit(solution)/shard_map/ppermute | solution.py:117
  56.9 2.3 %slice-start.6 = ((bf16[3072,6144]{1,0:T(8,128)(2,1)}), bf16[3072,768]{1,0:T(8,128)(2,1)S(1)}, s32[]{:S(2)}) async-start(bf16[3072,6144]{1,0:T(8,128)(2,1)} %param.10), calls=%async_computation.6 | async-start | bytes 9437184 | tf_op jit(solution)/shard_map/slice | solution.py:100
  59.2 4.9 %slice-start.9 = ((bf16[6144,3072]{1,0:T(8,128)(2,1)}), bf16[768,3072]{1,0:T(8,128)(2,1)S(1)}, s32[]{:S(2)}) async-start(bf16[6144,3072]{1,0:T(8,128)(2,1)} %param.12), calls=%async_computation.9 | async-start | bytes 9437184 | tf_op jit(solution)/shard_map/slice | solution.py:100
  65.3 6.0 %collective-permute-start.14 = (bf16[192,768]{1,0:T(8,128)(2,1)S(1)}, bf16[192,768]{1,0:T(8,128)(2,1)S(1)}, u32[]{:S(2)}, u32[]{:S(2)}) collective-permute-start(bf16[192,768]{1,0:T(8,128)(2,1)S(1)} %add_convert_fusion.4), channel_id=1, source_target_pairs={{0,1},{1,0},{2,3},{3,2},{4,5},{5,4},{6,7},{7,6},{8,16},{9,17},{10,... | collective-permute-start | bytes 884744 | tf_op jit(solution)/shard_map/ppermute | solution.py:120
  65.7 9.5 %collective-permute-start.13 = (bf16[192,768]{1,0:T(8,128)(2,1)S(1)}, bf16[192,768]{1,0:T(8,128)(2,1)S(1)}, u32[]{:S(2)}, u32[]{:S(2)}) collective-permute-start(bf16[192,768]{1,0:T(8,128)(2,1)S(1)} %broadcast_select_fusion.3), channel_id=1, source_target_pairs={{0,8},{8,0},{16,24},{24,16},{1,9},{9,1},{17,25},{25,17},{2,10},{10... | collective-permute-start | bytes 884744 | tf_op jit(solution)/shard_map/ppermute | solution.py:117
  75.3 4.3 %collective-permute-start.16 = (bf16[192,768]{1,0:T(8,128)(2,1)S(1)}, bf16[192,768]{1,0:T(8,128)(2,1)S(1)}, u32[]{:S(2)}, u32[]{:S(2)}) collective-permute-start(bf16[192,768]{1,0:T(8,128)(2,1)S(1)} %add_convert_fusion.3), channel_id=1, source_target_pairs={{0,1},{1,0},{2,3},{3,2},{4,5},{5,4},{6,7},{7,6},{8,16},{9,17},{10,... | collective-permute-start | bytes 884744 | tf_op jit(solution)/shard_map/ppermute | solution.py:120
  75.7 2.3 %slice-start.10 = ((bf16[6144,3072]{1,0:T(8,128)(2,1)}), bf16[768,3072]{1,0:T(8,128)(2,1)S(1)}, s32[]{:S(2)}) async-start(bf16[6144,3072]{1,0:T(8,128)(2,1)} %param.12), calls=%async_computation.10 | async-start | bytes 9437184 | tf_op jit(solution)/shard_map/slice | solution.py:100
  75.7 9.5 %collective-permute-start.15 = (bf16[192,768]{1,0:T(8,128)(2,1)S(1)}, bf16[192,768]{1,0:T(8,128)(2,1)S(1)}, u32[]{:S(2)}, u32[]{:S(2)}) collective-permute-start(bf16[192,768]{1,0:T(8,128)(2,1)S(1)} %broadcast_select_fusion.2), channel_id=1, source_target_pairs={{0,8},{8,0},{16,24},{24,16},{1,9},{9,1},{17,25},{25,17},{2,10},{10... | collective-permute-start | bytes 884744 | tf_op jit(solution)/shard_map/ppermute | solution.py:117
  85.2 4.3 %collective-permute-start.18 = (bf16[192,768]{1,0:T(8,128)(2,1)S(1)}, bf16[192,768]{1,0:T(8,128)(2,1)S(1)}, u32[]{:S(2)}, u32[]{:S(2)}) collective-permute-start(bf16[192,768]{1,0:T(8,128)(2,1)S(1)} %add_convert_fusion.2), channel_id=1, source_target_pairs={{0,1},{1,0},{2,3},{3,2},{4,5},{5,4},{6,7},{7,6},{8,16},{9,17},{10,... | collective-permute-start | bytes 884744 | tf_op jit(solution)/shard_map/ppermute | solution.py:120
  85.6 2.3 %slice-start.11 = ((bf16[6144,3072]{1,0:T(8,128)(2,1)}), bf16[768,3072]{1,0:T(8,128)(2,1)S(1)}, s32[]{:S(2)}) async-start(bf16[6144,3072]{1,0:T(8,128)(2,1)} %param.12), calls=%async_computation.11 | async-start | bytes 9437184 | tf_op jit(solution)/shard_map/slice | solution.py:100
  85.6 9.5 %collective-permute-start.17 = (bf16[192,768]{1,0:T(8,128)(2,1)S(1)}, bf16[192,768]{1,0:T(8,128)(2,1)S(1)}, u32[]{:S(2)}, u32[]{:S(2)}) collective-permute-start(bf16[192,768]{1,0:T(8,128)(2,1)S(1)} %broadcast_select_fusion.1), channel_id=1, source_target_pairs={{0,8},{8,0},{16,24},{24,16},{1,9},{9,1},{17,25},{25,17},{2,10},{10... | collective-permute-start | bytes 884744 | tf_op jit(solution)/shard_map/ppermute | solution.py:117
  95.2 4.3 %collective-permute-start.20 = (bf16[192,768]{1,0:T(8,128)(2,1)S(1)}, bf16[192,768]{1,0:T(8,128)(2,1)S(1)}, u32[]{:S(2)}, u32[]{:S(2)}) collective-permute-start(bf16[192,768]{1,0:T(8,128)(2,1)S(1)} %add_convert_fusion.1), channel_id=1, source_target_pairs={{0,1},{1,0},{2,3},{3,2},{4,5},{5,4},{6,7},{7,6},{8,16},{9,17},{10,... | collective-permute-start | bytes 884744 | tf_op jit(solution)/shard_map/ppermute | solution.py:120
  95.6 2.3 %slice-start.12 = ((bf16[6144,3072]{1,0:T(8,128)(2,1)}), bf16[768,3072]{1,0:T(8,128)(2,1)S(1)}, s32[]{:S(2)}) async-start(bf16[6144,3072]{1,0:T(8,128)(2,1)} %param.12), calls=%async_computation.12 | async-start | bytes 9437184 | tf_op jit(solution)/shard_map/slice | solution.py:100
  95.6 9.5 %collective-permute-start.19 = (bf16[192,768]{1,0:T(8,128)(2,1)S(1)}, bf16[192,768]{1,0:T(8,128)(2,1)S(1)}, u32[]{:S(2)}, u32[]{:S(2)}) collective-permute-start(bf16[192,768]{1,0:T(8,128)(2,1)S(1)} %broadcast_select_fusion), channel_id=1, source_target_pairs={{0,8},{8,0},{16,24},{24,16},{1,9},{9,1},{17,25},{25,17},{2,10},{10... | collective-permute-start | bytes 884744 | tf_op jit(solution)/shard_map/ppermute | solution.py:117
  105.1 4.0 %collective-permute-start.22 = (bf16[192,768]{1,0:T(8,128)(2,1)S(1)}, bf16[192,768]{1,0:T(8,128)(2,1)S(1)}, u32[]{:S(2)}, u32[]{:S(2)}) collective-permute-start(bf16[192,768]{1,0:T(8,128)(2,1)S(1)} %add_convert_fusion), channel_id=1, source_target_pairs={{0,1},{1,0},{2,3},{3,2},{4,5},{5,4},{6,7},{7,6},{8,16},{9,17},{10,... | collective-permute-start | bytes 884744 | tf_op jit(solution)/shard_map/ppermute | solution.py:120
  105.5 2.3 %slice-start.13 = ((bf16[6144,3072]{1,0:T(8,128)(2,1)}), bf16[768,3072]{1,0:T(8,128)(2,1)S(1)}, s32[]{:S(2)}) async-start(bf16[6144,3072]{1,0:T(8,128)(2,1)} %param.12), calls=%async_computation.13 | async-start | bytes 9437184 | tf_op jit(solution)/shard_map/slice | solution.py:100
  105.5 9.5 %collective-permute-start.21 = (bf16[192,768]{1,0:T(8,128)(2,1)S(1)}, bf16[192,768]{1,0:T(8,128)(2,1)S(1)}, u32[]{:S(2)}, u32[]{:S(2)}) collective-permute-start(bf16[192,768]{1,0:T(8,128)(2,1)S(1)} %fusion.55), channel_id=1, source_target_pairs={{0,8},{8,0},{16,24},{24,16},{1,9},{9,1},{17,25},{25,17},{2,10},{10... | collective-permute-start | bytes 884744 | tf_op jit(solution)/shard_map/ppermute | solution.py:117
  107.8 7.8 %slice-start.14 = ((bf16[6144,3072]{1,0:T(8,128)(2,1)}), bf16[768,3072]{1,0:T(8,128)(2,1)S(1)}, s32[]{:S(2)}) async-start(bf16[6144,3072]{1,0:T(8,128)(2,1)} %param.12), calls=%async_computation.14 | async-start | bytes 9437184 | tf_op jit(solution)/shard_map/slice | solution.py:100
  115.2 8.6 %collective-permute-start.23 = (bf16[192,768]{1,0:T(8,128)(2,1)S(1)}, bf16[192,768]{1,0:T(8,128)(2,1)S(1)}, u32[]{:S(2)}, u32[]{:S(2)}) collective-permute-start(bf16[192,768]{1,0:T(8,128)(2,1)S(1)} %fusion.63), channel_id=1, source_target_pairs={{0,8},{8,0},{16,24},{24,16},{1,9},{9,1},{17,25},{25,17},{2,10},{10... | collective-permute-start | bytes 884744 | tf_op jit(solution)/shard_map/ppermute | solution.py:117
  116.7 7.2 %slice-start.15 = ((bf16[6144,3072]{1,0:T(8,128)(2,1)}), bf16[768,3072]{1,0:T(8,128)(2,1)S(1)}, s32[]{:S(2)}) async-start(bf16[6144,3072]{1,0:T(8,128)(2,1)} %param.12), calls=%async_computation.15 | async-start | bytes 9437184 | tf_op jit(solution)/shard_map/slice | solution.py:100
  125.3 11.7 %copy-start.2 = (f32[3072]{0:T(1024)S(1)}, f32[3072]{0:T(1024)}, u32[]{:S(2)}) copy-start(f32[3072]{0:T(1024)} %param.13) | copy-start | bytes 36868
  125.4 2.1 %collective-permute-start.24 = (bf16[96,3072]{1,0:T(8,128)(2,1)S(1)}, bf16[96,3072]{1,0:T(8,128)(2,1)S(1)}, u32[]{:S(2)}, u32[]{:S(2)}) collective-permute-start(bf16[96,3072]{1,0:T(8,128)(2,1)S(1)} %slice.148), channel_id=1, source_target_pairs={{0,1},{1,0},{2,3},{3,2},{4,5},{5,4},{6,7},{7,6},{8,9},{9,8},{10,11... | collective-permute-start | bytes 1769480 | tf_op jit(solution)/shard_map/ppermute | solution.py:34
  127.7 6.8 %collective-permute-start.25 = (bf16[24,3072]{1,0:T(8,128)(2,1)S(1)}, bf16[24,3072]{1,0:T(8,128)(2,1)S(1)}, u32[]{:S(2)}, u32[]{:S(2)}) collective-permute-start(bf16[24,3072]{1,0:T(8,128)(2,1)S(1)} %get-tuple-element.109), channel_id=1, source_target_pairs={{0,2},{1,3},{2,0},{3,1},{4,6},{5,7},{6,4},{7,5},{8,10},{9,11},{10,... | collective-permute-start | bytes 442376 | tf_op jit(solution)/shard_map/ppermute | solution.py:34
  128.3 8.8 %collective-permute-start.26 = (bf16[24,3072]{1,0:T(8,128)(2,1)S(1)}, bf16[24,3072]{1,0:T(8,128)(2,1)S(1)}, u32[]{:S(2)}, u32[]{:S(2)}) collective-permute-start(bf16[24,3072]{1,0:T(8,128)(2,1)S(1)} %get-tuple-element.111), channel_id=1, source_target_pairs={{0,4},{1,5},{2,6},{3,7},{4,0},{5,1},{6,2},{7,3},{8,12},{9,13},{10,... | collective-permute-start | bytes 442376 | tf_op jit(solution)/shard_map/ppermute | solution.py:34
  129.0 8.1 %collective-permute-start.27 = (bf16[24,3072]{1,0:T(8,128)(2,1)S(1)}, bf16[24,3072]{1,0:T(8,128)(2,1)S(1)}, u32[]{:S(2)}, u32[]{:S(2)}) collective-permute-start(bf16[24,3072]{1,0:T(8,128)(2,1)S(1)} %get-tuple-element.110), channel_id=1, source_target_pairs={{0,6},{1,7},{2,4},{3,5},{4,2},{5,3},{6,0},{7,1},{8,14},{9,15},{10,... | collective-permute-start | bytes 442376 | tf_op jit(solution)/shard_map/ppermute | solution.py:34
  (1 other events, 2.3 us)

commit v2 on v1

--- a/solution.py
+++ b/solution.py
@@ -9,7 +9,7 @@
 
 SHARES = (3, 3, 3, 3, 3, 3, 3, 3)
 UP_AHEAD = 3
-DOWN_AHEAD = 2
+DOWN_AHEAD = 3
 
 
 class Grid:
@@ -47,13 +47,13 @@
     for k in range(1, grid.side * grid.side):
         held.append(grid.take(own, k // grid.side, k % grid.side, 0))
     held = jnp.concatenate(held)
-    return jnp.concatenate([held, grid.take(held, 0, 0, 1)])
-
-
-def scatter_sum(grid, terms):
-    half = terms.shape[0] // grid.cores
-    other = grid.give(terms[half:].astype(jnp.bfloat16), 0, 0, 1)
-    pair = terms[:half] + other.astype(jnp.float32)
+    return held, grid.take(held, 0, 0, 1)
+
+
+def scatter_sum(grid, kept, given):
+    half = kept.shape[0]
+    other = grid.give(given.astype(jnp.bfloat16), 0, 0, 1)
+    pair = kept + other.astype(jnp.float32)
     rows = half // (grid.side * grid.side)
     total = pair[:rows]
     sent = pair.astype(jnp.bfloat16)
@@ -63,9 +63,10 @@
     return total
 
 
-def chained_middle(grid, gathered, w_up, up_bias, w_down):
-    n_row, tokens = grid.n_row, gathered.shape[0]
-    half = tokens // 2
+def chained_middle(grid, held, swapped, w_up, up_bias, w_down):
+    n_row = grid.n_row
+    gathered = jnp.concatenate([held, swapped])
+    half = held.shape[0]
     row = lax.axis_index("row")
     middle = n_row // 2
     upper = row >= middle
@@ -85,7 +86,8 @@
     for hop in range(middle - 1):
         got = lax.ppermute(out, "row", outward)
         out = jnp.where(depth == middle - 2 - hop, got, out)
-    return jnp.dot(out, w_down, preferred_element_type=jnp.float32)
+    terms = jnp.dot(out, w_down, preferred_element_type=jnp.float32)
+    return terms[:half], terms[half:]
 
 
 def chunk_edges(units):
@@ -100,7 +102,7 @@
     return lax.optimization_barrier(lax.slice_in_dim(weights, low, high, axis=axis))
 
 
-def four_rows(grid, is_end, early, gathered, w_up, up_bias, w_down):
+def four_rows(grid, is_end, early, held, swapped, w_up, up_bias, w_down):
     facing = [(0, 1), (1, 0), (2, 3), (3, 2)]
     across = []
     for i in range(grid.n_row * grid.n_col):
@@ -128,6 +130,8 @@
         k = t - 3 + DOWN_AHEAD
         if 0 <= k < count:
             down_part[k] = cut(w_down, 0, edges[k], edges[k + 1], after)
+        if k == count - 1:
+            down_part[count] = cut(w_down, 0, edges[k], edges[k + 1], down_part[k])
 
     def up(k):
         return jnp.dot(gathered, up_part[k], preferred_element_type=jnp.float32).astype(jnp.bfloat16)
@@ -138,13 +142,17 @@
     def widened(v, width):
         return v if v.shape[1] == width else jnp.pad(v, ((0, 0), (0, width - v.shape[1])))
 
+    gathered, half = jnp.concatenate([held, swapped]), held.shape[0]
     for k in range(len(early), UP_AHEAD):
         up_part[k] = cut(w_up, 1, edges[k], edges[k + 1], gathered)
-    partial, sums, own, hidden = {0: up(0)}, {}, {}, {}
+    first = [jnp.dot(v, up_part[0], preferred_element_type=jnp.float32).astype(jnp.bfloat16) for v in (held, swapped)]
+    partial, sums, own, hidden = {0: jnp.concatenate(first)}, {}, {}, {}
     terms = None
-    for t in range(count + 2):
+    for t in range(count + 1):
         crossed = None
-        if t < 2:
+        if t == 0:
+            faced = jnp.concatenate([face(v, facing) for v in first])
+        elif t == 1:
             faced = face(partial[t], facing)
         elif t < count:
             width = max(size[t], size[t - 2])
@@ -179,7 +187,17 @@
             sums[t] = (partial[t].astype(jnp.float32) + faced[:, : size[t]].astype(jnp.float32)).astype(jnp.bfloat16)
         if t >= 2:
             hidden[t - 2] = jnp.where(is_end, faced[:, : size[t - 2]], own[t - 2])
-    return terms + down(count - 1)
+    last = own[count - 1]
+    given = face(last[half:], facing)
+    kept = face(last[:half], facing)
+    terms = terms + down(count - 2)
+
+    def finish(came, mine, before, weights):
+        rows = jnp.where(is_end, came, mine)
+        return before + jnp.dot(rows, weights, preferred_element_type=jnp.float32)
+
+    given = finish(given, last[half:], terms[half:], down_part[count - 1])
+    return finish(kept, last[:half], terms[:half], down_part[count]), given
 
 
 def local(grid, inputs, ln_gain, ln_bias, w_up, up_bias, w_down, down_bias):
@@ -199,12 +217,12 @@
     normed = (normed * ln_gain + ln_bias).astype(jnp.bfloat16)
     if grid.n_row == 4:
         early.append(cut(w_up, 1, edges[1], edges[2], normed))
-    gathered = gather(grid, normed)
+    held, swapped = gather(grid, normed)
     if grid.n_row == 4:
-        terms = four_rows(grid, is_end, early, gathered, w_up, up_bias, w_down)
+        terms = four_rows(grid, is_end, early, held, swapped, w_up, up_bias, w_down)
     else:
-        terms = chained_middle(grid, gathered, w_up, up_bias, w_down)
-    down_sum = scatter_sum(grid, terms)
+        terms = chained_middle(grid, held, swapped, w_up, up_bias, w_down)
+    down_sum = scatter_sum(grid, *terms)
     return (in_float + down_sum + down_bias).astype(jnp.bfloat16)
 
 

time: 138 us -> 140 us (1.014)
  local copies, waits for them, and re-layouts: 14.9 us -> 19.6 us
  starting transfers between devices: 34.5 us -> 30 us
    ppermute x10 -> x12, waiting for transfers between devices: 43 us -> 48.9 us  [face(): return lax.ppermute(sent, 'row', pairs)]
    ppermute x10 -> x12, starting transfers between devices: 20.5 us -> 16 us  [face(): return lax.ppermute(sent, 'row', pairs)]
    dot_general x0 -> x4, matrix products: none -> 3.61 us  [the longest x2 1.84 us: finish(): return before + jnp.dot(rows, weights, preferred_element_type=jnp.float32)]
    slice x2 -> x1, local copies, waits for them, and re-layouts: 0.01 us -> 2.64 us  [local(): lax.slice_in_dim(w_first, edges[0], edges[1], axis=1)]
    ppermute x4, waiting for transfers between devices: 7.82 us -> 5.45 us  [give(): return lax.ppermute(value, 'col', pairs)]
    slice x30 -> x32, local copies, waits for them, and re-layouts: 14.7 us -> 16.8 us  [cut(): lax.slice_in_dim(weights, low, high, axis=axis)]
    ppermute x4, waiting for transfers between devices: 7.81 us -> 5.87 us  [take(): return lax.ppermute(value, 'col', pairs)]
    ppermute x2, waiting for transfers between devices: 3.11 us -> 1.56 us  [row_sum(): lax.ppermute(value, 'row', [(i, i ^ step) for i in range(grid.n_row)])]
  transfers between devices with their start and end apart: 28 -> 30, of which waited for: 18 -> 15; matrix products, arithmetic and copies ran while one was open for 13% -> 16% of each run, Pallas kernels for 0% -> 0%
where the time goes in v2:
time: 140 us; the launch traced here: 139 us
  waiting for transfers between devices  61.8 us (44%)
  starting transfers between devices  30 us (21%)
  matrix products  19.9 us (14%)
  local copies, waits for them, and re-layouts  19.6 us (14%)
  other arithmetic  7.11 us (5%)
    ppermute x12, waiting for transfers between devices, face(): return lax.ppermute(sent, 'row', pairs)  48.9 us
    slice x32, local copies, waits for them, and re-layouts, cut(): lax.slice_in_dim(weights, low, high, axis=axis)  16.8 us
    ppermute x12, starting transfers between devices, face(): return lax.ppermute(sent, 'row', pairs)  16 us
    dot_general x7, matrix products, down(): return jnp.dot(hidden[k], down_part[k], preferred_element_type=jnp.float32)  8.66 us
    dot_general x7, matrix products, up(): jnp.dot(gathered, up_part[k], preferred_element_type=jnp.float32)  7.66 us
    ppermute x2, starting transfers between devices, row_sum(): lax.ppermute(value, 'row', [(i, i ^ step) for i in range(grid.n_row)])  6.21 us
    ppermute x4, waiting for transfers between devices, take(): return lax.ppermute(value, 'col', pairs)  5.87 us
    ppermute x4, waiting for transfers between devices, give(): return lax.ppermute(value, 'col', pairs)  5.45 us
  transfers between devices with their start and end apart: 30, of which 15 were waited for; matrix products, arithmetic and copies ran while one was open for 16% of the time, Pallas kernels for 0%

profile of v2, /device:TPU:0, one launch (start us, length us, event | category | flops | bytes accessed | tf_op | source)
XLA Modules:
  0.0 139.1 jit_solution(16470657958038155004)
XLA Ops:
  1.1 3.1 %collective-permute-start = (f32[2,24]{1,0:T(2,128)S(1)}, f32[2,24]{1,0:T(2,128)S(1)}, u32[]{:S(2)}, u32[]{:S(2)}) collective-permute-start(f32[2,24]{1,0:T(2,128)S(1)} %pad_maximum_fusion.3), channel_id=1, source_target_pairs={{0,8},{8,0},{16,24},{24,16},{1,9},{9,1},{17,25},{25,17},{2,10},{10... | collective-permute-start | bytes 584 | tf_op jit(solution)/shard_map/ppermute | solution.py:40
  4.2 1.6 %collective-permute-done = f32[2,24]{1,0:T(2,128)S(1)} collective-permute-done((f32[2,24]{1,0:T(2,128)S(1)}, f32[2,24]{1,0:T(2,128)S(1)}, u32[]{:S(2)}, u32[]{:S(2)}) %collective-permute-start) | collective-permute-done | bytes 224 | tf_op jit(solution)/shard_map/ppermute | solution.py:40
  5.8 3.1 %collective-permute-start.1 = (f32[2,24]{1,0:T(2,128)S(1)}, f32[2,24]{1,0:T(2,128)S(1)}, u32[]{:S(2)}, u32[]{:S(2)}) collective-permute-start(f32[2,24]{1,0:T(2,128)S(1)} %fusion.108), channel_id=1, source_target_pairs={{0,16},{8,24},{16,0},{24,8},{1,17},{9,25},{17,1},{25,9},{2,18},{10... | collective-permute-start | bytes 584 | tf_op jit(solution)/shard_map/ppermute | solution.py:40
  8.9 2.6 %slice.109 = bf16[3072,768]{1,0:T(8,128)(2,1)S(1)} slice(bf16[3072,6144]{1,0:T(8,128)(2,1)} %param.10), slice={[0:3072], [0:768]} | slice | bytes 9437184 | tf_op jit(solution)/shard_map/slice | solution.py:210
  11.8 1.6 %collective-permute-start.2 = (bf16[24,3072]{1,0:T(8,128)(2,1)S(1)}, bf16[24,3072]{1,0:T(8,128)(2,1)S(1)}, u32[]{:S(2)}, u32[]{:S(2)}) collective-permute-start(bf16[24,3072]{1,0:T(8,128)(2,1)S(1)} %get-tuple-element.104), channel_id=1, source_target_pairs={{2,0},{3,1},{0,2},{1,3},{6,4},{7,5},{4,6},{5,7},{10,8},{11,9},{8,1... | collective-permute-start | bytes 442376 | tf_op jit(solution)/shard_map/ppermute | solution.py:30
  13.3 1.5 %collective-permute-start.3 = (bf16[24,3072]{1,0:T(8,128)(2,1)S(1)}, bf16[24,3072]{1,0:T(8,128)(2,1)S(1)}, u32[]{:S(2)}, u32[]{:S(2)}) collective-permute-start(bf16[24,3072]{1,0:T(8,128)(2,1)S(1)} %get-tuple-element.104), channel_id=1, source_target_pairs={{4,0},{5,1},{6,2},{7,3},{0,4},{1,5},{2,6},{3,7},{12,8},{13,9},{14,... | collective-permute-start | bytes 442376 | tf_op jit(solution)/shard_map/ppermute | solution.py:30
  15.3 3.1 %collective-permute-done.2 = bf16[24,3072]{1,0:T(8,128)(2,1)S(1)} collective-permute-done((bf16[24,3072]{1,0:T(8,128)(2,1)S(1)}, bf16[24,3072]{1,0:T(8,128)(2,1)S(1)}, u32[]{:S(2)}, u32[]{:S(2)}) %collective-permute-start.2) | collective-permute-done | bytes 147488 | tf_op jit(solution)/shard_map/ppermute | solution.py:30
  18.4 2.8 %collective-permute-done.3 = bf16[24,3072]{1,0:T(8,128)(2,1)S(1)} collective-permute-done((bf16[24,3072]{1,0:T(8,128)(2,1)S(1)}, bf16[24,3072]{1,0:T(8,128)(2,1)S(1)}, u32[]{:S(2)}, u32[]{:S(2)}) %collective-permute-start.3) | collective-permute-done | bytes 147488 | tf_op jit(solution)/shard_map/ppermute | solution.py:30
  22.2 1.7 %collective-permute-start.5 = (bf16[96,768]{1,0:T(8,128)(2,1)S(1)}, bf16[96,768]{1,0:T(8,128)(2,1)S(1)}, u32[]{:S(2)}, u32[]{:S(2)}) collective-permute-start(bf16[96,768]{1,0:T(8,128)(2,1)S(1)} %convolution_convert_fusion.8), channel_id=1, source_target_pairs={{0,8},{8,0},{16,24},{24,16},{1,9},{9,1},{17,25},{25,17},{2,10},{10... | collective-permute-start | bytes 442376 | tf_op jit(solution)/shard_map/ppermute | solution.py:119
  25.9 1.3 slice-done.10
  27.1 1.1 convolution_convert_fusion.4
  28.3 2.3 %slice-done.11 = bf16[3072,768]{1,0:T(8,128)(2,1)S(1)} async-done(((bf16[3072,6144]{1,0:T(8,128)(2,1)}), bf16[3072,768]{1,0:T(8,128)(2,1)S(1)}, s32[]{:S(2)}) %slice-start.11) | async-done | bytes 4718616 | tf_op jit(solution)/shard_map/slice | solution.py:102
  30.6 1.1 convolution_convert_fusion.5
  31.7 1.2 slice-done.9
  32.9 1.1 convolution_convert_fusion.6
  35.3 2.3 %slice-done.12 = bf16[3072,768]{1,0:T(8,128)(2,1)S(1)} async-done(((bf16[3072,6144]{1,0:T(8,128)(2,1)}), bf16[3072,768]{1,0:T(8,128)(2,1)S(1)}, s32[]{:S(2)}) %slice-start.12) | async-done | bytes 4718616 | tf_op jit(solution)/shard_map/slice | solution.py:102
  38.7 4.5 %collective-permute-done.8 = bf16[192,768]{1,0:T(8,128)(2,1)S(1)} collective-permute-done((bf16[192,768]{1,0:T(8,128)(2,1)S(1)}, bf16[192,768]{1,0:T(8,128)(2,1)S(1)}, u32[]{:S(2)}, u32[]{:S(2)}) %collective-permute-start.8) | collective-permute-done | bytes 294944 | tf_op jit(solution)/shard_map/ppermute | solution.py:119
  43.7 2.9 %collective-permute-start.10 = (bf16[192,768]{1,0:T(8,128)(2,1)S(1)}, bf16[192,768]{1,0:T(8,128)(2,1)S(1)}, u32[]{:S(2)}, u32[]{:S(2)}) collective-permute-start(bf16[192,768]{1,0:T(8,128)(2,1)S(1)} %broadcast_select_fusion.5), channel_id=1, source_target_pairs={{0,8},{8,0},{16,24},{24,16},{1,9},{9,1},{17,25},{25,17},{2,10},{10... | collective-permute-start | bytes 884744 | tf_op jit(solution)/shard_map/ppermute | solution.py:119
  46.6 2.3 %slice-done.13 = bf16[3072,768]{1,0:T(8,128)(2,1)S(1)} async-done(((bf16[3072,6144]{1,0:T(8,128)(2,1)}), bf16[3072,768]{1,0:T(8,128)(2,1)S(1)}, s32[]{:S(2)}) %slice-start.13) | async-done | bytes 4718616 | tf_op jit(solution)/shard_map/slice | solution.py:102
  50.1 3.1 %collective-permute-done.10 = bf16[192,768]{1,0:T(8,128)(2,1)S(1)} collective-permute-done((bf16[192,768]{1,0:T(8,128)(2,1)S(1)}, bf16[192,768]{1,0:T(8,128)(2,1)S(1)}, u32[]{:S(2)}, u32[]{:S(2)}) %collective-permute-start.10) | collective-permute-done | bytes 294944 | tf_op jit(solution)/shard_map/ppermute | solution.py:119
  53.3 1.3 fusion.87
  54.9 2.2 %collective-permute-start.12 = (bf16[192,768]{1,0:T(8,128)(2,1)S(1)}, bf16[192,768]{1,0:T(8,128)(2,1)S(1)}, u32[]{:S(2)}, u32[]{:S(2)}) collective-permute-start(bf16[192,768]{1,0:T(8,128)(2,1)S(1)} %broadcast_select_fusion.4), channel_id=1, source_target_pairs={{0,8},{8,0},{16,24},{24,16},{1,9},{9,1},{17,25},{25,17},{2,10},{10... | collective-permute-start | bytes 884744 | tf_op jit(solution)/shard_map/ppermute | solution.py:119
  57.2 2.3 %slice-done.14 = bf16[3072,768]{1,0:T(8,128)(2,1)S(1)} async-done(((bf16[3072,6144]{1,0:T(8,128)(2,1)}), bf16[3072,768]{1,0:T(8,128)(2,1)S(1)}, s32[]{:S(2)}) %slice-start.14) | async-done | bytes 4718616 | tf_op jit(solution)/shard_map/slice | solution.py:102
  59.5 1.1 convolution_convert_fusion.1
  60.6 3.8 %collective-permute-done.12 = bf16[192,768]{1,0:T(8,128)(2,1)S(1)} collective-permute-done((bf16[192,768]{1,0:T(8,128)(2,1)S(1)}, bf16[192,768]{1,0:T(8,128)(2,1)S(1)}, u32[]{:S(2)}, u32[]{:S(2)}) %collective-permute-start.12) | collective-permute-done | bytes 294944 | tf_op jit(solution)/shard_map/ppermute | solution.py:119
  64.5 1.3 fusion.85
  66.1 1.3 collective-permute-start.14
  67.9 1.8 %slice-done.15 = bf16[3072,768]{1,0:T(8,128)(2,1)S(1)} async-done(((bf16[3072,6144]{1,0:T(8,128)(2,1)}), bf16[3072,768]{1,0:T(8,128)(2,1)S(1)}, s32[]{:S(2)}) %slice-start.15) | async-done | bytes 4718616 | tf_op jit(solution)/shard_map/slice | solution.py:102
  69.8 1.1 convolution_convert_fusion
  70.9 4.7 %collective-permute-done.14 = bf16[192,768]{1,0:T(8,128)(2,1)S(1)} collective-permute-done((bf16[192,768]{1,0:T(8,128)(2,1)S(1)}, bf16[192,768]{1,0:T(8,128)(2,1)S(1)}, u32[]{:S(2)}, u32[]{:S(2)}) %collective-permute-start.14) | collective-permute-done | bytes 294944 | tf_op jit(solution)/shard_map/ppermute | solution.py:119
  76.1 1.3 collective-permute-start.16
  78.4 1.3 fusion.83
  80.0 5.5 %collective-permute-done.16 = bf16[192,768]{1,0:T(8,128)(2,1)S(1)} collective-permute-done((bf16[192,768]{1,0:T(8,128)(2,1)S(1)}, bf16[192,768]{1,0:T(8,128)(2,1)S(1)}, u32[]{:S(2)}, u32[]{:S(2)}) %collective-permute-start.16) | collective-permute-done | bytes 294944 | tf_op jit(solution)/shard_map/ppermute | solution.py:119
  86.0 1.3 collective-permute-start.18
  88.4 1.3 fusion.81
  90.0 5.5 %collective-permute-done.18 = bf16[192,768]{1,0:T(8,128)(2,1)S(1)} collective-permute-done((bf16[192,768]{1,0:T(8,128)(2,1)S(1)}, bf16[192,768]{1,0:T(8,128)(2,1)S(1)}, u32[]{:S(2)}, u32[]{:S(2)}) %collective-permute-start.18) | collective-permute-done | bytes 294944 | tf_op jit(solution)/shard_map/ppermute | solution.py:119
  96.0 1.3 collective-permute-start.20
  98.3 1.3 fusion.79
  99.9 5.5 %collective-permute-done.20 = bf16[192,768]{1,0:T(8,128)(2,1)S(1)} collective-permute-done((bf16[192,768]{1,0:T(8,128)(2,1)S(1)}, bf16[192,768]{1,0:T(8,128)(2,1)S(1)}, u32[]{:S(2)}, u32[]{:S(2)}) %collective-permute-start.20) | collective-permute-done | bytes 294944 | tf_op jit(solution)/shard_map/ppermute | solution.py:119
  105.9 1.3 collective-permute-start.22
  107.2 1.3 fusion.77
  108.8 6.6 %collective-permute-done.22 = bf16[192,768]{1,0:T(8,128)(2,1)S(1)} collective-permute-done((bf16[192,768]{1,0:T(8,128)(2,1)S(1)}, bf16[192,768]{1,0:T(8,128)(2,1)S(1)}, u32[]{:S(2)}, u32[]{:S(2)}) %collective-permute-start.22) | collective-permute-done | bytes 294944 | tf_op jit(solution)/shard_map/ppermute | solution.py:119
  116.0 1.1 fusion.75
  117.5 3.6 %collective-permute-done.25 = bf16[96,768]{1,0:T(8,128)(2,1)S(1)} collective-permute-done((bf16[96,768]{1,0:T(8,128)(2,1)S(1)}, bf16[96,768]{1,0:T(8,128)(2,1)S(1)}, u32[]{:S(2)}, u32[]{:S(2)}) %collective-permute-start.25) | collective-permute-done | bytes 147488 | tf_op jit(solution)/shard_map/ppermute | solution.py:119
  122.4 5.9 %collective-permute-done.24 = bf16[96,768]{1,0:T(8,128)(2,1)S(1)} collective-permute-done((bf16[96,768]{1,0:T(8,128)(2,1)S(1)}, bf16[96,768]{1,0:T(8,128)(2,1)S(1)}, u32[]{:S(2)}, u32[]{:S(2)}) %collective-permute-start.24) | collective-permute-done | bytes 147488 | tf_op jit(solution)/shard_map/ppermute | solution.py:119
  130.6 2.2 %collective-permute-start.29 = (bf16[24,3072]{1,0:T(8,128)(2,1)S(1)}, bf16[24,3072]{1,0:T(8,128)(2,1)S(1)}, u32[]{:S(2)}, u32[]{:S(2)}) collective-permute-start(bf16[24,3072]{1,0:T(8,128)(2,1)S(1)} %get-tuple-element.106), channel_id=1, source_target_pairs={{0,6},{1,7},{2,4},{3,5},{4,2},{5,3},{6,0},{7,1},{8,14},{9,15},{10,... | collective-permute-start | bytes 442376 | tf_op jit(solution)/shard_map/ppermute | solution.py:34
  132.9 3.2 %collective-permute-done.27 = bf16[24,3072]{1,0:T(8,128)(2,1)S(1)} collective-permute-done((bf16[24,3072]{1,0:T(8,128)(2,1)S(1)}, bf16[24,3072]{1,0:T(8,128)(2,1)S(1)}, u32[]{:S(2)}, u32[]{:S(2)}) %collective-permute-start.27) | collective-permute-done | bytes 147488 | tf_op jit(solution)/shard_map/ppermute | solution.py:34
  136.1 2.2 %collective-permute-done.29 = bf16[24,3072]{1,0:T(8,128)(2,1)S(1)} collective-permute-done((bf16[24,3072]{1,0:T(8,128)(2,1)S(1)}, bf16[24,3072]{1,0:T(8,128)(2,1)S(1)}, u32[]{:S(2)}, u32[]{:S(2)}) %collective-permute-start.29) | collective-permute-done | bytes 147488 | tf_op jit(solution)/shard_map/ppermute | solution.py:34
  (112 shorter events, 21.6 us)
Async XLA Ops:
  1.1 4.7 %collective-permute-start = (f32[2,24]{1,0:T(2,128)S(1)}, f32[2,24]{1,0:T(2,128)S(1)}, u32[]{:S(2)}, u32[]{:S(2)}) collective-permute-start(f32[2,24]{1,0:T(2,128)S(1)} %pad_maximum_fusion.3), channel_id=1, source_target_pairs={{0,8},{8,0},{16,24},{24,16},{1,9},{9,1},{17,25},{25,17},{2,10},{10... | collective-permute-start | bytes 584 | tf_op jit(solution)/shard_map/ppermute | solution.py:40
  5.8 5.8 %copy-start = (bf16[24,3072]{1,0:T(8,128)(2,1)S(1)}, bf16[24,3072]{1,0:T(8,128)(2,1)}, u32[]{:S(2)}) copy-start(bf16[24,3072]{1,0:T(8,128)(2,1)} %param.7) | copy-start | bytes 442372
  5.8 5.8 %copy-start.3 = (f32[3072]{0:T(1024)S(1)}, f32[3072]{0:T(1024)}, u32[]{:S(2)}) copy-start(f32[3072]{0:T(1024)} %param.9) | copy-start | bytes 36868
  5.8 5.8 %copy-start.4 = (f32[3072]{0:T(1024)S(1)}, f32[3072]{0:T(1024)}, u32[]{:S(2)}) copy-start(f32[3072]{0:T(1024)} %param.8) | copy-start | bytes 36868
  5.8 9.5 %copy-start.1 = (f32[6144]{0:T(1024)S(1)}, f32[6144]{0:T(1024)}, u32[]{:S(2)}) copy-start(f32[6144]{0:T(1024)} %param.11) | copy-start | bytes 73732
  5.8 5.7 %collective-permute-start.1 = (f32[2,24]{1,0:T(2,128)S(1)}, f32[2,24]{1,0:T(2,128)S(1)}, u32[]{:S(2)}, u32[]{:S(2)}) collective-permute-start(f32[2,24]{1,0:T(2,128)S(1)} %fusion.108), channel_id=1, source_target_pairs={{0,16},{8,24},{16,0},{24,8},{1,17},{9,25},{17,1},{25,9},{2,18},{10... | collective-permute-start | bytes 584 | tf_op jit(solution)/shard_map/ppermute | solution.py:40
  11.8 6.6 %collective-permute-start.2 = (bf16[24,3072]{1,0:T(8,128)(2,1)S(1)}, bf16[24,3072]{1,0:T(8,128)(2,1)S(1)}, u32[]{:S(2)}, u32[]{:S(2)}) collective-permute-start(bf16[24,3072]{1,0:T(8,128)(2,1)S(1)} %get-tuple-element.104), channel_id=1, source_target_pairs={{2,0},{3,1},{0,2},{1,3},{6,4},{7,5},{4,6},{5,7},{10,8},{11,9},{8,1... | collective-permute-start | bytes 442376 | tf_op jit(solution)/shard_map/ppermute | solution.py:30
  13.3 7.9 %collective-permute-start.3 = (bf16[24,3072]{1,0:T(8,128)(2,1)S(1)}, bf16[24,3072]{1,0:T(8,128)(2,1)S(1)}, u32[]{:S(2)}, u32[]{:S(2)}) collective-permute-start(bf16[24,3072]{1,0:T(8,128)(2,1)S(1)} %get-tuple-element.104), channel_id=1, source_target_pairs={{4,0},{5,1},{6,2},{7,3},{0,4},{1,5},{2,6},{3,7},{12,8},{13,9},{14,... | collective-permute-start | bytes 442376 | tf_op jit(solution)/shard_map/ppermute | solution.py:30
  14.8 6.3 %collective-permute-start.4 = (bf16[24,3072]{1,0:T(8,128)(2,1)S(1)}, bf16[24,3072]{1,0:T(8,128)(2,1)S(1)}, u32[]{:S(2)}, u32[]{:S(2)}) collective-permute-start(bf16[24,3072]{1,0:T(8,128)(2,1)S(1)} %get-tuple-element.104), channel_id=1, source_target_pairs={{6,0},{7,1},{4,2},{5,3},{2,4},{3,5},{0,6},{1,7},{14,8},{15,9},{12,... | collective-permute-start | bytes 442376 | tf_op jit(solution)/shard_map/ppermute | solution.py:30
  21.2 2.7 %collective-permute-start.6 = (bf16[96,3072]{1,0:T(8,128)(2,1)S(1)}, bf16[96,3072]{1,0:T(8,128)(2,1)S(1)}, u32[]{:S(2)}, u32[]{:S(2)}) collective-permute-start(bf16[96,3072]{1,0:T(8,128)(2,1)S(1)} %pad_maximum_fusion), channel_id=1, source_target_pairs={{1,0},{0,1},{3,2},{2,3},{5,4},{4,5},{7,6},{6,7},{9,8},{8,9},{11,10... | collective-permute-start | bytes 1769480 | tf_op jit(solution)/shard_map/ppermute | solution.py:30
  22.2 11.8 %collective-permute-start.5 = (bf16[96,768]{1,0:T(8,128)(2,1)S(1)}, bf16[96,768]{1,0:T(8,128)(2,1)S(1)}, u32[]{:S(2)}, u32[]{:S(2)}) collective-permute-start(bf16[96,768]{1,0:T(8,128)(2,1)S(1)} %convolution_convert_fusion.8), channel_id=1, source_target_pairs={{0,8},{8,0},{16,24},{24,16},{1,9},{9,1},{17,25},{25,17},{2,10},{10... | collective-permute-start | bytes 442376 | tf_op jit(solution)/shard_map/ppermute | solution.py:119
  24.8 2.3 %slice-start.10 = ((bf16[3072,6144]{1,0:T(8,128)(2,1)}), bf16[3072,768]{1,0:T(8,128)(2,1)S(1)}, s32[]{:S(2)}) async-start(bf16[3072,6144]{1,0:T(8,128)(2,1)} %param.10), calls=%async_computation.10 | async-start | bytes 9437184 | tf_op jit(solution)/shard_map/slice | solution.py:102
  24.8 9.2 %collective-permute-start.7 = (bf16[96,768]{1,0:T(8,128)(2,1)S(1)}, bf16[96,768]{1,0:T(8,128)(2,1)S(1)}, u32[]{:S(2)}, u32[]{:S(2)}) collective-permute-start(bf16[96,768]{1,0:T(8,128)(2,1)S(1)} %convolution_convert_fusion.7), channel_id=1, source_target_pairs={{0,8},{8,0},{16,24},{24,16},{1,9},{9,1},{17,25},{25,17},{2,10},{10... | collective-permute-start | bytes 442376 | tf_op jit(solution)/shard_map/ppermute | solution.py:119
  28.2 2.3 %slice-start.11 = ((bf16[3072,6144]{1,0:T(8,128)(2,1)}), bf16[3072,768]{1,0:T(8,128)(2,1)S(1)}, s32[]{:S(2)}) async-start(bf16[3072,6144]{1,0:T(8,128)(2,1)} %param.10), calls=%async_computation.11 | async-start | bytes 9437184 | tf_op jit(solution)/shard_map/slice | solution.py:102
  30.6 2.3 %slice-start.9 = ((bf16[3072,6144]{1,0:T(8,128)(2,1)}), bf16[3072,768]{1,0:T(8,128)(2,1)S(1)}, s32[]{:S(2)}) async-start(bf16[3072,6144]{1,0:T(8,128)(2,1)} %param.10), calls=%async_computation.9 | async-start | bytes 9437184 | tf_op jit(solution)/shard_map/slice | solution.py:102
  34.1 9.2 %collective-permute-start.8 = (bf16[192,768]{1,0:T(8,128)(2,1)S(1)}, bf16[192,768]{1,0:T(8,128)(2,1)S(1)}, u32[]{:S(2)}, u32[]{:S(2)}) collective-permute-start(bf16[192,768]{1,0:T(8,128)(2,1)S(1)} %convolution_convert_fusion.6), channel_id=1, source_target_pairs={{0,8},{8,0},{16,24},{24,16},{1,9},{9,1},{17,25},{25,17},{2,10},{10... | collective-permute-start | bytes 884744 | tf_op jit(solution)/shard_map/ppermute | solution.py:119
  35.2 3.5 %collective-permute-start.9 = (bf16[192,768]{1,0:T(8,128)(2,1)S(1)}, bf16[192,768]{1,0:T(8,128)(2,1)S(1)}, u32[]{:S(2)}, u32[]{:S(2)}) collective-permute-start(bf16[192,768]{1,0:T(8,128)(2,1)S(1)} %add_convert_fusion.7), channel_id=1, source_target_pairs={{0,1},{1,0},{2,3},{3,2},{4,5},{5,4},{6,7},{7,6},{8,16},{9,17},{10,... | collective-permute-start | bytes 884744 | tf_op jit(solution)/shard_map/ppermute | solution.py:122
  35.3 2.3 %slice-start.12 = ((bf16[3072,6144]{1,0:T(8,128)(2,1)}), bf16[3072,768]{1,0:T(8,128)(2,1)S(1)}, s32[]{:S(2)}) async-start(bf16[3072,6144]{1,0:T(8,128)(2,1)} %param.10), calls=%async_computation.12 | async-start | bytes 9437184 | tf_op jit(solution)/shard_map/slice | solution.py:102
  43.3 6.7 %collective-permute-start.11 = (bf16[192,768]{1,0:T(8,128)(2,1)S(1)}, bf16[192,768]{1,0:T(8,128)(2,1)S(1)}, u32[]{:S(2)}, u32[]{:S(2)}) collective-permute-start(bf16[192,768]{1,0:T(8,128)(2,1)S(1)} %add_convert_fusion.6), channel_id=1, source_target_pairs={{0,1},{1,0},{2,3},{3,2},{4,5},{5,4},{6,7},{7,6},{8,16},{9,17},{10,... | collective-permute-start | bytes 884744 | tf_op jit(solution)/shard_map/ppermute | solution.py:122
  43.7 9.5 %collective-permute-start.10 = (bf16[192,768]{1,0:T(8,128)(2,1)S(1)}, bf16[192,768]{1,0:T(8,128)(2,1)S(1)}, u32[]{:S(2)}, u32[]{:S(2)}) collective-permute-start(bf16[192,768]{1,0:T(8,128)(2,1)S(1)} %broadcast_select_fusion.5), channel_id=1, source_target_pairs={{0,8},{8,0},{16,24},{24,16},{1,9},{9,1},{17,25},{25,17},{2,10},{10... | collective-permute-start | bytes 884744 | tf_op jit(solution)/shard_map/ppermute | solution.py:119
  48.9 4.3 %slice-start = ((bf16[6144,3072]{1,0:T(8,128)(2,1)}), bf16[768,3072]{1,0:T(8,128)(2,1)S(1)}, s32[]{:S(2)}) async-start(bf16[6144,3072]{1,0:T(8,128)(2,1)} %param.12), calls=%async_computation | async-start | bytes 9437184 | tf_op jit(solution)/shard_map/slice | solution.py:102
  54.5 6.1 %collective-permute-start.13 = (bf16[192,768]{1,0:T(8,128)(2,1)S(1)}, bf16[192,768]{1,0:T(8,128)(2,1)S(1)}, u32[]{:S(2)}, u32[]{:S(2)}) collective-permute-start(bf16[192,768]{1,0:T(8,128)(2,1)S(1)} %add_convert_fusion.5), channel_id=1, source_target_pairs={{0,1},{1,0},{2,3},{3,2},{4,5},{5,4},{6,7},{7,6},{8,16},{9,17},{10,... | collective-permute-start | bytes 884744 | tf_op jit(solution)/shard_map/ppermute | solution.py:122
  54.9 9.5 %collective-permute-start.12 = (bf16[192,768]{1,0:T(8,128)(2,1)S(1)}, bf16[192,768]{1,0:T(8,128)(2,1)S(1)}, u32[]{:S(2)}, u32[]{:S(2)}) collective-permute-start(bf16[192,768]{1,0:T(8,128)(2,1)S(1)} %broadcast_select_fusion.4), channel_id=1, source_target_pairs={{0,8},{8,0},{16,24},{24,16},{1,9},{9,1},{17,25},{25,17},{2,10},{10... | collective-permute-start | bytes 884744 | tf_op jit(solution)/shard_map/ppermute | solution.py:119
  59.5 5.0 %slice-start.1 = ((bf16[6144,3072]{1,0:T(8,128)(2,1)}), bf16[768,3072]{1,0:T(8,128)(2,1)S(1)}, s32[]{:S(2)}) async-start(bf16[6144,3072]{1,0:T(8,128)(2,1)} %param.12), calls=%async_computation.1 | async-start | bytes 9437184 | tf_op jit(solution)/shard_map/slice | solution.py:102
  65.8 5.1 %collective-permute-start.15 = (bf16[192,768]{1,0:T(8,128)(2,1)S(1)}, bf16[192,768]{1,0:T(8,128)(2,1)S(1)}, u32[]{:S(2)}, u32[]{:S(2)}) collective-permute-start(bf16[192,768]{1,0:T(8,128)(2,1)S(1)} %add_convert_fusion.4), channel_id=1, source_target_pairs={{0,1},{1,0},{2,3},{3,2},{4,5},{5,4},{6,7},{7,6},{8,16},{9,17},{10,... | collective-permute-start | bytes 884744 | tf_op jit(solution)/shard_map/ppermute | solution.py:122
  66.1 9.5 %collective-permute-start.14 = (bf16[192,768]{1,0:T(8,128)(2,1)S(1)}, bf16[192,768]{1,0:T(8,128)(2,1)S(1)}, u32[]{:S(2)}, u32[]{:S(2)}) collective-permute-start(bf16[192,768]{1,0:T(8,128)(2,1)S(1)} %broadcast_select_fusion.3), channel_id=1, source_target_pairs={{0,8},{8,0},{16,24},{24,16},{1,9},{9,1},{17,25},{25,17},{2,10},{10... | collective-permute-start | bytes 884744 | tf_op jit(solution)/shard_map/ppermute | solution.py:119
  75.7 4.3 %collective-permute-start.17 = (bf16[192,768]{1,0:T(8,128)(2,1)S(1)}, bf16[192,768]{1,0:T(8,128)(2,1)S(1)}, u32[]{:S(2)}, u32[]{:S(2)}) collective-permute-start(bf16[192,768]{1,0:T(8,128)(2,1)S(1)} %add_convert_fusion.3), channel_id=1, source_target_pairs={{0,1},{1,0},{2,3},{3,2},{4,5},{5,4},{6,7},{7,6},{8,16},{9,17},{10,... | collective-permute-start | bytes 884744 | tf_op jit(solution)/shard_map/ppermute | solution.py:122
  76.1 2.3 %slice-start.2 = ((bf16[6144,3072]{1,0:T(8,128)(2,1)}), bf16[768,3072]{1,0:T(8,128)(2,1)S(1)}, s32[]{:S(2)}) async-start(bf16[6144,3072]{1,0:T(8,128)(2,1)} %param.12), calls=%async_computation.2 | async-start | bytes 9437184 | tf_op jit(solution)/shard_map/slice | solution.py:102
  76.1 9.5 %collective-permute-start.16 = (bf16[192,768]{1,0:T(8,128)(2,1)S(1)}, bf16[192,768]{1,0:T(8,128)(2,1)S(1)}, u32[]{:S(2)}, u32[]{:S(2)}) collective-permute-start(bf16[192,768]{1,0:T(8,128)(2,1)S(1)} %broadcast_select_fusion.2), channel_id=1, source_target_pairs={{0,8},{8,0},{16,24},{24,16},{1,9},{9,1},{17,25},{25,17},{2,10},{10... | collective-permute-start | bytes 884744 | tf_op jit(solution)/shard_map/ppermute | solution.py:119
  85.6 4.3 %collective-permute-start.19 = (bf16[192,768]{1,0:T(8,128)(2,1)S(1)}, bf16[192,768]{1,0:T(8,128)(2,1)S(1)}, u32[]{:S(2)}, u32[]{:S(2)}) collective-permute-start(bf16[192,768]{1,0:T(8,128)(2,1)S(1)} %add_convert_fusion.2), channel_id=1, source_target_pairs={{0,1},{1,0},{2,3},{3,2},{4,5},{5,4},{6,7},{7,6},{8,16},{9,17},{10,... | collective-permute-start | bytes 884744 | tf_op jit(solution)/shard_map/ppermute | solution.py:122
  86.0 2.3 %slice-start.3 = ((bf16[6144,3072]{1,0:T(8,128)(2,1)}), bf16[768,3072]{1,0:T(8,128)(2,1)S(1)}, s32[]{:S(2)}) async-start(bf16[6144,3072]{1,0:T(8,128)(2,1)} %param.12), calls=%async_computation.3 | async-start | bytes 9437184 | tf_op jit(solution)/shard_map/slice | solution.py:102
  86.0 9.5 %collective-permute-start.18 = (bf16[192,768]{1,0:T(8,128)(2,1)S(1)}, bf16[192,768]{1,0:T(8,128)(2,1)S(1)}, u32[]{:S(2)}, u32[]{:S(2)}) collective-permute-start(bf16[192,768]{1,0:T(8,128)(2,1)S(1)} %broadcast_select_fusion.1), channel_id=1, source_target_pairs={{0,8},{8,0},{16,24},{24,16},{1,9},{9,1},{17,25},{25,17},{2,10},{10... | collective-permute-start | bytes 884744 | tf_op jit(solution)/shard_map/ppermute | solution.py:119
  95.6 4.3 %collective-permute-start.21 = (bf16[192,768]{1,0:T(8,128)(2,1)S(1)}, bf16[192,768]{1,0:T(8,128)(2,1)S(1)}, u32[]{:S(2)}, u32[]{:S(2)}) collective-permute-start(bf16[192,768]{1,0:T(8,128)(2,1)S(1)} %add_convert_fusion.1), channel_id=1, source_target_pairs={{0,1},{1,0},{2,3},{3,2},{4,5},{5,4},{6,7},{7,6},{8,16},{9,17},{10,... | collective-permute-start | bytes 884744 | tf_op jit(solution)/shard_map/ppermute | solution.py:122
  96.0 2.3 %slice-start.4 = ((bf16[6144,3072]{1,0:T(8,128)(2,1)}), bf16[768,3072]{1,0:T(8,128)(2,1)S(1)}, s32[]{:S(2)}) async-start(bf16[6144,3072]{1,0:T(8,128)(2,1)} %param.12), calls=%async_computation.4 | async-start | bytes 9437184 | tf_op jit(solution)/shard_map/slice | solution.py:102
  96.0 9.5 %collective-permute-start.20 = (bf16[192,768]{1,0:T(8,128)(2,1)S(1)}, bf16[192,768]{1,0:T(8,128)(2,1)S(1)}, u32[]{:S(2)}, u32[]{:S(2)}) collective-permute-start(bf16[192,768]{1,0:T(8,128)(2,1)S(1)} %broadcast_select_fusion), channel_id=1, source_target_pairs={{0,8},{8,0},{16,24},{24,16},{1,9},{9,1},{17,25},{25,17},{2,10},{10... | collective-permute-start | bytes 884744 | tf_op jit(solution)/shard_map/ppermute | solution.py:119
  99.6 7.6 %slice-start.5 = ((bf16[6144,3072]{1,0:T(8,128)(2,1)}), bf16[768,3072]{1,0:T(8,128)(2,1)S(1)}, s32[]{:S(2)}) async-start(bf16[6144,3072]{1,0:T(8,128)(2,1)} %param.12), calls=%async_computation.5 | async-start | bytes 9437184 | tf_op jit(solution)/shard_map/slice | solution.py:102
  105.5 3.3 %collective-permute-start.23 = (bf16[192,768]{1,0:T(8,128)(2,1)S(1)}, bf16[192,768]{1,0:T(8,128)(2,1)S(1)}, u32[]{:S(2)}, u32[]{:S(2)}) collective-permute-start(bf16[192,768]{1,0:T(8,128)(2,1)S(1)} %add_convert_fusion), channel_id=1, source_target_pairs={{0,1},{1,0},{2,3},{3,2},{4,5},{5,4},{6,7},{7,6},{8,16},{9,17},{10,... | collective-permute-start | bytes 884744 | tf_op jit(solution)/shard_map/ppermute | solution.py:122
  105.9 9.5 %collective-permute-start.22 = (bf16[192,768]{1,0:T(8,128)(2,1)S(1)}, bf16[192,768]{1,0:T(8,128)(2,1)S(1)}, u32[]{:S(2)}, u32[]{:S(2)}) collective-permute-start(bf16[192,768]{1,0:T(8,128)(2,1)S(1)} %fusion.57), channel_id=1, source_target_pairs={{0,8},{8,0},{16,24},{24,16},{1,9},{9,1},{17,25},{25,17},{2,10},{10... | collective-permute-start | bytes 884744 | tf_op jit(solution)/shard_map/ppermute | solution.py:119
  108.5 7.6 %slice-start.6 = ((bf16[6144,3072]{1,0:T(8,128)(2,1)}), bf16[768,3072]{1,0:T(8,128)(2,1)S(1)}, s32[]{:S(2)}) async-start(bf16[6144,3072]{1,0:T(8,128)(2,1)} %param.12), calls=%async_computation.6 | async-start | bytes 9437184 | tf_op jit(solution)/shard_map/slice | solution.py:102
  115.7 5.5 %collective-permute-start.25 = (bf16[96,768]{1,0:T(8,128)(2,1)S(1)}, bf16[96,768]{1,0:T(8,128)(2,1)S(1)}, u32[]{:S(2)}, u32[]{:S(2)}) collective-permute-start(bf16[96,768]{1,0:T(8,128)(2,1)S(1)} %get-tuple-element.109), channel_id=1, source_target_pairs={{0,8},{8,0},{16,24},{24,16},{1,9},{9,1},{17,25},{25,17},{2,10},{10... | collective-permute-start | bytes 442376 | tf_op jit(solution)/shard_map/ppermute | solution.py:119
  117.1 4.0 %slice-start.7 = ((bf16[6144,3072]{1,0:T(8,128)(2,1)}), bf16[768,3072]{1,0:T(8,128)(2,1)S(1)}, s32[]{:S(2)}) async-start(bf16[6144,3072]{1,0:T(8,128)(2,1)} %param.12), calls=%async_computation.7 | async-start | bytes 9437184 | tf_op jit(solution)/shard_map/slice | solution.py:102
  122.0 6.3 %collective-permute-start.26 = (bf16[96,3072]{1,0:T(8,128)(2,1)S(1)}, bf16[96,3072]{1,0:T(8,128)(2,1)S(1)}, u32[]{:S(2)}, u32[]{:S(2)}) collective-permute-start(bf16[96,3072]{1,0:T(8,128)(2,1)S(1)} %fusion), channel_id=1, source_target_pairs={{0,1},{1,0},{2,3},{3,2},{4,5},{5,4},{6,7},{7,6},{8,9},{9,8},{10,11... | collective-permute-start | bytes 1769480 | tf_op jit(solution)/shard_map/ppermute | solution.py:34
  122.1 6.2 %collective-permute-start.24 = (bf16[96,768]{1,0:T(8,128)(2,1)S(1)}, bf16[96,768]{1,0:T(8,128)(2,1)S(1)}, u32[]{:S(2)}, u32[]{:S(2)}) collective-permute-start(bf16[96,768]{1,0:T(8,128)(2,1)S(1)} %get-tuple-element.108), channel_id=1, source_target_pairs={{0,8},{8,0},{16,24},{24,16},{1,9},{9,1},{17,25},{25,17},{2,10},{10... | collective-permute-start | bytes 442376 | tf_op jit(solution)/shard_map/ppermute | solution.py:119
  122.4 5.9 %slice-start.8 = ((bf16[6144,3072]{1,0:T(8,128)(2,1)}), bf16[768,3072]{1,0:T(8,128)(2,1)S(1)}, s32[]{:S(2)}) async-start(bf16[6144,3072]{1,0:T(8,128)(2,1)} %param.12), calls=%async_computation.8 | async-start | bytes 9437184 | tf_op jit(solution)/shard_map/slice | solution.py:102
  122.4 15.9 %copy-start.2 = (f32[3072]{0:T(1024)S(1)}, f32[3072]{0:T(1024)}, u32[]{:S(2)}) copy-start(f32[3072]{0:T(1024)} %param.13) | copy-start | bytes 36868
  129.3 6.8 %collective-permute-start.27 = (bf16[24,3072]{1,0:T(8,128)(2,1)S(1)}, bf16[24,3072]{1,0:T(8,128)(2,1)S(1)}, u32[]{:S(2)}, u32[]{:S(2)}) collective-permute-start(bf16[24,3072]{1,0:T(8,128)(2,1)S(1)} %get-tuple-element.105), channel_id=1, source_target_pairs={{0,2},{1,3},{2,0},{3,1},{4,6},{5,7},{6,4},{7,5},{8,10},{9,11},{10,... | collective-permute-start | bytes 442376 | tf_op jit(solution)/shard_map/ppermute | solution.py:34
  129.8 6.3 %collective-permute-start.28 = (bf16[24,3072]{1,0:T(8,128)(2,1)S(1)}, bf16[24,3072]{1,0:T(8,128)(2,1)S(1)}, u32[]{:S(2)}, u32[]{:S(2)}) collective-permute-start(bf16[24,3072]{1,0:T(8,128)(2,1)S(1)} %get-tuple-element.107), channel_id=1, source_target_pairs={{0,4},{1,5},{2,6},{3,7},{4,0},{5,1},{6,2},{7,3},{8,12},{9,13},{10,... | collective-permute-start | bytes 442376 | tf_op jit(solution)/shard_map/ppermute | solution.py:34
  130.6 7.7 %collective-permute-start.29 = (bf16[24,3072]{1,0:T(8,128)(2,1)S(1)}, bf16[24,3072]{1,0:T(8,128)(2,1)S(1)}, u32[]{:S(2)}, u32[]{:S(2)}) collective-permute-start(bf16[24,3072]{1,0:T(8,128)(2,1)S(1)} %get-tuple-element.106), channel_id=1, source_target_pairs={{0,6},{1,7},{2,4},{3,5},{4,2},{5,3},{6,0},{7,1},{8,14},{9,15},{10,... | collective-permute-start | bytes 442376 | tf_op jit(solution)/shard_map/ppermute | solution.py:34
  (3 other events, 7.0 us)

commit v3 on v2

--- a/solution.py
+++ b/solution.py
@@ -46,8 +46,7 @@
     held = [own]
     for k in range(1, grid.side * grid.side):
         held.append(grid.take(own, k // grid.side, k % grid.side, 0))
-    held = jnp.concatenate(held)
-    return held, grid.take(held, 0, 0, 1)
+    return jnp.concatenate(held[:-1]), held[-1]
 
 
 def scatter_sum(grid, kept, given):
@@ -63,9 +62,10 @@
     return total
 
 
-def chained_middle(grid, held, swapped, w_up, up_bias, w_down):
+def chained_middle(grid, sooner, farthest, w_up, up_bias, w_down):
     n_row = grid.n_row
-    gathered = jnp.concatenate([held, swapped])
+    held = jnp.concatenate([sooner, farthest])
+    gathered = jnp.concatenate([held, grid.take(held, 0, 0, 1)])
     half = held.shape[0]
     row = lax.axis_index("row")
     middle = n_row // 2
@@ -102,7 +102,7 @@
     return lax.optimization_barrier(lax.slice_in_dim(weights, low, high, axis=axis))
 
 
-def four_rows(grid, is_end, early, held, swapped, w_up, up_bias, w_down):
+def four_rows(grid, is_end, early, sooner, farthest, w_up, up_bias, w_down):
     facing = [(0, 1), (1, 0), (2, 3), (3, 2)]
     across = []
     for i in range(grid.n_row * grid.n_col):
@@ -139,16 +139,28 @@
     def down(k):
         return jnp.dot(hidden[k], down_part[k], preferred_element_type=jnp.float32)
 
+    def activated(k, mine, came):
+        summed = mine.astype(jnp.float32) + came.astype(jnp.float32) + up_bias[edges[k] : edges[k + 1]]
+        return jax.nn.gelu(summed, approximate=True).astype(jnp.bfloat16)
+
     def widened(v, width):
         return v if v.shape[1] == width else jnp.pad(v, ((0, 0), (0, width - v.shape[1])))
 
-    gathered, half = jnp.concatenate([held, swapped]), held.shape[0]
+    def up_first(v):
+        return jnp.dot(v, up_part[0], preferred_element_type=jnp.float32).astype(jnp.bfloat16)
+
+    first = [up_first(sooner)]
+    farthest, first[0] = lax.optimization_barrier((farthest, first[0]))
+    held = jnp.concatenate([sooner, farthest])
+    half = held.shape[0]
+    later = jnp.concatenate([farthest, grid.take(held, 0, 0, 1)])
+    gathered = jnp.concatenate([sooner, later])
+    first.append(up_first(later))
     for k in range(len(early), UP_AHEAD):
         up_part[k] = cut(w_up, 1, edges[k], edges[k + 1], gathered)
-    first = [jnp.dot(v, up_part[0], preferred_element_type=jnp.float32).astype(jnp.bfloat16) for v in (held, swapped)]
     partial, sums, own, hidden = {0: jnp.concatenate(first)}, {}, {}, {}
     terms = None
-    for t in range(count + 1):
+    for t in range(count):
         crossed = None
         if t == 0:
             faced = jnp.concatenate([face(v, facing) for v in first])
@@ -157,11 +169,9 @@
         elif t < count:
             width = max(size[t], size[t - 2])
             faced = face(jnp.where(is_end, widened(partial[t], width), widened(own[t - 2], width)), facing)
-        else:
-            faced = face(own[t - 2], facing)
-        if 0 <= t - 1 < count:
+        if t > 0:
             crossed = cross(sums[t - 1])
-        stage(t, partial[t] if t < count else terms)
+        stage(t, partial[t])
         computed = []
         if t + 1 < count:
             partial[t + 1] = up(t + 1)
@@ -179,25 +189,29 @@
         if joined:
             terms = joined.pop(0)
         if crossed is not None:
-            k = t - 1
-            summed = sums[k].astype(jnp.float32) + crossed.astype(jnp.float32)
-            summed = summed + up_bias[edges[k] : edges[k + 1]]
-            own[k] = jax.nn.gelu(summed, approximate=True).astype(jnp.bfloat16)
-        if t < count:
-            sums[t] = (partial[t].astype(jnp.float32) + faced[:, : size[t]].astype(jnp.float32)).astype(jnp.bfloat16)
+            own[t - 1] = activated(t - 1, sums[t - 1], crossed)
+        sums[t] = (partial[t].astype(jnp.float32) + faced[:, : size[t]].astype(jnp.float32)).astype(jnp.bfloat16)
         if t >= 2:
             hidden[t - 2] = jnp.where(is_end, faced[:, : size[t - 2]], own[t - 2])
-    last = own[count - 1]
-    given = face(last[half:], facing)
-    kept = face(last[:half], facing)
+    faced = face(own[count - 2], facing)
+    spans = (slice(half, None), slice(0, half))
+    crossed = [cross(sums[count - 1][span]) for span in spans]
+    stage(count, terms)
+    terms = terms + down(count - 3)
+    last = [activated(count - 1, sums[count - 1][spans[0]], crossed[0])]
+    given = face(last[0], facing)
+    crossed[1], _ = lax.optimization_barrier((crossed[1], last[0]))
+    last.append(activated(count - 1, sums[count - 1][spans[1]], crossed[1]))
+    kept = face(last[1], facing)
+    hidden[count - 2] = jnp.where(is_end, faced, own[count - 2])
     terms = terms + down(count - 2)
 
     def finish(came, mine, before, weights):
         rows = jnp.where(is_end, came, mine)
         return before + jnp.dot(rows, weights, preferred_element_type=jnp.float32)
 
-    given = finish(given, last[half:], terms[half:], down_part[count - 1])
-    return finish(kept, last[:half], terms[:half], down_part[count]), given
+    given = finish(given, last[0], terms[half:], down_part[count - 1])
+    return finish(kept, last[1], terms[:half], down_part[count]), given
 
 
 def local(grid, inputs, ln_gain, ln_bias, w_up, up_bias, w_down, down_bias):
@@ -217,11 +231,11 @@
     normed = (normed * ln_gain + ln_bias).astype(jnp.bfloat16)
     if grid.n_row == 4:
         early.append(cut(w_up, 1, edges[1], edges[2], normed))
-    held, swapped = gather(grid, normed)
+    sooner, farthest = gather(grid, normed)
     if grid.n_row == 4:
-        terms = four_rows(grid, is_end, early, held, swapped, w_up, up_bias, w_down)
+        terms = four_rows(grid, is_end, early, sooner, farthest, w_up, up_bias, w_down)
     else:
-        terms = chained_middle(grid, held, swapped, w_up, up_bias, w_down)
+        terms = chained_middle(grid, sooner, farthest, w_up, up_bias, w_down)
     down_sum = scatter_sum(grid, *terms)
     return (in_float + down_sum + down_bias).astype(jnp.bfloat16)
 

time: 140 us -> 141 us (level)
  starting transfers between devices: 30 us -> 36.7 us
  waiting for transfers between devices: 61.8 us -> 56.7 us
    ppermute x12, waiting for transfers between devices: 48.9 us -> 42.3 us  [face(): return lax.ppermute(sent, 'row', pairs)]
    ppermute x12, starting transfers between devices: 16 us -> 22.1 us  [face(): return lax.ppermute(sent, 'row', pairs)]
    ppermute x8 -> x9, waiting for transfers between devices: 0.02 us -> 1.73 us  [cross(): return lax.ppermute(sent, ('row', 'col'), across)]
  transfers between devices with their start and end apart: 30 -> 31, of which waited for: 15 -> 18; matrix products, arithmetic and copies ran while one was open for 16% -> 16% of each run, Pallas kernels for 0% -> 0%
where the time goes in v3:
time: 141 us; the launch traced here: 140 us
  waiting for transfers between devices  56.7 us (40%)
  starting transfers between devices  36.7 us (26%)
  matrix products  20 us (14%)
  local copies, waits for them, and re-layouts  19.8 us (14%)
  other arithmetic  6.47 us (5%)
    ppermute x12, waiting for transfers between devices, face(): return lax.ppermute(sent, 'row', pairs)  42.3 us
    ppermute x12, starting transfers between devices, face(): return lax.ppermute(sent, 'row', pairs)  22.1 us
    slice x32, local copies, waits for them, and re-layouts, cut(): lax.slice_in_dim(weights, low, high, axis=axis)  17 us
    dot_general x7, matrix products, down(): return jnp.dot(hidden[k], down_part[k], preferred_element_type=jnp.float32)  8.74 us
    dot_general x7, matrix products, up(): jnp.dot(gathered, up_part[k], preferred_element_type=jnp.float32)  7.66 us
    ppermute x2, starting transfers between devices, row_sum(): lax.ppermute(value, 'row', [(i, i ^ step) for i in range(grid.n_row)])  6.21 us
    ppermute x4, waiting for transfers between devices, take(): return lax.ppermute(value, 'col', pairs)  6.17 us
    ppermute x4, waiting for transfers between devices, give(): return lax.ppermute(value, 'col', pairs)  4.87 us
  transfers between devices with their start and end apart: 31, of which 18 were waited for; matrix products, arithmetic and copies ran while one was open for 16% of the time, Pallas kernels for 0%

profile of v3, /device:TPU:0, one launch (start us, length us, event | category | flops | bytes accessed | tf_op | source)
XLA Modules:
  0.0 140.3 jit_solution(11021104317073674793)
XLA Ops:
  1.1 3.1 %collective-permute-start = (f32[2,24]{1,0:T(2,128)S(1)}, f32[2,24]{1,0:T(2,128)S(1)}, u32[]{:S(2)}, u32[]{:S(2)}) collective-permute-start(f32[2,24]{1,0:T(2,128)S(1)} %pad_maximum_fusion.3), channel_id=1, source_target_pairs={{0,8},{8,0},{16,24},{24,16},{1,9},{9,1},{17,25},{25,17},{2,10},{10... | collective-permute-start | bytes 584 | tf_op jit(solution)/shard_map/ppermute | solution.py:40
  4.2 1.6 %collective-permute-done = f32[2,24]{1,0:T(2,128)S(1)} collective-permute-done((f32[2,24]{1,0:T(2,128)S(1)}, f32[2,24]{1,0:T(2,128)S(1)}, u32[]{:S(2)}, u32[]{:S(2)}) %collective-permute-start) | collective-permute-done | bytes 224 | tf_op jit(solution)/shard_map/ppermute | solution.py:40
  5.8 3.1 %collective-permute-start.1 = (f32[2,24]{1,0:T(2,128)S(1)}, f32[2,24]{1,0:T(2,128)S(1)}, u32[]{:S(2)}, u32[]{:S(2)}) collective-permute-start(f32[2,24]{1,0:T(2,128)S(1)} %fusion.128), channel_id=1, source_target_pairs={{0,16},{8,24},{16,0},{24,8},{1,17},{9,25},{17,1},{25,9},{2,18},{10... | collective-permute-start | bytes 584 | tf_op jit(solution)/shard_map/ppermute | solution.py:40
  8.9 2.6 %slice.110 = bf16[3072,768]{1,0:T(8,128)(2,1)S(1)} slice(bf16[3072,6144]{1,0:T(8,128)(2,1)} %param.10), slice={[0:3072], [0:768]} | slice | bytes 9437184 | tf_op jit(solution)/shard_map/slice | solution.py:224
  11.8 1.6 %collective-permute-start.3 = (bf16[24,3072]{1,0:T(8,128)(2,1)S(1)}, bf16[24,3072]{1,0:T(8,128)(2,1)S(1)}, u32[]{:S(2)}, u32[]{:S(2)}) collective-permute-start(bf16[24,3072]{1,0:T(8,128)(2,1)S(1)} %get-tuple-element.104), channel_id=1, source_target_pairs={{2,0},{3,1},{0,2},{1,3},{6,4},{7,5},{4,6},{5,7},{10,8},{11,9},{8,1... | collective-permute-start | bytes 442376 | tf_op jit(solution)/shard_map/ppermute | solution.py:30
  13.3 1.5 %collective-permute-start.4 = (bf16[24,3072]{1,0:T(8,128)(2,1)S(1)}, bf16[24,3072]{1,0:T(8,128)(2,1)S(1)}, u32[]{:S(2)}, u32[]{:S(2)}) collective-permute-start(bf16[24,3072]{1,0:T(8,128)(2,1)S(1)} %get-tuple-element.104), channel_id=1, source_target_pairs={{4,0},{5,1},{6,2},{7,3},{0,4},{1,5},{2,6},{3,7},{12,8},{13,9},{14,... | collective-permute-start | bytes 442376 | tf_op jit(solution)/shard_map/ppermute | solution.py:30
  15.4 3.1 %collective-permute-done.3 = bf16[24,3072]{1,0:T(8,128)(2,1)S(1)} collective-permute-done((bf16[24,3072]{1,0:T(8,128)(2,1)S(1)}, bf16[24,3072]{1,0:T(8,128)(2,1)S(1)}, u32[]{:S(2)}, u32[]{:S(2)}) %collective-permute-start.3) | collective-permute-done | bytes 147488 | tf_op jit(solution)/shard_map/ppermute | solution.py:30
  18.4 2.8 %collective-permute-done.4 = bf16[24,3072]{1,0:T(8,128)(2,1)S(1)} collective-permute-done((bf16[24,3072]{1,0:T(8,128)(2,1)S(1)}, bf16[24,3072]{1,0:T(8,128)(2,1)S(1)}, u32[]{:S(2)}, u32[]{:S(2)}) %collective-permute-start.4) | collective-permute-done | bytes 147488 | tf_op jit(solution)/shard_map/ppermute | solution.py:30
  22.3 1.6 %collective-permute-start.5 = (bf16[72,768]{1,0:T(8,128)(2,1)S(1)}, bf16[72,768]{1,0:T(8,128)(2,1)S(1)}, u32[]{:S(2)}, u32[]{:S(2)}) collective-permute-start(bf16[72,768]{1,0:T(8,128)(2,1)S(1)} %convolution_convert_fusion.8), channel_id=1, source_target_pairs={{0,8},{8,0},{16,24},{24,16},{1,9},{9,1},{17,25},{25,17},{2,10},{10... | collective-permute-start | bytes 331784 | tf_op jit(solution)/shard_map/ppermute | solution.py:119
  25.1 1.6 %collective-permute-start.7 = (bf16[120,768]{1,0:T(8,128)(2,1)S(1)}, bf16[120,768]{1,0:T(8,128)(2,1)S(1)}, u32[]{:S(2)}, u32[]{:S(2)}) collective-permute-start(bf16[120,768]{1,0:T(8,128)(2,1)S(1)} %convolution_convert_fusion.7), channel_id=1, source_target_pairs={{0,8},{8,0},{16,24},{24,16},{1,9},{9,1},{17,25},{25,17},{2,10},{10... | collective-permute-start | bytes 552968 | tf_op jit(solution)/shard_map/ppermute | solution.py:119
  28.6 2.3 %slice-done.11 = bf16[3072,768]{1,0:T(8,128)(2,1)S(1)} async-done(((bf16[3072,6144]{1,0:T(8,128)(2,1)}), bf16[3072,768]{1,0:T(8,128)(2,1)S(1)}, s32[]{:S(2)}) %slice-start.11) | async-done | bytes 4718616 | tf_op jit(solution)/shard_map/slice | solution.py:102
  30.9 1.1 convolution_convert_fusion.5
  32.0 1.2 slice-done.9
  34.4 1.6 %collective-permute-start.8 = (bf16[192,768]{1,0:T(8,128)(2,1)S(1)}, bf16[192,768]{1,0:T(8,128)(2,1)S(1)}, u32[]{:S(2)}, u32[]{:S(2)}) collective-permute-start(bf16[192,768]{1,0:T(8,128)(2,1)S(1)} %convolution_convert_fusion.6), channel_id=1, source_target_pairs={{0,8},{8,0},{16,24},{24,16},{1,9},{9,1},{17,25},{25,17},{2,10},{10... | collective-permute-start | bytes 884744 | tf_op jit(solution)/shard_map/ppermute | solution.py:119
  36.2 2.3 %slice-done.12 = bf16[3072,768]{1,0:T(8,128)(2,1)S(1)} async-done(((bf16[3072,6144]{1,0:T(8,128)(2,1)}), bf16[3072,768]{1,0:T(8,128)(2,1)S(1)}, s32[]{:S(2)}) %slice-start.12) | async-done | bytes 4718616 | tf_op jit(solution)/shard_map/slice | solution.py:102
  39.6 3.9 %collective-permute-done.8 = bf16[192,768]{1,0:T(8,128)(2,1)S(1)} collective-permute-done((bf16[192,768]{1,0:T(8,128)(2,1)S(1)}, bf16[192,768]{1,0:T(8,128)(2,1)S(1)}, u32[]{:S(2)}, u32[]{:S(2)}) %collective-permute-start.8) | collective-permute-done | bytes 294944 | tf_op jit(solution)/shard_map/ppermute | solution.py:119
  44.0 2.6 %collective-permute-start.10 = (bf16[192,768]{1,0:T(8,128)(2,1)S(1)}, bf16[192,768]{1,0:T(8,128)(2,1)S(1)}, u32[]{:S(2)}, u32[]{:S(2)}) collective-permute-start(bf16[192,768]{1,0:T(8,128)(2,1)S(1)} %broadcast_select_fusion.5), channel_id=1, source_target_pairs={{0,8},{8,0},{16,24},{24,16},{1,9},{9,1},{17,25},{25,17},{2,10},{10... | collective-permute-start | bytes 884744 | tf_op jit(solution)/shard_map/ppermute | solution.py:119
  46.6 2.3 %slice-done.13 = bf16[3072,768]{1,0:T(8,128)(2,1)S(1)} async-done(((bf16[3072,6144]{1,0:T(8,128)(2,1)}), bf16[3072,768]{1,0:T(8,128)(2,1)S(1)}, s32[]{:S(2)}) %slice-start.13) | async-done | bytes 4718616 | tf_op jit(solution)/shard_map/slice | solution.py:102
  50.1 3.4 %collective-permute-done.10 = bf16[192,768]{1,0:T(8,128)(2,1)S(1)} collective-permute-done((bf16[192,768]{1,0:T(8,128)(2,1)S(1)}, bf16[192,768]{1,0:T(8,128)(2,1)S(1)}, u32[]{:S(2)}, u32[]{:S(2)}) %collective-permute-start.10) | collective-permute-done | bytes 294944 | tf_op jit(solution)/shard_map/ppermute | solution.py:119
  53.5 1.3 fusion.105
  55.2 2.2 %collective-permute-start.12 = (bf16[192,768]{1,0:T(8,128)(2,1)S(1)}, bf16[192,768]{1,0:T(8,128)(2,1)S(1)}, u32[]{:S(2)}, u32[]{:S(2)}) collective-permute-start(bf16[192,768]{1,0:T(8,128)(2,1)S(1)} %broadcast_select_fusion.4), channel_id=1, source_target_pairs={{0,8},{8,0},{16,24},{24,16},{1,9},{9,1},{17,25},{25,17},{2,10},{10... | collective-permute-start | bytes 884744 | tf_op jit(solution)/shard_map/ppermute | solution.py:119
  57.4 2.3 %slice-done.14 = bf16[3072,768]{1,0:T(8,128)(2,1)S(1)} async-done(((bf16[3072,6144]{1,0:T(8,128)(2,1)}), bf16[3072,768]{1,0:T(8,128)(2,1)S(1)}, s32[]{:S(2)}) %slice-start.14) | async-done | bytes 4718616 | tf_op jit(solution)/shard_map/slice | solution.py:102
  59.7 1.1 convolution_convert_fusion.1
  60.8 3.8 %collective-permute-done.12 = bf16[192,768]{1,0:T(8,128)(2,1)S(1)} collective-permute-done((bf16[192,768]{1,0:T(8,128)(2,1)S(1)}, bf16[192,768]{1,0:T(8,128)(2,1)S(1)}, u32[]{:S(2)}, u32[]{:S(2)}) %collective-permute-start.12) | collective-permute-done | bytes 294944 | tf_op jit(solution)/shard_map/ppermute | solution.py:119
  64.8 1.3 fusion.103
  67.9 1.8 %slice-done.15 = bf16[3072,768]{1,0:T(8,128)(2,1)S(1)} async-done(((bf16[3072,6144]{1,0:T(8,128)(2,1)}), bf16[3072,768]{1,0:T(8,128)(2,1)S(1)}, s32[]{:S(2)}) %slice-start.15) | async-done | bytes 4718616 | tf_op jit(solution)/shard_map/slice | solution.py:102
  70.9 5.0 %collective-permute-done.14 = bf16[192,768]{1,0:T(8,128)(2,1)S(1)} collective-permute-done((bf16[192,768]{1,0:T(8,128)(2,1)S(1)}, bf16[192,768]{1,0:T(8,128)(2,1)S(1)}, u32[]{:S(2)}, u32[]{:S(2)}) %collective-permute-start.14) | collective-permute-done | bytes 294944 | tf_op jit(solution)/shard_map/ppermute | solution.py:119
  77.4 1.3 slice-done.2
  78.7 1.3 fusion.101
  80.3 5.5 %collective-permute-done.16 = bf16[192,768]{1,0:T(8,128)(2,1)S(1)} collective-permute-done((bf16[192,768]{1,0:T(8,128)(2,1)S(1)}, bf16[192,768]{1,0:T(8,128)(2,1)S(1)}, u32[]{:S(2)}, u32[]{:S(2)}) %collective-permute-start.16) | collective-permute-done | bytes 294944 | tf_op jit(solution)/shard_map/ppermute | solution.py:119
  87.3 1.3 slice-done.3
  88.6 1.3 fusion.99
  90.2 5.5 %collective-permute-done.18 = bf16[192,768]{1,0:T(8,128)(2,1)S(1)} collective-permute-done((bf16[192,768]{1,0:T(8,128)(2,1)S(1)}, bf16[192,768]{1,0:T(8,128)(2,1)S(1)}, u32[]{:S(2)}, u32[]{:S(2)}) %collective-permute-start.18) | collective-permute-done | bytes 294944 | tf_op jit(solution)/shard_map/ppermute | solution.py:119
  97.3 1.3 slice-done.4
  98.6 1.3 fusion.97
  100.2 5.5 %collective-permute-done.20 = bf16[192,768]{1,0:T(8,128)(2,1)S(1)} collective-permute-done((bf16[192,768]{1,0:T(8,128)(2,1)S(1)}, bf16[192,768]{1,0:T(8,128)(2,1)S(1)}, u32[]{:S(2)}, u32[]{:S(2)}) %collective-permute-start.20) | collective-permute-done | bytes 294944 | tf_op jit(solution)/shard_map/ppermute | solution.py:119
  107.2 1.3 fusion.95
  108.6 2.9 %collective-permute-start.26 = (bf16[96,768]{1,0:T(8,128)(2,1)S(1)}, bf16[96,768]{1,0:T(8,128)(2,1)S(1)}, u32[]{:S(2)}, u32[]{:S(2)}) collective-permute-start(bf16[96,768]{1,0:T(8,128)(2,1)S(1)} %fusion.73), channel_id=1, source_target_pairs={{0,8},{8,0},{16,24},{24,16},{1,9},{9,1},{17,25},{25,17},{2,10},{10... | collective-permute-start | bytes 442376 | tf_op jit(solution)/shard_map/ppermute | solution.py:119
  111.6 4.6 %collective-permute-done.22 = bf16[192,768]{1,0:T(8,128)(2,1)S(1)} collective-permute-done((bf16[192,768]{1,0:T(8,128)(2,1)S(1)}, bf16[192,768]{1,0:T(8,128)(2,1)S(1)}, u32[]{:S(2)}, u32[]{:S(2)}) %collective-permute-start.22) | collective-permute-done | bytes 294944 | tf_op jit(solution)/shard_map/ppermute | solution.py:119
  116.1 1.2 add_add_fusion
  117.3 1.5 %collective-permute-done.26 = bf16[96,768]{1,0:T(8,128)(2,1)S(1)} collective-permute-done((bf16[96,768]{1,0:T(8,128)(2,1)S(1)}, bf16[96,768]{1,0:T(8,128)(2,1)S(1)}, u32[]{:S(2)}, u32[]{:S(2)}) %collective-permute-start.26) | collective-permute-done | bytes 147488 | tf_op jit(solution)/shard_map/ppermute | solution.py:119
  120.3 1.7 %collective-permute-done.23 = bf16[96,768]{1,0:T(8,128)(2,1)S(1)} collective-permute-done((bf16[96,768]{1,0:T(8,128)(2,1)S(1)}, bf16[96,768]{1,0:T(8,128)(2,1)S(1)}, u32[]{:S(2)}, u32[]{:S(2)}) %collective-permute-start.23) | collective-permute-done | bytes 147488 | tf_op jit(solution)/shard_map/ppermute | solution.py:122
  122.1 4.4 %collective-permute-start.25 = (bf16[96,768]{1,0:T(8,128)(2,1)S(1)}, bf16[96,768]{1,0:T(8,128)(2,1)S(1)}, u32[]{:S(2)}, u32[]{:S(2)}) collective-permute-start(bf16[96,768]{1,0:T(8,128)(2,1)S(1)} %fusion.81), channel_id=1, source_target_pairs={{0,8},{8,0},{16,24},{24,16},{1,9},{9,1},{17,25},{25,17},{2,10},{10... | collective-permute-start | bytes 442376 | tf_op jit(solution)/shard_map/ppermute | solution.py:119
  126.5 3.6 %collective-permute-done.25 = bf16[96,768]{1,0:T(8,128)(2,1)S(1)} collective-permute-done((bf16[96,768]{1,0:T(8,128)(2,1)S(1)}, bf16[96,768]{1,0:T(8,128)(2,1)S(1)}, u32[]{:S(2)}, u32[]{:S(2)}) %collective-permute-start.25) | collective-permute-done | bytes 147488 | tf_op jit(solution)/shard_map/ppermute | solution.py:119
  131.2 1.2 collective-permute-start.29
  132.3 2.3 %collective-permute-start.30 = (bf16[24,3072]{1,0:T(8,128)(2,1)S(1)}, bf16[24,3072]{1,0:T(8,128)(2,1)S(1)}, u32[]{:S(2)}, u32[]{:S(2)}) collective-permute-start(bf16[24,3072]{1,0:T(8,128)(2,1)S(1)} %get-tuple-element.106), channel_id=1, source_target_pairs={{0,6},{1,7},{2,4},{3,5},{4,2},{5,3},{6,0},{7,1},{8,14},{9,15},{10,... | collective-permute-start | bytes 442376 | tf_op jit(solution)/shard_map/ppermute | solution.py:34
  134.7 2.9 %collective-permute-done.28 = bf16[24,3072]{1,0:T(8,128)(2,1)S(1)} collective-permute-done((bf16[24,3072]{1,0:T(8,128)(2,1)S(1)}, bf16[24,3072]{1,0:T(8,128)(2,1)S(1)}, u32[]{:S(2)}, u32[]{:S(2)}) %collective-permute-start.28) | collective-permute-done | bytes 147488 | tf_op jit(solution)/shard_map/ppermute | solution.py:34
  137.9 1.6 %collective-permute-done.30 = bf16[24,3072]{1,0:T(8,128)(2,1)S(1)} collective-permute-done((bf16[24,3072]{1,0:T(8,128)(2,1)S(1)}, bf16[24,3072]{1,0:T(8,128)(2,1)S(1)}, u32[]{:S(2)}, u32[]{:S(2)}) %collective-permute-start.30) | collective-permute-done | bytes 147488 | tf_op jit(solution)/shard_map/ppermute | solution.py:34
  (113 shorter events, 24.0 us)
Async XLA Ops:
  1.1 4.7 %collective-permute-start = (f32[2,24]{1,0:T(2,128)S(1)}, f32[2,24]{1,0:T(2,128)S(1)}, u32[]{:S(2)}, u32[]{:S(2)}) collective-permute-start(f32[2,24]{1,0:T(2,128)S(1)} %pad_maximum_fusion.3), channel_id=1, source_target_pairs={{0,8},{8,0},{16,24},{24,16},{1,9},{9,1},{17,25},{25,17},{2,10},{10... | collective-permute-start | bytes 584 | tf_op jit(solution)/shard_map/ppermute | solution.py:40
  5.8 5.8 %copy-start = (bf16[24,3072]{1,0:T(8,128)(2,1)S(1)}, bf16[24,3072]{1,0:T(8,128)(2,1)}, u32[]{:S(2)}) copy-start(bf16[24,3072]{1,0:T(8,128)(2,1)} %param.7) | copy-start | bytes 442372
  5.8 5.8 %copy-start.3 = (f32[3072]{0:T(1024)S(1)}, f32[3072]{0:T(1024)}, u32[]{:S(2)}) copy-start(f32[3072]{0:T(1024)} %param.9) | copy-start | bytes 36868
  5.8 5.8 %copy-start.4 = (f32[3072]{0:T(1024)S(1)}, f32[3072]{0:T(1024)}, u32[]{:S(2)}) copy-start(f32[3072]{0:T(1024)} %param.8) | copy-start | bytes 36868
  5.8 9.1 %copy-start.1 = (f32[6144]{0:T(1024)S(1)}, f32[6144]{0:T(1024)}, u32[]{:S(2)}) copy-start(f32[6144]{0:T(1024)} %param.11) | copy-start | bytes 73732
  5.8 5.7 %collective-permute-start.1 = (f32[2,24]{1,0:T(2,128)S(1)}, f32[2,24]{1,0:T(2,128)S(1)}, u32[]{:S(2)}, u32[]{:S(2)}) collective-permute-start(f32[2,24]{1,0:T(2,128)S(1)} %fusion.128), channel_id=1, source_target_pairs={{0,16},{8,24},{16,0},{24,8},{1,17},{9,25},{17,1},{25,9},{2,18},{10... | collective-permute-start | bytes 584 | tf_op jit(solution)/shard_map/ppermute | solution.py:40
  11.8 6.7 %collective-permute-start.3 = (bf16[24,3072]{1,0:T(8,128)(2,1)S(1)}, bf16[24,3072]{1,0:T(8,128)(2,1)S(1)}, u32[]{:S(2)}, u32[]{:S(2)}) collective-permute-start(bf16[24,3072]{1,0:T(8,128)(2,1)S(1)} %get-tuple-element.104), channel_id=1, source_target_pairs={{2,0},{3,1},{0,2},{1,3},{6,4},{7,5},{4,6},{5,7},{10,8},{11,9},{8,1... | collective-permute-start | bytes 442376 | tf_op jit(solution)/shard_map/ppermute | solution.py:30
  13.3 7.9 %collective-permute-start.4 = (bf16[24,3072]{1,0:T(8,128)(2,1)S(1)}, bf16[24,3072]{1,0:T(8,128)(2,1)S(1)}, u32[]{:S(2)}, u32[]{:S(2)}) collective-permute-start(bf16[24,3072]{1,0:T(8,128)(2,1)S(1)} %get-tuple-element.104), channel_id=1, source_target_pairs={{4,0},{5,1},{6,2},{7,3},{0,4},{1,5},{2,6},{3,7},{12,8},{13,9},{14,... | collective-permute-start | bytes 442376 | tf_op jit(solution)/shard_map/ppermute | solution.py:30
  14.8 7.3 %collective-permute-start.2 = (bf16[24,3072]{1,0:T(8,128)(2,1)S(1)}, bf16[24,3072]{1,0:T(8,128)(2,1)S(1)}, u32[]{:S(2)}, u32[]{:S(2)}) collective-permute-start(bf16[24,3072]{1,0:T(8,128)(2,1)S(1)} %get-tuple-element.104), channel_id=1, source_target_pairs={{6,0},{7,1},{4,2},{5,3},{2,4},{3,5},{0,6},{1,7},{14,8},{15,9},{12,... | collective-permute-start | bytes 442376 | tf_op jit(solution)/shard_map/ppermute | solution.py:30
  22.2 2.1 %collective-permute-start.6 = (bf16[96,3072]{1,0:T(8,128)(2,1)S(1)}, bf16[96,3072]{1,0:T(8,128)(2,1)S(1)}, u32[]{:S(2)}, u32[]{:S(2)}) collective-permute-start(bf16[96,3072]{1,0:T(8,128)(2,1)S(1)} %pad_maximum_fusion), channel_id=1, source_target_pairs={{1,0},{0,1},{3,2},{2,3},{5,4},{4,5},{7,6},{6,7},{9,8},{8,9},{11,10... | collective-permute-start | bytes 1769480 | tf_op jit(solution)/shard_map/ppermute | solution.py:30
  22.3 12.0 %collective-permute-start.5 = (bf16[72,768]{1,0:T(8,128)(2,1)S(1)}, bf16[72,768]{1,0:T(8,128)(2,1)S(1)}, u32[]{:S(2)}, u32[]{:S(2)}) collective-permute-start(bf16[72,768]{1,0:T(8,128)(2,1)S(1)} %convolution_convert_fusion.8), channel_id=1, source_target_pairs={{0,8},{8,0},{16,24},{24,16},{1,9},{9,1},{17,25},{25,17},{2,10},{10... | collective-permute-start | bytes 331784 | tf_op jit(solution)/shard_map/ppermute | solution.py:119
  25.1 2.3 %slice-start.10 = ((bf16[3072,6144]{1,0:T(8,128)(2,1)}), bf16[3072,768]{1,0:T(8,128)(2,1)S(1)}, s32[]{:S(2)}) async-start(bf16[3072,6144]{1,0:T(8,128)(2,1)} %param.10), calls=%async_computation.10 | async-start | bytes 9437184 | tf_op jit(solution)/shard_map/slice | solution.py:102
  25.1 9.2 %collective-permute-start.7 = (bf16[120,768]{1,0:T(8,128)(2,1)S(1)}, bf16[120,768]{1,0:T(8,128)(2,1)S(1)}, u32[]{:S(2)}, u32[]{:S(2)}) collective-permute-start(bf16[120,768]{1,0:T(8,128)(2,1)S(1)} %convolution_convert_fusion.7), channel_id=1, source_target_pairs={{0,8},{8,0},{16,24},{24,16},{1,9},{9,1},{17,25},{25,17},{2,10},{10... | collective-permute-start | bytes 552968 | tf_op jit(solution)/shard_map/ppermute | solution.py:119
  28.6 2.3 %slice-start.11 = ((bf16[3072,6144]{1,0:T(8,128)(2,1)}), bf16[3072,768]{1,0:T(8,128)(2,1)S(1)}, s32[]{:S(2)}) async-start(bf16[3072,6144]{1,0:T(8,128)(2,1)} %param.10), calls=%async_computation.11 | async-start | bytes 9437184 | tf_op jit(solution)/shard_map/slice | solution.py:102
  34.4 9.1 %collective-permute-start.8 = (bf16[192,768]{1,0:T(8,128)(2,1)S(1)}, bf16[192,768]{1,0:T(8,128)(2,1)S(1)}, u32[]{:S(2)}, u32[]{:S(2)}) collective-permute-start(bf16[192,768]{1,0:T(8,128)(2,1)S(1)} %convolution_convert_fusion.6), channel_id=1, source_target_pairs={{0,8},{8,0},{16,24},{24,16},{1,9},{9,1},{17,25},{25,17},{2,10},{10... | collective-permute-start | bytes 884744 | tf_op jit(solution)/shard_map/ppermute | solution.py:119
  36.1 3.5 %collective-permute-start.9 = (bf16[192,768]{1,0:T(8,128)(2,1)S(1)}, bf16[192,768]{1,0:T(8,128)(2,1)S(1)}, u32[]{:S(2)}, u32[]{:S(2)}) collective-permute-start(bf16[192,768]{1,0:T(8,128)(2,1)S(1)} %add_convert_fusion.7), channel_id=1, source_target_pairs={{0,1},{1,0},{2,3},{3,2},{4,5},{5,4},{6,7},{7,6},{8,16},{9,17},{10,... | collective-permute-start | bytes 884744 | tf_op jit(solution)/shard_map/ppermute | solution.py:122
  36.2 2.3 %slice-start.12 = ((bf16[3072,6144]{1,0:T(8,128)(2,1)}), bf16[3072,768]{1,0:T(8,128)(2,1)S(1)}, s32[]{:S(2)}) async-start(bf16[3072,6144]{1,0:T(8,128)(2,1)} %param.10), calls=%async_computation.12 | async-start | bytes 9437184 | tf_op jit(solution)/shard_map/slice | solution.py:102
  43.6 6.5 %collective-permute-start.11 = (bf16[192,768]{1,0:T(8,128)(2,1)S(1)}, bf16[192,768]{1,0:T(8,128)(2,1)S(1)}, u32[]{:S(2)}, u32[]{:S(2)}) collective-permute-start(bf16[192,768]{1,0:T(8,128)(2,1)S(1)} %add_convert_fusion.6), channel_id=1, source_target_pairs={{0,1},{1,0},{2,3},{3,2},{4,5},{5,4},{6,7},{7,6},{8,16},{9,17},{10,... | collective-permute-start | bytes 884744 | tf_op jit(solution)/shard_map/ppermute | solution.py:122
  44.0 9.5 %collective-permute-start.10 = (bf16[192,768]{1,0:T(8,128)(2,1)S(1)}, bf16[192,768]{1,0:T(8,128)(2,1)S(1)}, u32[]{:S(2)}, u32[]{:S(2)}) collective-permute-start(bf16[192,768]{1,0:T(8,128)(2,1)S(1)} %broadcast_select_fusion.5), channel_id=1, source_target_pairs={{0,8},{8,0},{16,24},{24,16},{1,9},{9,1},{17,25},{25,17},{2,10},{10... | collective-permute-start | bytes 884744 | tf_op jit(solution)/shard_map/ppermute | solution.py:119
  48.9 4.6 %slice-start = ((bf16[6144,3072]{1,0:T(8,128)(2,1)}), bf16[768,3072]{1,0:T(8,128)(2,1)S(1)}, s32[]{:S(2)}) async-start(bf16[6144,3072]{1,0:T(8,128)(2,1)} %param.12), calls=%async_computation | async-start | bytes 9437184 | tf_op jit(solution)/shard_map/slice | solution.py:102
  54.8 6.0 %collective-permute-start.13 = (bf16[192,768]{1,0:T(8,128)(2,1)S(1)}, bf16[192,768]{1,0:T(8,128)(2,1)S(1)}, u32[]{:S(2)}, u32[]{:S(2)}) collective-permute-start(bf16[192,768]{1,0:T(8,128)(2,1)S(1)} %add_convert_fusion.5), channel_id=1, source_target_pairs={{0,1},{1,0},{2,3},{3,2},{4,5},{5,4},{6,7},{7,6},{8,16},{9,17},{10,... | collective-permute-start | bytes 884744 | tf_op jit(solution)/shard_map/ppermute | solution.py:122
  55.2 9.5 %collective-permute-start.12 = (bf16[192,768]{1,0:T(8,128)(2,1)S(1)}, bf16[192,768]{1,0:T(8,128)(2,1)S(1)}, u32[]{:S(2)}, u32[]{:S(2)}) collective-permute-start(bf16[192,768]{1,0:T(8,128)(2,1)S(1)} %broadcast_select_fusion.4), channel_id=1, source_target_pairs={{0,8},{8,0},{16,24},{24,16},{1,9},{9,1},{17,25},{25,17},{2,10},{10... | collective-permute-start | bytes 884744 | tf_op jit(solution)/shard_map/ppermute | solution.py:119
  59.7 5.0 %slice-start.1 = ((bf16[6144,3072]{1,0:T(8,128)(2,1)}), bf16[768,3072]{1,0:T(8,128)(2,1)S(1)}, s32[]{:S(2)}) async-start(bf16[6144,3072]{1,0:T(8,128)(2,1)} %param.12), calls=%async_computation.1 | async-start | bytes 9437184 | tf_op jit(solution)/shard_map/slice | solution.py:102
  66.0 4.9 %collective-permute-start.15 = (bf16[192,768]{1,0:T(8,128)(2,1)S(1)}, bf16[192,768]{1,0:T(8,128)(2,1)S(1)}, u32[]{:S(2)}, u32[]{:S(2)}) collective-permute-start(bf16[192,768]{1,0:T(8,128)(2,1)S(1)} %add_convert_fusion.4), channel_id=1, source_target_pairs={{0,1},{1,0},{2,3},{3,2},{4,5},{5,4},{6,7},{7,6},{8,16},{9,17},{10,... | collective-permute-start | bytes 884744 | tf_op jit(solution)/shard_map/ppermute | solution.py:122
  66.4 9.5 %collective-permute-start.14 = (bf16[192,768]{1,0:T(8,128)(2,1)S(1)}, bf16[192,768]{1,0:T(8,128)(2,1)S(1)}, u32[]{:S(2)}, u32[]{:S(2)}) collective-permute-start(bf16[192,768]{1,0:T(8,128)(2,1)S(1)} %broadcast_select_fusion.3), channel_id=1, source_target_pairs={{0,8},{8,0},{16,24},{24,16},{1,9},{9,1},{17,25},{25,17},{2,10},{10... | collective-permute-start | bytes 884744 | tf_op jit(solution)/shard_map/ppermute | solution.py:119
  76.0 4.3 %collective-permute-start.17 = (bf16[192,768]{1,0:T(8,128)(2,1)S(1)}, bf16[192,768]{1,0:T(8,128)(2,1)S(1)}, u32[]{:S(2)}, u32[]{:S(2)}) collective-permute-start(bf16[192,768]{1,0:T(8,128)(2,1)S(1)} %add_convert_fusion.3), channel_id=1, source_target_pairs={{0,1},{1,0},{2,3},{3,2},{4,5},{5,4},{6,7},{7,6},{8,16},{9,17},{10,... | collective-permute-start | bytes 884744 | tf_op jit(solution)/shard_map/ppermute | solution.py:122
  76.4 2.3 %slice-start.2 = ((bf16[6144,3072]{1,0:T(8,128)(2,1)}), bf16[768,3072]{1,0:T(8,128)(2,1)S(1)}, s32[]{:S(2)}) async-start(bf16[6144,3072]{1,0:T(8,128)(2,1)} %param.12), calls=%async_computation.2 | async-start | bytes 9437184 | tf_op jit(solution)/shard_map/slice | solution.py:102
  76.4 9.5 %collective-permute-start.16 = (bf16[192,768]{1,0:T(8,128)(2,1)S(1)}, bf16[192,768]{1,0:T(8,128)(2,1)S(1)}, u32[]{:S(2)}, u32[]{:S(2)}) collective-permute-start(bf16[192,768]{1,0:T(8,128)(2,1)S(1)} %broadcast_select_fusion.2), channel_id=1, source_target_pairs={{0,8},{8,0},{16,24},{24,16},{1,9},{9,1},{17,25},{25,17},{2,10},{10... | collective-permute-start | bytes 884744 | tf_op jit(solution)/shard_map/ppermute | solution.py:119
  85.9 4.3 %collective-permute-start.19 = (bf16[192,768]{1,0:T(8,128)(2,1)S(1)}, bf16[192,768]{1,0:T(8,128)(2,1)S(1)}, u32[]{:S(2)}, u32[]{:S(2)}) collective-permute-start(bf16[192,768]{1,0:T(8,128)(2,1)S(1)} %add_convert_fusion.2), channel_id=1, source_target_pairs={{0,1},{1,0},{2,3},{3,2},{4,5},{5,4},{6,7},{7,6},{8,16},{9,17},{10,... | collective-permute-start | bytes 884744 | tf_op jit(solution)/shard_map/ppermute | solution.py:122
  86.3 2.3 %slice-start.3 = ((bf16[6144,3072]{1,0:T(8,128)(2,1)}), bf16[768,3072]{1,0:T(8,128)(2,1)S(1)}, s32[]{:S(2)}) async-start(bf16[6144,3072]{1,0:T(8,128)(2,1)} %param.12), calls=%async_computation.3 | async-start | bytes 9437184 | tf_op jit(solution)/shard_map/slice | solution.py:102
  86.3 9.5 %collective-permute-start.18 = (bf16[192,768]{1,0:T(8,128)(2,1)S(1)}, bf16[192,768]{1,0:T(8,128)(2,1)S(1)}, u32[]{:S(2)}, u32[]{:S(2)}) collective-permute-start(bf16[192,768]{1,0:T(8,128)(2,1)S(1)} %broadcast_select_fusion.1), channel_id=1, source_target_pairs={{0,8},{8,0},{16,24},{24,16},{1,9},{9,1},{17,25},{25,17},{2,10},{10... | collective-permute-start | bytes 884744 | tf_op jit(solution)/shard_map/ppermute | solution.py:119
  95.9 4.4 %collective-permute-start.21 = (bf16[192,768]{1,0:T(8,128)(2,1)S(1)}, bf16[192,768]{1,0:T(8,128)(2,1)S(1)}, u32[]{:S(2)}, u32[]{:S(2)}) collective-permute-start(bf16[192,768]{1,0:T(8,128)(2,1)S(1)} %add_convert_fusion.1), channel_id=1, source_target_pairs={{0,1},{1,0},{2,3},{3,2},{4,5},{5,4},{6,7},{7,6},{8,16},{9,17},{10,... | collective-permute-start | bytes 884744 | tf_op jit(solution)/shard_map/ppermute | solution.py:122
  96.3 2.3 %slice-start.4 = ((bf16[6144,3072]{1,0:T(8,128)(2,1)}), bf16[768,3072]{1,0:T(8,128)(2,1)S(1)}, s32[]{:S(2)}) async-start(bf16[6144,3072]{1,0:T(8,128)(2,1)} %param.12), calls=%async_computation.4 | async-start | bytes 9437184 | tf_op jit(solution)/shard_map/slice | solution.py:102
  96.3 9.5 %collective-permute-start.20 = (bf16[192,768]{1,0:T(8,128)(2,1)S(1)}, bf16[192,768]{1,0:T(8,128)(2,1)S(1)}, u32[]{:S(2)}, u32[]{:S(2)}) collective-permute-start(bf16[192,768]{1,0:T(8,128)(2,1)S(1)} %broadcast_select_fusion), channel_id=1, source_target_pairs={{0,8},{8,0},{16,24},{24,16},{1,9},{9,1},{17,25},{25,17},{2,10},{10... | collective-permute-start | bytes 884744 | tf_op jit(solution)/shard_map/ppermute | solution.py:119
  99.9 7.3 %slice-start.5 = ((bf16[6144,3072]{1,0:T(8,128)(2,1)}), bf16[768,3072]{1,0:T(8,128)(2,1)S(1)}, s32[]{:S(2)}) async-start(bf16[6144,3072]{1,0:T(8,128)(2,1)} %param.12), calls=%async_computation.5 | async-start | bytes 9437184 | tf_op jit(solution)/shard_map/slice | solution.py:102
  105.8 2.6 %collective-permute-start.24 = (bf16[96,768]{1,0:T(8,128)(2,1)S(1)}, bf16[96,768]{1,0:T(8,128)(2,1)S(1)}, u32[]{:S(2)}, u32[]{:S(2)}) collective-permute-start(bf16[96,768]{1,0:T(8,128)(2,1)S(1)} %get-tuple-element.109), channel_id=1, source_target_pairs={{0,1},{1,0},{2,3},{3,2},{4,5},{5,4},{6,7},{7,6},{8,16},{9,17},{10,... | collective-permute-start | bytes 442376 | tf_op jit(solution)/shard_map/ppermute | solution.py:122
  106.2 9.9 %collective-permute-start.22 = (bf16[192,768]{1,0:T(8,128)(2,1)S(1)}, bf16[192,768]{1,0:T(8,128)(2,1)S(1)}, u32[]{:S(2)}, u32[]{:S(2)}) collective-permute-start(bf16[192,768]{1,0:T(8,128)(2,1)S(1)} %fusion.60), channel_id=1, source_target_pairs={{0,8},{8,0},{16,24},{24,16},{1,9},{9,1},{17,25},{25,17},{2,10},{10... | collective-permute-start | bytes 884744 | tf_op jit(solution)/shard_map/ppermute | solution.py:119
  107.2 8.9 %slice-start.6 = ((bf16[6144,3072]{1,0:T(8,128)(2,1)}), bf16[768,3072]{1,0:T(8,128)(2,1)S(1)}, s32[]{:S(2)}) async-start(bf16[6144,3072]{1,0:T(8,128)(2,1)} %param.12), calls=%async_computation.6 | async-start | bytes 9437184 | tf_op jit(solution)/shard_map/slice | solution.py:102
  108.6 10.2 %slice-start.7 = ((bf16[6144,3072]{1,0:T(8,128)(2,1)}), bf16[768,3072]{1,0:T(8,128)(2,1)S(1)}, s32[]{:S(2)}) async-start(bf16[6144,3072]{1,0:T(8,128)(2,1)} %param.12), calls=%async_computation.7 | async-start | bytes 9437184 | tf_op jit(solution)/shard_map/slice | solution.py:102
  108.6 10.2 %collective-permute-start.26 = (bf16[96,768]{1,0:T(8,128)(2,1)S(1)}, bf16[96,768]{1,0:T(8,128)(2,1)S(1)}, u32[]{:S(2)}, u32[]{:S(2)}) collective-permute-start(bf16[96,768]{1,0:T(8,128)(2,1)S(1)} %fusion.73), channel_id=1, source_target_pairs={{0,8},{8,0},{16,24},{24,16},{1,9},{9,1},{17,25},{25,17},{2,10},{10... | collective-permute-start | bytes 442376 | tf_op jit(solution)/shard_map/ppermute | solution.py:119
  119.7 10.4 %collective-permute-start.27 = (bf16[96,3072]{1,0:T(8,128)(2,1)S(1)}, bf16[96,3072]{1,0:T(8,128)(2,1)S(1)}, u32[]{:S(2)}, u32[]{:S(2)}) collective-permute-start(bf16[96,3072]{1,0:T(8,128)(2,1)S(1)} %fusion), channel_id=1, source_target_pairs={{0,1},{1,0},{2,3},{3,2},{4,5},{5,4},{6,7},{7,6},{8,9},{9,8},{10,11... | collective-permute-start | bytes 1769480 | tf_op jit(solution)/shard_map/ppermute | solution.py:34
  119.8 2.2 %collective-permute-start.23 = (bf16[96,768]{1,0:T(8,128)(2,1)S(1)}, bf16[96,768]{1,0:T(8,128)(2,1)S(1)}, u32[]{:S(2)}, u32[]{:S(2)}) collective-permute-start(bf16[96,768]{1,0:T(8,128)(2,1)S(1)} %get-tuple-element.108), channel_id=1, source_target_pairs={{0,1},{1,0},{2,3},{3,2},{4,5},{5,4},{6,7},{7,6},{8,16},{9,17},{10,... | collective-permute-start | bytes 442376 | tf_op jit(solution)/shard_map/ppermute | solution.py:122
  122.1 8.0 %collective-permute-start.25 = (bf16[96,768]{1,0:T(8,128)(2,1)S(1)}, bf16[96,768]{1,0:T(8,128)(2,1)S(1)}, u32[]{:S(2)}, u32[]{:S(2)}) collective-permute-start(bf16[96,768]{1,0:T(8,128)(2,1)S(1)} %fusion.81), channel_id=1, source_target_pairs={{0,8},{8,0},{16,24},{24,16},{1,9},{9,1},{17,25},{25,17},{2,10},{10... | collective-permute-start | bytes 442376 | tf_op jit(solution)/shard_map/ppermute | solution.py:119
  126.5 3.6 %slice-start.8 = ((bf16[6144,3072]{1,0:T(8,128)(2,1)}), bf16[768,3072]{1,0:T(8,128)(2,1)S(1)}, s32[]{:S(2)}) async-start(bf16[6144,3072]{1,0:T(8,128)(2,1)} %param.12), calls=%async_computation.8 | async-start | bytes 9437184 | tf_op jit(solution)/shard_map/slice | solution.py:102
  126.5 13.0 %copy-start.2 = (f32[3072]{0:T(1024)S(1)}, f32[3072]{0:T(1024)}, u32[]{:S(2)}) copy-start(f32[3072]{0:T(1024)} %param.13) | copy-start | bytes 36868
  131.1 6.4 %collective-permute-start.28 = (bf16[24,3072]{1,0:T(8,128)(2,1)S(1)}, bf16[24,3072]{1,0:T(8,128)(2,1)S(1)}, u32[]{:S(2)}, u32[]{:S(2)}) collective-permute-start(bf16[24,3072]{1,0:T(8,128)(2,1)S(1)} %get-tuple-element.105), channel_id=1, source_target_pairs={{0,2},{1,3},{2,0},{3,1},{4,6},{5,7},{6,4},{7,5},{8,10},{9,11},{10,... | collective-permute-start | bytes 442376 | tf_op jit(solution)/shard_map/ppermute | solution.py:34
  131.2 6.8 %collective-permute-start.29 = (bf16[24,3072]{1,0:T(8,128)(2,1)S(1)}, bf16[24,3072]{1,0:T(8,128)(2,1)S(1)}, u32[]{:S(2)}, u32[]{:S(2)}) collective-permute-start(bf16[24,3072]{1,0:T(8,128)(2,1)S(1)} %get-tuple-element.107), channel_id=1, source_target_pairs={{0,4},{1,5},{2,6},{3,7},{4,0},{5,1},{6,2},{7,3},{8,12},{9,13},{10,... | collective-permute-start | bytes 442376 | tf_op jit(solution)/shard_map/ppermute | solution.py:34
  132.3 7.2 %collective-permute-start.30 = (bf16[24,3072]{1,0:T(8,128)(2,1)S(1)}, bf16[24,3072]{1,0:T(8,128)(2,1)S(1)}, u32[]{:S(2)}, u32[]{:S(2)}) collective-permute-start(bf16[24,3072]{1,0:T(8,128)(2,1)S(1)} %get-tuple-element.106), channel_id=1, source_target_pairs={{0,6},{1,7},{2,4},{3,5},{4,2},{5,3},{6,0},{7,1},{8,14},{9,15},{10,... | collective-permute-start | bytes 442376 | tf_op jit(solution)/shard_map/ppermute | solution.py:34
  (4 other events, 9.3 us)

commit v4 on v3

--- a/solution.py
+++ b/solution.py
@@ -9,7 +9,7 @@
 
 SHARES = (3, 3, 3, 3, 3, 3, 3, 3)
 UP_AHEAD = 3
-DOWN_AHEAD = 3
+DOWN_AHEAD = 2
 
 
 class Grid:
@@ -160,17 +160,24 @@
         up_part[k] = cut(w_up, 1, edges[k], edges[k + 1], gathered)
     partial, sums, own, hidden = {0: jnp.concatenate(first)}, {}, {}, {}
     terms = None
-    for t in range(count):
-        crossed = None
-        if t == 0:
-            faced = jnp.concatenate([face(v, facing) for v in first])
-        elif t == 1:
-            faced = face(partial[t], facing)
-        elif t < count:
-            width = max(size[t], size[t - 2])
-            faced = face(jnp.where(is_end, widened(partial[t], width), widened(own[t - 2], width)), facing)
-        if t > 0:
-            crossed = cross(sums[t - 1])
+
+    faced = [face(v, facing) for v in first]
+    stage(0, partial[0])
+    partial[1] = up(1)
+    ahead = face(partial[1], facing)
+    faced, _ = lax.optimization_barrier((faced, partial[1]))
+    parts = [(v.astype(jnp.float32) + came.astype(jnp.float32)).astype(jnp.bfloat16) for v, came in zip(first, faced)]
+    crossed = [cross(v) for v in parts]
+    stage(1, partial[1])
+    partial[2] = up(2)
+    ahead, crossed, partial[2] = lax.optimization_barrier((ahead, crossed, partial[2]))
+    sums[0] = jnp.concatenate(parts)
+    own[0] = activated(0, sums[0], jnp.concatenate(crossed))
+    sums[1] = (partial[1].astype(jnp.float32) + ahead.astype(jnp.float32)).astype(jnp.bfloat16)
+    for t in range(2, count):
+        width = max(size[t], size[t - 2])
+        faced = face(jnp.where(is_end, widened(partial[t], width), widened(own[t - 2], width)), facing)
+        crossed = cross(sums[t - 1])
         stage(t, partial[t])
         computed = []
         if t + 1 < count:
@@ -180,19 +187,15 @@
             product = down(t - 3)
             terms = product if terms is None else terms + product
             computed.append(terms)
-        joined = list(lax.optimization_barrier(tuple(v for v in (faced, crossed, *computed) if v is not None)))
-        faced = joined.pop(0)
-        if crossed is not None:
-            crossed = joined.pop(0)
+        joined = list(lax.optimization_barrier((faced, crossed, *computed)))
+        faced, crossed = joined.pop(0), joined.pop(0)
         if t + 1 < count:
             partial[t + 1] = joined.pop(0)
         if joined:
             terms = joined.pop(0)
-        if crossed is not None:
-            own[t - 1] = activated(t - 1, sums[t - 1], crossed)
+        own[t - 1] = activated(t - 1, sums[t - 1], crossed)
         sums[t] = (partial[t].astype(jnp.float32) + faced[:, : size[t]].astype(jnp.float32)).astype(jnp.bfloat16)
-        if t >= 2:
-            hidden[t - 2] = jnp.where(is_end, faced[:, : size[t - 2]], own[t - 2])
+        hidden[t - 2] = jnp.where(is_end, faced[:, : size[t - 2]], own[t - 2])
     faced = face(own[count - 2], facing)
     spans = (slice(half, None), slice(0, half))
     crossed = [cross(sums[count - 1][span]) for span in spans]

time: 141 us -> 141 us (level)
  local copies, waits for them, and re-layouts: 19.8 us -> 14.8 us
  waiting for transfers between devices: 56.7 us -> 59.6 us
  starting transfers between devices: 36.7 us -> 39.1 us
    slice x32, local copies, waits for them, and re-layouts: 17 us -> 12 us  [cut(): lax.slice_in_dim(weights, low, high, axis=axis)]
    ppermute x12, starting transfers between devices: 22.1 us -> 24.4 us  [face(): return lax.ppermute(sent, 'row', pairs)]
    ppermute x4, waiting for transfers between devices: 6.17 us -> 7.72 us  [take(): return lax.ppermute(value, 'col', pairs)]
  transfers between devices with their start and end apart: 31 -> 32, of which waited for: 18 -> 19; matrix products, arithmetic and copies ran while one was open for 16% -> 16% of each run, Pallas kernels for 0% -> 0%
where the time goes in v4:
time: 141 us
  waiting for transfers between devices  59.6 us (42%)
  starting transfers between devices  39.1 us (28%)
  matrix products  20.1 us (14%)
  local copies, waits for them, and re-layouts  14.8 us (10%)
  other arithmetic  6.45 us (5%)
    ppermute x12, waiting for transfers between devices, face(): return lax.ppermute(sent, 'row', pairs)  43.2 us
    ppermute x12, starting transfers between devices, face(): return lax.ppermute(sent, 'row', pairs)  24.4 us
    slice x32, local copies, waits for them, and re-layouts, cut(): lax.slice_in_dim(weights, low, high, axis=axis)  12 us
    dot_general x7, matrix products, down(): return jnp.dot(hidden[k], down_part[k], preferred_element_type=jnp.float32)  8.73 us
    dot_general x7, matrix products, up(): jnp.dot(gathered, up_part[k], preferred_element_type=jnp.float32)  7.78 us
    ppermute x4, waiting for transfers between devices, take(): return lax.ppermute(value, 'col', pairs)  7.72 us
    ppermute x2, starting transfers between devices, row_sum(): lax.ppermute(value, 'row', [(i, i ^ step) for i in range(grid.n_row)])  5.77 us
    ppermute x4, waiting for transfers between devices, give(): return lax.ppermute(value, 'col', pairs)  5 us
  transfers between devices with their start and end apart: 32, of which 19 were waited for; matrix products, arithmetic and copies ran while one was open for 16% of the time, Pallas kernels for 0%

profile of v4, /device:TPU:0, one launch (start us, length us, event | category | flops | bytes accessed | tf_op | source)
XLA Modules:
  0.0 140.7 jit_solution(5407107951659569812)
XLA Ops:
  1.1 3.1 %collective-permute-start = (f32[2,24]{1,0:T(2,128)S(1)}, f32[2,24]{1,0:T(2,128)S(1)}, u32[]{:S(2)}, u32[]{:S(2)}) collective-permute-start(f32[2,24]{1,0:T(2,128)S(1)} %pad_maximum_fusion.1), channel_id=1, source_target_pairs={{0,8},{8,0},{16,24},{24,16},{1,9},{9,1},{17,25},{25,17},{2,10},{10... | collective-permute-start | bytes 584 | tf_op jit(solution)/shard_map/ppermute | solution.py:40
  4.2 2.6 %slice.110 = bf16[3072,768]{1,0:T(8,128)(2,1)S(1)} slice(bf16[3072,6144]{1,0:T(8,128)(2,1)} %param.10), slice={[0:3072], [0:768]} | slice | bytes 9437184 | tf_op jit(solution)/shard_map/slice | solution.py:227
  6.9 2.7 %collective-permute-start.1 = (f32[2,24]{1,0:T(2,128)S(1)}, f32[2,24]{1,0:T(2,128)S(1)}, u32[]{:S(2)}, u32[]{:S(2)}) collective-permute-start(f32[2,24]{1,0:T(2,128)S(1)} %fusion.126), channel_id=1, source_target_pairs={{0,16},{8,24},{16,0},{24,8},{1,17},{9,25},{17,1},{25,9},{2,18},{10... | collective-permute-start | bytes 584 | tf_op jit(solution)/shard_map/ppermute | solution.py:40
  9.6 1.9 %collective-permute-done.1 = f32[2,24]{1,0:T(2,128)S(1)} collective-permute-done((f32[2,24]{1,0:T(2,128)S(1)}, f32[2,24]{1,0:T(2,128)S(1)}, u32[]{:S(2)}, u32[]{:S(2)}) %collective-permute-start.1) | collective-permute-done | bytes 224 | tf_op jit(solution)/shard_map/ppermute | solution.py:40
  11.6 1.6 %collective-permute-start.2 = (bf16[24,3072]{1,0:T(8,128)(2,1)S(1)}, bf16[24,3072]{1,0:T(8,128)(2,1)S(1)}, u32[]{:S(2)}, u32[]{:S(2)}) collective-permute-start(bf16[24,3072]{1,0:T(8,128)(2,1)S(1)} %get-tuple-element.104), channel_id=1, source_target_pairs={{2,0},{3,1},{0,2},{1,3},{6,4},{7,5},{4,6},{5,7},{10,8},{11,9},{8,1... | collective-permute-start | bytes 442376 | tf_op jit(solution)/shard_map/ppermute | solution.py:30
  13.2 1.5 %collective-permute-start.3 = (bf16[24,3072]{1,0:T(8,128)(2,1)S(1)}, bf16[24,3072]{1,0:T(8,128)(2,1)S(1)}, u32[]{:S(2)}, u32[]{:S(2)}) collective-permute-start(bf16[24,3072]{1,0:T(8,128)(2,1)S(1)} %get-tuple-element.104), channel_id=1, source_target_pairs={{4,0},{5,1},{6,2},{7,3},{0,4},{1,5},{2,6},{3,7},{12,8},{13,9},{14,... | collective-permute-start | bytes 442376 | tf_op jit(solution)/shard_map/ppermute | solution.py:30
  15.3 3.1 %collective-permute-done.2 = bf16[24,3072]{1,0:T(8,128)(2,1)S(1)} collective-permute-done((bf16[24,3072]{1,0:T(8,128)(2,1)S(1)}, bf16[24,3072]{1,0:T(8,128)(2,1)S(1)}, u32[]{:S(2)}, u32[]{:S(2)}) %collective-permute-start.2) | collective-permute-done | bytes 147488 | tf_op jit(solution)/shard_map/ppermute | solution.py:30
  18.3 2.8 %collective-permute-done.3 = bf16[24,3072]{1,0:T(8,128)(2,1)S(1)} collective-permute-done((bf16[24,3072]{1,0:T(8,128)(2,1)S(1)}, bf16[24,3072]{1,0:T(8,128)(2,1)S(1)}, u32[]{:S(2)}, u32[]{:S(2)}) %collective-permute-start.3) | collective-permute-done | bytes 147488 | tf_op jit(solution)/shard_map/ppermute | solution.py:30
  22.3 1.9 %collective-permute-done.5 = bf16[96,3072]{1,0:T(8,128)(2,1)S(1)} collective-permute-done((bf16[96,3072]{1,0:T(8,128)(2,1)S(1)}, bf16[96,3072]{1,0:T(8,128)(2,1)S(1)}, u32[]{:S(2)}, u32[]{:S(2)}) %collective-permute-start.5) | collective-permute-done | bytes 589856 | tf_op jit(solution)/shard_map/ppermute | solution.py:30
  24.2 2.3 %slice-done.11 = bf16[3072,768]{1,0:T(8,128)(2,1)S(1)} async-done(((bf16[3072,6144]{1,0:T(8,128)(2,1)}), bf16[3072,768]{1,0:T(8,128)(2,1)S(1)}, s32[]{:S(2)}) %slice-start.11) | async-done | bytes 4718616 | tf_op jit(solution)/shard_map/slice | solution.py:102
  26.6 1.1 convolution_convert_fusion.5
  28.8 1.3 slice-done.10
  31.8 1.1 convolution_convert_fusion.4
  33.0 3.1 %collective-permute-done.8 = bf16[120,768]{1,0:T(8,128)(2,1)S(1)} collective-permute-done((bf16[120,768]{1,0:T(8,128)(2,1)S(1)}, bf16[120,768]{1,0:T(8,128)(2,1)S(1)}, u32[]{:S(2)}, u32[]{:S(2)}) %collective-permute-start.8) | collective-permute-done | bytes 184352 | tf_op jit(solution)/shard_map/ppermute | solution.py:119
  36.8 1.1 convolution_convert_fusion.3
  38.0 3.6 %collective-permute-done.6 = bf16[192,768]{1,0:T(8,128)(2,1)S(1)} collective-permute-done((bf16[192,768]{1,0:T(8,128)(2,1)S(1)}, bf16[192,768]{1,0:T(8,128)(2,1)S(1)}, u32[]{:S(2)}, u32[]{:S(2)}) %collective-permute-start.6) | collective-permute-done | bytes 294944 | tf_op jit(solution)/shard_map/ppermute | solution.py:119
  42.1 5.2 %collective-permute-start.11 = (bf16[192,768]{1,0:T(8,128)(2,1)S(1)}, bf16[192,768]{1,0:T(8,128)(2,1)S(1)}, u32[]{:S(2)}, u32[]{:S(2)}) collective-permute-start(bf16[192,768]{1,0:T(8,128)(2,1)S(1)} %broadcast_select_fusion.5), channel_id=1, source_target_pairs={{0,8},{8,0},{16,24},{24,16},{1,9},{9,1},{17,25},{25,17},{2,10},{10... | collective-permute-start | bytes 884744 | tf_op jit(solution)/shard_map/ppermute | solution.py:119
  47.3 2.3 %slice-done.13 = bf16[3072,768]{1,0:T(8,128)(2,1)S(1)} async-done(((bf16[3072,6144]{1,0:T(8,128)(2,1)}), bf16[3072,768]{1,0:T(8,128)(2,1)S(1)}, s32[]{:S(2)}) %slice-start.13) | async-done | bytes 4718616 | tf_op jit(solution)/shard_map/slice | solution.py:102
  50.7 1.2 collective-permute-done.11
  52.0 1.3 fusion.103
  53.7 2.3 %collective-permute-start.13 = (bf16[192,768]{1,0:T(8,128)(2,1)S(1)}, bf16[192,768]{1,0:T(8,128)(2,1)S(1)}, u32[]{:S(2)}, u32[]{:S(2)}) collective-permute-start(bf16[192,768]{1,0:T(8,128)(2,1)S(1)} %broadcast_select_fusion.4), channel_id=1, source_target_pairs={{0,8},{8,0},{16,24},{24,16},{1,9},{9,1},{17,25},{25,17},{2,10},{10... | collective-permute-start | bytes 884744 | tf_op jit(solution)/shard_map/ppermute | solution.py:119
  56.1 2.3 %slice-done.14 = bf16[3072,768]{1,0:T(8,128)(2,1)S(1)} async-done(((bf16[3072,6144]{1,0:T(8,128)(2,1)}), bf16[3072,768]{1,0:T(8,128)(2,1)S(1)}, s32[]{:S(2)}) %slice-start.14) | async-done | bytes 4718616 | tf_op jit(solution)/shard_map/slice | solution.py:102
  59.5 3.6 %collective-permute-done.13 = bf16[192,768]{1,0:T(8,128)(2,1)S(1)} collective-permute-done((bf16[192,768]{1,0:T(8,128)(2,1)S(1)}, bf16[192,768]{1,0:T(8,128)(2,1)S(1)}, u32[]{:S(2)}, u32[]{:S(2)}) %collective-permute-start.13) | collective-permute-done | bytes 294944 | tf_op jit(solution)/shard_map/ppermute | solution.py:119
  63.3 1.3 fusion.101
  64.9 1.4 collective-permute-start.15
  66.8 1.8 %slice-done.15 = bf16[3072,768]{1,0:T(8,128)(2,1)S(1)} async-done(((bf16[3072,6144]{1,0:T(8,128)(2,1)}), bf16[3072,768]{1,0:T(8,128)(2,1)S(1)}, s32[]{:S(2)}) %slice-start.15) | async-done | bytes 4718616 | tf_op jit(solution)/shard_map/slice | solution.py:102
  68.7 1.1 convolution_convert_fusion
  69.8 4.6 %collective-permute-done.15 = bf16[192,768]{1,0:T(8,128)(2,1)S(1)} collective-permute-done((bf16[192,768]{1,0:T(8,128)(2,1)S(1)}, bf16[192,768]{1,0:T(8,128)(2,1)S(1)}, u32[]{:S(2)}, u32[]{:S(2)}) %collective-permute-start.15) | collective-permute-done | bytes 294944 | tf_op jit(solution)/shard_map/ppermute | solution.py:119
  74.9 1.3 collective-permute-start.17
  77.2 1.3 fusion.99
  78.8 5.5 %collective-permute-done.17 = bf16[192,768]{1,0:T(8,128)(2,1)S(1)} collective-permute-done((bf16[192,768]{1,0:T(8,128)(2,1)S(1)}, bf16[192,768]{1,0:T(8,128)(2,1)S(1)}, u32[]{:S(2)}, u32[]{:S(2)}) %collective-permute-start.17) | collective-permute-done | bytes 294944 | tf_op jit(solution)/shard_map/ppermute | solution.py:119
  84.8 1.3 collective-permute-start.19
  86.1 1.3 fusion.97
  87.8 6.5 %collective-permute-done.19 = bf16[192,768]{1,0:T(8,128)(2,1)S(1)} collective-permute-done((bf16[192,768]{1,0:T(8,128)(2,1)S(1)}, bf16[192,768]{1,0:T(8,128)(2,1)S(1)}, u32[]{:S(2)}, u32[]{:S(2)}) %collective-permute-start.19) | collective-permute-done | bytes 294944 | tf_op jit(solution)/shard_map/ppermute | solution.py:119
  94.8 1.3 collective-permute-start.21
  96.1 1.3 fusion.95
  97.7 6.5 %collective-permute-done.21 = bf16[192,768]{1,0:T(8,128)(2,1)S(1)} collective-permute-done((bf16[192,768]{1,0:T(8,128)(2,1)S(1)}, bf16[192,768]{1,0:T(8,128)(2,1)S(1)}, u32[]{:S(2)}, u32[]{:S(2)}) %collective-permute-start.21) | collective-permute-done | bytes 294944 | tf_op jit(solution)/shard_map/ppermute | solution.py:119
  104.7 1.3 collective-permute-start.23
  106.2 3.9 %collective-permute-start.27 = (bf16[96,768]{1,0:T(8,128)(2,1)S(1)}, bf16[96,768]{1,0:T(8,128)(2,1)S(1)}, u32[]{:S(2)}, u32[]{:S(2)}) collective-permute-start(bf16[96,768]{1,0:T(8,128)(2,1)S(1)} %fusion.74), channel_id=1, source_target_pairs={{0,8},{8,0},{16,24},{24,16},{1,9},{9,1},{17,25},{25,17},{2,10},{10... | collective-permute-start | bytes 442376 | tf_op jit(solution)/shard_map/ppermute | solution.py:119
  110.0 4.6 %collective-permute-done.23 = bf16[192,768]{1,0:T(8,128)(2,1)S(1)} collective-permute-done((bf16[192,768]{1,0:T(8,128)(2,1)S(1)}, bf16[192,768]{1,0:T(8,128)(2,1)S(1)}, u32[]{:S(2)}, u32[]{:S(2)}) %collective-permute-start.23) | collective-permute-done | bytes 294944 | tf_op jit(solution)/shard_map/ppermute | solution.py:119
  115.8 1.3 fusion
  119.6 1.7 %collective-permute-done.24 = bf16[96,768]{1,0:T(8,128)(2,1)S(1)} collective-permute-done((bf16[96,768]{1,0:T(8,128)(2,1)S(1)}, bf16[96,768]{1,0:T(8,128)(2,1)S(1)}, u32[]{:S(2)}, u32[]{:S(2)}) %collective-permute-start.24) | collective-permute-done | bytes 147488 | tf_op jit(solution)/shard_map/ppermute | solution.py:122
  121.4 5.4 %collective-permute-start.26 = (bf16[96,768]{1,0:T(8,128)(2,1)S(1)}, bf16[96,768]{1,0:T(8,128)(2,1)S(1)}, u32[]{:S(2)}, u32[]{:S(2)}) collective-permute-start(bf16[96,768]{1,0:T(8,128)(2,1)S(1)} %fusion.82), channel_id=1, source_target_pairs={{0,8},{8,0},{16,24},{24,16},{1,9},{9,1},{17,25},{25,17},{2,10},{10... | collective-permute-start | bytes 442376 | tf_op jit(solution)/shard_map/ppermute | solution.py:119
  126.8 3.6 %collective-permute-done.26 = bf16[96,768]{1,0:T(8,128)(2,1)S(1)} collective-permute-done((bf16[96,768]{1,0:T(8,128)(2,1)S(1)}, bf16[96,768]{1,0:T(8,128)(2,1)S(1)}, u32[]{:S(2)}, u32[]{:S(2)}) %collective-permute-start.26) | collective-permute-done | bytes 147488 | tf_op jit(solution)/shard_map/ppermute | solution.py:119
  131.4 1.3 collective-permute-start.30
  132.7 2.2 %collective-permute-start.31 = (bf16[24,3072]{1,0:T(8,128)(2,1)S(1)}, bf16[24,3072]{1,0:T(8,128)(2,1)S(1)}, u32[]{:S(2)}, u32[]{:S(2)}) collective-permute-start(bf16[24,3072]{1,0:T(8,128)(2,1)S(1)} %get-tuple-element.106), channel_id=1, source_target_pairs={{0,6},{1,7},{2,4},{3,5},{4,2},{5,3},{6,0},{7,1},{8,14},{9,15},{10,... | collective-permute-start | bytes 442376 | tf_op jit(solution)/shard_map/ppermute | solution.py:34
  134.9 2.8 %collective-permute-done.29 = bf16[24,3072]{1,0:T(8,128)(2,1)S(1)} collective-permute-done((bf16[24,3072]{1,0:T(8,128)(2,1)S(1)}, bf16[24,3072]{1,0:T(8,128)(2,1)S(1)}, u32[]{:S(2)}, u32[]{:S(2)}) %collective-permute-start.29) | collective-permute-done | bytes 147488 | tf_op jit(solution)/shard_map/ppermute | solution.py:34
  138.2 1.7 %collective-permute-done.31 = bf16[24,3072]{1,0:T(8,128)(2,1)S(1)} collective-permute-done((bf16[24,3072]{1,0:T(8,128)(2,1)S(1)}, bf16[24,3072]{1,0:T(8,128)(2,1)S(1)}, u32[]{:S(2)}, u32[]{:S(2)}) %collective-permute-start.31) | collective-permute-done | bytes 147488 | tf_op jit(solution)/shard_map/ppermute | solution.py:34
  (115 shorter events, 20.6 us)
Async XLA Ops:
  1.1 5.8 %collective-permute-start = (f32[2,24]{1,0:T(2,128)S(1)}, f32[2,24]{1,0:T(2,128)S(1)}, u32[]{:S(2)}, u32[]{:S(2)}) collective-permute-start(f32[2,24]{1,0:T(2,128)S(1)} %pad_maximum_fusion.1), channel_id=1, source_target_pairs={{0,8},{8,0},{16,24},{24,16},{1,9},{9,1},{17,25},{25,17},{2,10},{10... | collective-permute-start | bytes 584 | tf_op jit(solution)/shard_map/ppermute | solution.py:40
  6.9 4.6 %copy-start = (bf16[24,3072]{1,0:T(8,128)(2,1)S(1)}, bf16[24,3072]{1,0:T(8,128)(2,1)}, u32[]{:S(2)}) copy-start(bf16[24,3072]{1,0:T(8,128)(2,1)} %param.7) | copy-start | bytes 442372
  6.9 4.6 %copy-start.3 = (f32[3072]{0:T(1024)S(1)}, f32[3072]{0:T(1024)}, u32[]{:S(2)}) copy-start(f32[3072]{0:T(1024)} %param.9) | copy-start | bytes 36868
  6.9 4.6 %copy-start.4 = (f32[3072]{0:T(1024)S(1)}, f32[3072]{0:T(1024)}, u32[]{:S(2)}) copy-start(f32[3072]{0:T(1024)} %param.8) | copy-start | bytes 36868
  6.9 7.8 %copy-start.1 = (f32[6144]{0:T(1024)S(1)}, f32[6144]{0:T(1024)}, u32[]{:S(2)}) copy-start(f32[6144]{0:T(1024)} %param.11) | copy-start | bytes 73732
  6.9 4.5 %collective-permute-start.1 = (f32[2,24]{1,0:T(2,128)S(1)}, f32[2,24]{1,0:T(2,128)S(1)}, u32[]{:S(2)}, u32[]{:S(2)}) collective-permute-start(f32[2,24]{1,0:T(2,128)S(1)} %fusion.126), channel_id=1, source_target_pairs={{0,16},{8,24},{16,0},{24,8},{1,17},{9,25},{17,1},{25,9},{2,18},{10... | collective-permute-start | bytes 584 | tf_op jit(solution)/shard_map/ppermute | solution.py:40
  11.6 6.7 %collective-permute-start.2 = (bf16[24,3072]{1,0:T(8,128)(2,1)S(1)}, bf16[24,3072]{1,0:T(8,128)(2,1)S(1)}, u32[]{:S(2)}, u32[]{:S(2)}) collective-permute-start(bf16[24,3072]{1,0:T(8,128)(2,1)S(1)} %get-tuple-element.104), channel_id=1, source_target_pairs={{2,0},{3,1},{0,2},{1,3},{6,4},{7,5},{4,6},{5,7},{10,8},{11,9},{8,1... | collective-permute-start | bytes 442376 | tf_op jit(solution)/shard_map/ppermute | solution.py:30
  13.2 7.9 %collective-permute-start.3 = (bf16[24,3072]{1,0:T(8,128)(2,1)S(1)}, bf16[24,3072]{1,0:T(8,128)(2,1)S(1)}, u32[]{:S(2)}, u32[]{:S(2)}) collective-permute-start(bf16[24,3072]{1,0:T(8,128)(2,1)S(1)} %get-tuple-element.104), channel_id=1, source_target_pairs={{4,0},{5,1},{6,2},{7,3},{0,4},{1,5},{2,6},{3,7},{12,8},{13,9},{14,... | collective-permute-start | bytes 442376 | tf_op jit(solution)/shard_map/ppermute | solution.py:30
  14.7 7.3 %collective-permute-start.4 = (bf16[24,3072]{1,0:T(8,128)(2,1)S(1)}, bf16[24,3072]{1,0:T(8,128)(2,1)S(1)}, u32[]{:S(2)}, u32[]{:S(2)}) collective-permute-start(bf16[24,3072]{1,0:T(8,128)(2,1)S(1)} %get-tuple-element.104), channel_id=1, source_target_pairs={{6,0},{7,1},{4,2},{5,3},{2,4},{3,5},{0,6},{1,7},{14,8},{15,9},{12,... | collective-permute-start | bytes 442376 | tf_op jit(solution)/shard_map/ppermute | solution.py:30
  22.1 2.1 %collective-permute-start.5 = (bf16[96,3072]{1,0:T(8,128)(2,1)S(1)}, bf16[96,3072]{1,0:T(8,128)(2,1)S(1)}, u32[]{:S(2)}, u32[]{:S(2)}) collective-permute-start(bf16[96,3072]{1,0:T(8,128)(2,1)S(1)} %pad_maximum_fusion), channel_id=1, source_target_pairs={{1,0},{0,1},{3,2},{2,3},{5,4},{4,5},{7,6},{6,7},{9,8},{8,9},{11,10... | collective-permute-start | bytes 1769480 | tf_op jit(solution)/shard_map/ppermute | solution.py:30
  22.2 10.8 %collective-permute-start.7 = (bf16[72,768]{1,0:T(8,128)(2,1)S(1)}, bf16[72,768]{1,0:T(8,128)(2,1)S(1)}, u32[]{:S(2)}, u32[]{:S(2)}) collective-permute-start(bf16[72,768]{1,0:T(8,128)(2,1)S(1)} %convolution_convert_fusion.8), channel_id=1, source_target_pairs={{0,8},{8,0},{16,24},{24,16},{1,9},{9,1},{17,25},{25,17},{2,10},{10... | collective-permute-start | bytes 331784 | tf_op jit(solution)/shard_map/ppermute | solution.py:119
  24.2 2.3 %slice-start.11 = ((bf16[3072,6144]{1,0:T(8,128)(2,1)}), bf16[3072,768]{1,0:T(8,128)(2,1)S(1)}, s32[]{:S(2)}) async-start(bf16[3072,6144]{1,0:T(8,128)(2,1)} %param.10), calls=%async_computation.11 | async-start | bytes 9437184 | tf_op jit(solution)/shard_map/slice | solution.py:102
  27.7 2.3 %slice-start.10 = ((bf16[3072,6144]{1,0:T(8,128)(2,1)}), bf16[3072,768]{1,0:T(8,128)(2,1)S(1)}, s32[]{:S(2)}) async-start(bf16[3072,6144]{1,0:T(8,128)(2,1)} %param.10), calls=%async_computation.10 | async-start | bytes 9437184 | tf_op jit(solution)/shard_map/slice | solution.py:102
  28.5 3.3 %slice-start.9 = ((bf16[3072,6144]{1,0:T(8,128)(2,1)}), bf16[3072,768]{1,0:T(8,128)(2,1)S(1)}, s32[]{:S(2)}) async-start(bf16[3072,6144]{1,0:T(8,128)(2,1)} %param.10), calls=%async_computation.9 | async-start | bytes 9437184 | tf_op jit(solution)/shard_map/slice | solution.py:102
  28.5 7.6 %collective-permute-start.8 = (bf16[120,768]{1,0:T(8,128)(2,1)S(1)}, bf16[120,768]{1,0:T(8,128)(2,1)S(1)}, u32[]{:S(2)}, u32[]{:S(2)}) collective-permute-start(bf16[120,768]{1,0:T(8,128)(2,1)S(1)} %convolution_convert_fusion.7), channel_id=1, source_target_pairs={{0,8},{8,0},{16,24},{24,16},{1,9},{9,1},{17,25},{25,17},{2,10},{10... | collective-permute-start | bytes 552968 | tf_op jit(solution)/shard_map/ppermute | solution.py:119
  31.2 10.5 %collective-permute-start.6 = (bf16[192,768]{1,0:T(8,128)(2,1)S(1)}, bf16[192,768]{1,0:T(8,128)(2,1)S(1)}, u32[]{:S(2)}, u32[]{:S(2)}) collective-permute-start(bf16[192,768]{1,0:T(8,128)(2,1)S(1)} %convolution_convert_fusion.6), channel_id=1, source_target_pairs={{0,8},{8,0},{16,24},{24,16},{1,9},{9,1},{17,25},{25,17},{2,10},{10... | collective-permute-start | bytes 884744 | tf_op jit(solution)/shard_map/ppermute | solution.py:119
  32.9 3.9 %slice-start.12 = ((bf16[3072,6144]{1,0:T(8,128)(2,1)}), bf16[3072,768]{1,0:T(8,128)(2,1)S(1)}, s32[]{:S(2)}) async-start(bf16[3072,6144]{1,0:T(8,128)(2,1)} %param.10), calls=%async_computation.12 | async-start | bytes 9437184 | tf_op jit(solution)/shard_map/slice | solution.py:102
  36.2 5.4 %collective-permute-start.10 = (bf16[120,768]{1,0:T(8,128)(2,1)S(1)}, bf16[120,768]{1,0:T(8,128)(2,1)S(1)}, u32[]{:S(2)}, u32[]{:S(2)}) collective-permute-start(bf16[120,768]{1,0:T(8,128)(2,1)S(1)} %add_convert_fusion.7), channel_id=1, source_target_pairs={{0,1},{1,0},{2,3},{3,2},{4,5},{5,4},{6,7},{7,6},{8,16},{9,17},{10,... | collective-permute-start | bytes 552968 | tf_op jit(solution)/shard_map/ppermute | solution.py:122
  36.3 1.7 %collective-permute-start.9 = (bf16[72,768]{1,0:T(8,128)(2,1)S(1)}, bf16[72,768]{1,0:T(8,128)(2,1)S(1)}, u32[]{:S(2)}, u32[]{:S(2)}) collective-permute-start(bf16[72,768]{1,0:T(8,128)(2,1)S(1)} %add_convert_fusion.8), channel_id=1, source_target_pairs={{0,1},{1,0},{2,3},{3,2},{4,5},{5,4},{6,7},{7,6},{8,16},{9,17},{10,... | collective-permute-start | bytes 331784 | tf_op jit(solution)/shard_map/ppermute | solution.py:122
  41.7 9.0 %collective-permute-start.12 = (bf16[192,768]{1,0:T(8,128)(2,1)S(1)}, bf16[192,768]{1,0:T(8,128)(2,1)S(1)}, u32[]{:S(2)}, u32[]{:S(2)}) collective-permute-start(bf16[192,768]{1,0:T(8,128)(2,1)S(1)} %add_convert_fusion.6), channel_id=1, source_target_pairs={{0,1},{1,0},{2,3},{3,2},{4,5},{5,4},{6,7},{7,6},{8,16},{9,17},{10,... | collective-permute-start | bytes 884744 | tf_op jit(solution)/shard_map/ppermute | solution.py:122
  42.1 9.9 %collective-permute-start.11 = (bf16[192,768]{1,0:T(8,128)(2,1)S(1)}, bf16[192,768]{1,0:T(8,128)(2,1)S(1)}, u32[]{:S(2)}, u32[]{:S(2)}) collective-permute-start(bf16[192,768]{1,0:T(8,128)(2,1)S(1)} %broadcast_select_fusion.5), channel_id=1, source_target_pairs={{0,8},{8,0},{16,24},{24,16},{1,9},{9,1},{17,25},{25,17},{2,10},{10... | collective-permute-start | bytes 884744 | tf_op jit(solution)/shard_map/ppermute | solution.py:119
  49.6 2.4 %slice-start = ((bf16[6144,3072]{1,0:T(8,128)(2,1)}), bf16[768,3072]{1,0:T(8,128)(2,1)S(1)}, s32[]{:S(2)}) async-start(bf16[6144,3072]{1,0:T(8,128)(2,1)} %param.12), calls=%async_computation | async-start | bytes 9437184 | tf_op jit(solution)/shard_map/slice | solution.py:102
  53.3 6.2 %collective-permute-start.14 = (bf16[192,768]{1,0:T(8,128)(2,1)S(1)}, bf16[192,768]{1,0:T(8,128)(2,1)S(1)}, u32[]{:S(2)}, u32[]{:S(2)}) collective-permute-start(bf16[192,768]{1,0:T(8,128)(2,1)S(1)} %add_convert_fusion.5), channel_id=1, source_target_pairs={{0,1},{1,0},{2,3},{3,2},{4,5},{5,4},{6,7},{7,6},{8,16},{9,17},{10,... | collective-permute-start | bytes 884744 | tf_op jit(solution)/shard_map/ppermute | solution.py:122
  53.7 9.5 %collective-permute-start.13 = (bf16[192,768]{1,0:T(8,128)(2,1)S(1)}, bf16[192,768]{1,0:T(8,128)(2,1)S(1)}, u32[]{:S(2)}, u32[]{:S(2)}) collective-permute-start(bf16[192,768]{1,0:T(8,128)(2,1)S(1)} %broadcast_select_fusion.4), channel_id=1, source_target_pairs={{0,8},{8,0},{16,24},{24,16},{1,9},{9,1},{17,25},{25,17},{2,10},{10... | collective-permute-start | bytes 884744 | tf_op jit(solution)/shard_map/ppermute | solution.py:119
  58.4 4.9 %slice-start.1 = ((bf16[6144,3072]{1,0:T(8,128)(2,1)}), bf16[768,3072]{1,0:T(8,128)(2,1)S(1)}, s32[]{:S(2)}) async-start(bf16[6144,3072]{1,0:T(8,128)(2,1)} %param.12), calls=%async_computation.1 | async-start | bytes 9437184 | tf_op jit(solution)/shard_map/slice | solution.py:102
  64.5 5.2 %collective-permute-start.16 = (bf16[192,768]{1,0:T(8,128)(2,1)S(1)}, bf16[192,768]{1,0:T(8,128)(2,1)S(1)}, u32[]{:S(2)}, u32[]{:S(2)}) collective-permute-start(bf16[192,768]{1,0:T(8,128)(2,1)S(1)} %add_convert_fusion.4), channel_id=1, source_target_pairs={{0,1},{1,0},{2,3},{3,2},{4,5},{5,4},{6,7},{7,6},{8,16},{9,17},{10,... | collective-permute-start | bytes 884744 | tf_op jit(solution)/shard_map/ppermute | solution.py:122
  64.9 9.5 %collective-permute-start.15 = (bf16[192,768]{1,0:T(8,128)(2,1)S(1)}, bf16[192,768]{1,0:T(8,128)(2,1)S(1)}, u32[]{:S(2)}, u32[]{:S(2)}) collective-permute-start(bf16[192,768]{1,0:T(8,128)(2,1)S(1)} %broadcast_select_fusion.3), channel_id=1, source_target_pairs={{0,8},{8,0},{16,24},{24,16},{1,9},{9,1},{17,25},{25,17},{2,10},{10... | collective-permute-start | bytes 884744 | tf_op jit(solution)/shard_map/ppermute | solution.py:119
  74.5 4.3 %collective-permute-start.18 = (bf16[192,768]{1,0:T(8,128)(2,1)S(1)}, bf16[192,768]{1,0:T(8,128)(2,1)S(1)}, u32[]{:S(2)}, u32[]{:S(2)}) collective-permute-start(bf16[192,768]{1,0:T(8,128)(2,1)S(1)} %add_convert_fusion.3), channel_id=1, source_target_pairs={{0,1},{1,0},{2,3},{3,2},{4,5},{5,4},{6,7},{7,6},{8,16},{9,17},{10,... | collective-permute-start | bytes 884744 | tf_op jit(solution)/shard_map/ppermute | solution.py:122
  74.9 9.5 %collective-permute-start.17 = (bf16[192,768]{1,0:T(8,128)(2,1)S(1)}, bf16[192,768]{1,0:T(8,128)(2,1)S(1)}, u32[]{:S(2)}, u32[]{:S(2)}) collective-permute-start(bf16[192,768]{1,0:T(8,128)(2,1)S(1)} %broadcast_select_fusion.2), channel_id=1, source_target_pairs={{0,8},{8,0},{16,24},{24,16},{1,9},{9,1},{17,25},{25,17},{2,10},{10... | collective-permute-start | bytes 884744 | tf_op jit(solution)/shard_map/ppermute | solution.py:119
  78.5 7.7 %slice-start.3 = ((bf16[6144,3072]{1,0:T(8,128)(2,1)}), bf16[768,3072]{1,0:T(8,128)(2,1)S(1)}, s32[]{:S(2)}) async-start(bf16[6144,3072]{1,0:T(8,128)(2,1)} %param.12), calls=%async_computation.3 | async-start | bytes 9437184 | tf_op jit(solution)/shard_map/slice | solution.py:102
  84.4 3.3 %collective-permute-start.20 = (bf16[192,768]{1,0:T(8,128)(2,1)S(1)}, bf16[192,768]{1,0:T(8,128)(2,1)S(1)}, u32[]{:S(2)}, u32[]{:S(2)}) collective-permute-start(bf16[192,768]{1,0:T(8,128)(2,1)S(1)} %add_convert_fusion.2), channel_id=1, source_target_pairs={{0,1},{1,0},{2,3},{3,2},{4,5},{5,4},{6,7},{7,6},{8,16},{9,17},{10,... | collective-permute-start | bytes 884744 | tf_op jit(solution)/shard_map/ppermute | solution.py:122
  84.8 9.5 %collective-permute-start.19 = (bf16[192,768]{1,0:T(8,128)(2,1)S(1)}, bf16[192,768]{1,0:T(8,128)(2,1)S(1)}, u32[]{:S(2)}, u32[]{:S(2)}) collective-permute-start(bf16[192,768]{1,0:T(8,128)(2,1)S(1)} %broadcast_select_fusion.1), channel_id=1, source_target_pairs={{0,8},{8,0},{16,24},{24,16},{1,9},{9,1},{17,25},{25,17},{2,10},{10... | collective-permute-start | bytes 884744 | tf_op jit(solution)/shard_map/ppermute | solution.py:119
  87.4 8.7 %slice-start.4 = ((bf16[6144,3072]{1,0:T(8,128)(2,1)}), bf16[768,3072]{1,0:T(8,128)(2,1)S(1)}, s32[]{:S(2)}) async-start(bf16[6144,3072]{1,0:T(8,128)(2,1)} %param.12), calls=%async_computation.4 | async-start | bytes 9437184 | tf_op jit(solution)/shard_map/slice | solution.py:102
  94.4 3.3 %collective-permute-start.22 = (bf16[192,768]{1,0:T(8,128)(2,1)S(1)}, bf16[192,768]{1,0:T(8,128)(2,1)S(1)}, u32[]{:S(2)}, u32[]{:S(2)}) collective-permute-start(bf16[192,768]{1,0:T(8,128)(2,1)S(1)} %add_convert_fusion.1), channel_id=1, source_target_pairs={{0,1},{1,0},{2,3},{3,2},{4,5},{5,4},{6,7},{7,6},{8,16},{9,17},{10,... | collective-permute-start | bytes 884744 | tf_op jit(solution)/shard_map/ppermute | solution.py:122
  94.8 9.5 %collective-permute-start.21 = (bf16[192,768]{1,0:T(8,128)(2,1)S(1)}, bf16[192,768]{1,0:T(8,128)(2,1)S(1)}, u32[]{:S(2)}, u32[]{:S(2)}) collective-permute-start(bf16[192,768]{1,0:T(8,128)(2,1)S(1)} %broadcast_select_fusion), channel_id=1, source_target_pairs={{0,8},{8,0},{16,24},{24,16},{1,9},{9,1},{17,25},{25,17},{2,10},{10... | collective-permute-start | bytes 884744 | tf_op jit(solution)/shard_map/ppermute | solution.py:119
  104.3 1.7 %collective-permute-start.25 = (bf16[96,768]{1,0:T(8,128)(2,1)S(1)}, bf16[96,768]{1,0:T(8,128)(2,1)S(1)}, u32[]{:S(2)}, u32[]{:S(2)}) collective-permute-start(bf16[96,768]{1,0:T(8,128)(2,1)S(1)} %get-tuple-element.109), channel_id=1, source_target_pairs={{0,1},{1,0},{2,3},{3,2},{4,5},{5,4},{6,7},{7,6},{8,16},{9,17},{10,... | collective-permute-start | bytes 442376 | tf_op jit(solution)/shard_map/ppermute | solution.py:122
  104.7 9.9 %collective-permute-start.23 = (bf16[192,768]{1,0:T(8,128)(2,1)S(1)}, bf16[192,768]{1,0:T(8,128)(2,1)S(1)}, u32[]{:S(2)}, u32[]{:S(2)}) collective-permute-start(bf16[192,768]{1,0:T(8,128)(2,1)S(1)} %fusion.61), channel_id=1, source_target_pairs={{0,8},{8,0},{16,24},{24,16},{1,9},{9,1},{17,25},{25,17},{2,10},{10... | collective-permute-start | bytes 884744 | tf_op jit(solution)/shard_map/ppermute | solution.py:119
  106.0 8.6 %slice-start.6 = ((bf16[6144,3072]{1,0:T(8,128)(2,1)}), bf16[768,3072]{1,0:T(8,128)(2,1)S(1)}, s32[]{:S(2)}) async-start(bf16[6144,3072]{1,0:T(8,128)(2,1)} %param.12), calls=%async_computation.6 | async-start | bytes 9437184 | tf_op jit(solution)/shard_map/slice | solution.py:102
  106.2 9.6 %slice-start.5 = ((bf16[6144,3072]{1,0:T(8,128)(2,1)}), bf16[768,3072]{1,0:T(8,128)(2,1)S(1)}, s32[]{:S(2)}) async-start(bf16[6144,3072]{1,0:T(8,128)(2,1)} %param.12), calls=%async_computation.5 | async-start | bytes 9437184 | tf_op jit(solution)/shard_map/slice | solution.py:102
  106.2 11.1 %collective-permute-start.27 = (bf16[96,768]{1,0:T(8,128)(2,1)S(1)}, bf16[96,768]{1,0:T(8,128)(2,1)S(1)}, u32[]{:S(2)}, u32[]{:S(2)}) collective-permute-start(bf16[96,768]{1,0:T(8,128)(2,1)S(1)} %fusion.74), channel_id=1, source_target_pairs={{0,8},{8,0},{16,24},{24,16},{1,9},{9,1},{17,25},{25,17},{2,10},{10... | collective-permute-start | bytes 442376 | tf_op jit(solution)/shard_map/ppermute | solution.py:119
  119.0 11.4 %collective-permute-start.28 = (bf16[96,3072]{1,0:T(8,128)(2,1)S(1)}, bf16[96,3072]{1,0:T(8,128)(2,1)S(1)}, u32[]{:S(2)}, u32[]{:S(2)}) collective-permute-start(bf16[96,3072]{1,0:T(8,128)(2,1)S(1)} %fusion.1), channel_id=1, source_target_pairs={{0,1},{1,0},{2,3},{3,2},{4,5},{5,4},{6,7},{7,6},{8,9},{9,8},{10,11... | collective-permute-start | bytes 1769480 | tf_op jit(solution)/shard_map/ppermute | solution.py:34
  119.1 2.2 %collective-permute-start.24 = (bf16[96,768]{1,0:T(8,128)(2,1)S(1)}, bf16[96,768]{1,0:T(8,128)(2,1)S(1)}, u32[]{:S(2)}, u32[]{:S(2)}) collective-permute-start(bf16[96,768]{1,0:T(8,128)(2,1)S(1)} %get-tuple-element.108), channel_id=1, source_target_pairs={{0,1},{1,0},{2,3},{3,2},{4,5},{5,4},{6,7},{7,6},{8,16},{9,17},{10,... | collective-permute-start | bytes 442376 | tf_op jit(solution)/shard_map/ppermute | solution.py:122
  121.4 9.0 %collective-permute-start.26 = (bf16[96,768]{1,0:T(8,128)(2,1)S(1)}, bf16[96,768]{1,0:T(8,128)(2,1)S(1)}, u32[]{:S(2)}, u32[]{:S(2)}) collective-permute-start(bf16[96,768]{1,0:T(8,128)(2,1)S(1)} %fusion.82), channel_id=1, source_target_pairs={{0,8},{8,0},{16,24},{24,16},{1,9},{9,1},{17,25},{25,17},{2,10},{10... | collective-permute-start | bytes 442376 | tf_op jit(solution)/shard_map/ppermute | solution.py:119
  126.8 3.6 %slice-start.8 = ((bf16[6144,3072]{1,0:T(8,128)(2,1)}), bf16[768,3072]{1,0:T(8,128)(2,1)S(1)}, s32[]{:S(2)}) async-start(bf16[6144,3072]{1,0:T(8,128)(2,1)} %param.12), calls=%async_computation.8 | async-start | bytes 9437184 | tf_op jit(solution)/shard_map/slice | solution.py:102
  126.8 13.1 %copy-start.2 = (f32[3072]{0:T(1024)S(1)}, f32[3072]{0:T(1024)}, u32[]{:S(2)}) copy-start(f32[3072]{0:T(1024)} %param.13) | copy-start | bytes 36868
  131.4 6.4 %collective-permute-start.29 = (bf16[24,3072]{1,0:T(8,128)(2,1)S(1)}, bf16[24,3072]{1,0:T(8,128)(2,1)S(1)}, u32[]{:S(2)}, u32[]{:S(2)}) collective-permute-start(bf16[24,3072]{1,0:T(8,128)(2,1)S(1)} %get-tuple-element.105), channel_id=1, source_target_pairs={{0,2},{1,3},{2,0},{3,1},{4,6},{5,7},{6,4},{7,5},{8,10},{9,11},{10,... | collective-permute-start | bytes 442376 | tf_op jit(solution)/shard_map/ppermute | solution.py:34
  131.4 6.8 %collective-permute-start.30 = (bf16[24,3072]{1,0:T(8,128)(2,1)S(1)}, bf16[24,3072]{1,0:T(8,128)(2,1)S(1)}, u32[]{:S(2)}, u32[]{:S(2)}) collective-permute-start(bf16[24,3072]{1,0:T(8,128)(2,1)S(1)} %get-tuple-element.107), channel_id=1, source_target_pairs={{0,4},{1,5},{2,6},{3,7},{4,0},{5,1},{6,2},{7,3},{8,12},{9,13},{10,... | collective-permute-start | bytes 442376 | tf_op jit(solution)/shard_map/ppermute | solution.py:34
  132.7 7.2 %collective-permute-start.31 = (bf16[24,3072]{1,0:T(8,128)(2,1)S(1)}, bf16[24,3072]{1,0:T(8,128)(2,1)S(1)}, u32[]{:S(2)}, u32[]{:S(2)}) collective-permute-start(bf16[24,3072]{1,0:T(8,128)(2,1)S(1)} %get-tuple-element.106), channel_id=1, source_target_pairs={{0,6},{1,7},{2,4},{3,5},{4,2},{5,3},{6,0},{7,1},{8,14},{9,15},{10,... | collective-permute-start | bytes 442376 | tf_op jit(solution)/shard_map/ppermute | solution.py:34
  (5 other events, 11.7 us)
